TPU v7x, 32 devices: a whole 2x2x4 slice. The times are simulated.
32 devices in a mesh: wide: 16 (over z, x, core), seq: 2 (over y).
Axes of the slice: x: 2, y: 2, z: 4, core: 2. Of those that a mesh axis runs over, the one named last changes fastest.
Arguments:
- latents: bfloat16 [208, 128, 1152], P('wide', 'seq'), may hold values from -6 to 6
- skip_store: bfloat16 [208, 128, 1152], P('wide', None, 'seq'), may hold values from -6 to 6
- lengths: int32 [208], P('wide'), may hold values from 80 to 128, as said below
- cotangent: bfloat16 [208, 128, 1152], P('wide', 'seq'), may hold values from -6 to 6
- skip_weight: bfloat16 [2304, 1152], P('seq'), may hold values from -0.125 to 0.125
- skip_bias: bfloat16 [1152], P('seq'), may hold values from -1.75 to 1.75
- first_gain: bfloat16 [1152], P('seq'), may hold values from 0.099609375 to 1.8984375
- first_shift: bfloat16 [1152], P('seq'), may hold values from -1.75 to 1.75
- inward_weight: bfloat16 [1152, 3456], P('seq'), may hold values from -0.1875 to 0.1875
- outward_weight: bfloat16 [1152, 1152], P('seq'), may hold values from -0.5 to 0.5
- outward_bias: bfloat16 [1152], P('seq'), may hold values from -1.75 to 1.75
- second_gain: bfloat16 [1152], P('seq'), may hold values from 0.099609375 to 1.8984375
- second_shift: bfloat16 [1152], P('seq'), may hold values from -1.75 to 1.75
- expand_weight: bfloat16 [1152, 4608], P('seq'), may hold values from -0.1875 to 0.1875
- expand_bias: bfloat16 [4608], P('seq'), may hold values from -1.75 to 1.75
- contract_weight: bfloat16 [4608, 1152], P('seq'), may hold values from -0.09375 to 0.09375
- contract_bias: bfloat16 [1152], P('seq'), may hold values from -1.75 to 1.75
Outputs:
- output: bfloat16 [208, 128, 1152], P('wide', 'seq')
- latents_grad: float32 [208, 128, 1152], P('wide', 'seq')
- skip_grad: bfloat16 [208, 128, 1152], P('wide', None, 'seq')
- skip_weight_grad: float32 [2304, 1152], P('seq')
- skip_bias_grad: float32 [1152], P('seq')
- first_gain_grad: float32 [1152], P('seq')
- first_shift_grad: float32 [1152], P('seq')
- inward_weight_grad: float32 [1152, 3456], P('seq')
- outward_weight_grad: float32 [1152, 1152], P('seq')
- outward_bias_grad: float32 [1152], P('seq')
- second_gain_grad: float32 [1152], P('seq')
- second_shift_grad: float32 [1152], P('seq')
- expand_weight_grad: float32 [1152, 4608], P('seq')
- expand_bias_grad: float32 [4608], P('seq')
- contract_weight_grad: float32 [4608, 1152], P('seq')
- contract_bias_grad: float32 [1152], P('seq')
Inputs may be any that keep to these rules, and one draw needn't show every extreme that they name: `lengths`: among the 13 items of each index of wide, at least one has all 128 slots live.
All inputs are finite; a program needn't handle non-finite values.
Results may differ from a plain program's by a relative error of at most 0.02.
Values may be sent and summed in bfloat16 or wider, within the bound.
No kernel may reach another device: no remote copies, remote signals or barrier semaphores. Data moves between devices by JAX's collectives and lax.ppermute only.
A program may use at most 512 MiB of HBM per device.

v0:
```python
import jax
import jax.numpy as jnp
from jax import lax
from jax.sharding import PartitionSpec as P

HEAD_DIM = 72


EPS = 1e-05
NEG = -1e30


def across(left_side, right_side):
    return lax.dot_general(
        left_side, right_side, (((0,), (0,)), ((), ())), preferred_element_type=jnp.float32
    )


def against(left_side, right_side):
    return lax.dot_general(
        left_side, right_side, (((1,), (1,)), ((), ())), preferred_element_type=jnp.float32
    )


def simple(left_side, right_side):
    return jnp.dot(left_side, right_side, preferred_element_type=jnp.float32)


def layer_norm(hidden, gain, shift):
    mean_val = jnp.mean(hidden, -1, keepdims=True)
    centred = hidden - mean_val
    var_val = jnp.mean(centred * centred, -1, keepdims=True)
    return centred * lax.rsqrt(var_val + EPS) * gain + shift


def exact_gelu(values_in):
    return jax.nn.gelu(values_in, approximate=False)


def masked_scores(queries, keys_all, key_valid, score_scale):
    scores = (
        jnp.einsum("iqhd,ikhd->ihqk", queries, keys_all, preferred_element_type=jnp.float32)
        * score_scale
    )
    return jnp.where(key_valid[:, None, None, :], scores, NEG)


def attend(queries, keys_all, values_all, key_valid, score_scale):
    scores = masked_scores(queries, keys_all, key_valid, score_scale)
    peak = jnp.max(scores, -1, keepdims=True)
    raised = jnp.exp(scores - peak)
    total = jnp.sum(raised, -1, keepdims=True)
    probs = (raised / total).astype(jnp.bfloat16)
    mixed = jnp.einsum("ihqk,ikhd->iqhd", probs, values_all, preferred_element_type=jnp.float32)
    return (mixed.astype(jnp.bfloat16), peak + jnp.log(total))


def attend_back(queries, keys_all, values_all, key_valid, score_scale, log_total, grad_mixed):
    scores = masked_scores(queries, keys_all, key_valid, score_scale)
    probs = jnp.exp(scores - log_total)
    grad_probs = jnp.einsum(
        "iqhd,ikhd->ihqk", grad_mixed, values_all, preferred_element_type=jnp.float32
    )
    grad_scores = probs * (grad_probs - jnp.sum(grad_probs * probs, -1, keepdims=True))
    grad_scores = grad_scores.astype(jnp.bfloat16)
    grad_query = (
        jnp.einsum("ihqk,ikhd->iqhd", grad_scores, keys_all, preferred_element_type=jnp.float32)
        * score_scale
    )
    grad_key = (
        jnp.einsum("ihqk,iqhd->ikhd", grad_scores, queries, preferred_element_type=jnp.float32)
        * score_scale
    )
    grad_value = jnp.einsum(
        "ihqk,iqhd->ikhd",
        probs.astype(jnp.bfloat16),
        grad_mixed,
        preferred_element_type=jnp.float32,
    )
    return (grad_query, grad_key, grad_value)


def per_device(
    latents,
    skip_store,
    lengths,
    cotangent,
    skip_weight,
    skip_bias,
    first_gain,
    first_shift,
    inward_weight,
    outward_weight,
    outward_bias,
    second_gain,
    second_shift,
    expand_weight,
    expand_bias,
    contract_weight,
    contract_bias,
):
    shards = (
        skip_weight,
        skip_bias,
        first_gain,
        first_shift,
        inward_weight,
        outward_weight,
        outward_bias,
        second_gain,
        second_shift,
        expand_weight,
        expand_bias,
        contract_weight,
        contract_bias,
    )
    (
        skip_matrix,
        skip_offset,
        gain_first,
        shift_first,
        inward_matrix,
        outward_matrix,
        outward_offset,
        gain_second,
        shift_second,
        expand_matrix,
        expand_offset,
        contract_matrix,
        contract_offset,
    ) = (
        lax.all_gather(shards[0], "seq", axis=0, tiled=True),
        lax.all_gather(shards[1], "seq", axis=0, tiled=True),
        lax.all_gather(shards[2], "seq", axis=0, tiled=True),
        lax.all_gather(shards[3], "seq", axis=0, tiled=True),
        lax.all_gather(shards[4], "seq", axis=0, tiled=True),
        lax.all_gather(shards[5], "seq", axis=0, tiled=True),
        lax.all_gather(shards[6], "seq", axis=0, tiled=True),
        lax.all_gather(shards[7], "seq", axis=0, tiled=True),
        lax.all_gather(shards[8], "seq", axis=0, tiled=True),
        lax.all_gather(shards[9], "seq", axis=0, tiled=True),
        lax.all_gather(shards[10], "seq", axis=0, tiled=True),
        lax.all_gather(shards[11], "seq", axis=0, tiled=True),
        lax.all_gather(shards[12], "seq", axis=0, tiled=True),
    )
    gain_first = gain_first.astype(jnp.float32)
    shift_first = shift_first.astype(jnp.float32)
    gain_second = gain_second.astype(jnp.float32)
    shift_second = shift_second.astype(jnp.float32)
    item_count, slot_dev, model_width = latents.shape
    row_count = item_count * slot_dev
    seq_ways = lax.axis_size("seq")
    slot_count = slot_dev * seq_ways
    head_width = HEAD_DIM
    head_count = model_width // head_width
    score_scale = head_width ** (-0.5)
    key_valid = jnp.arange(slot_count, dtype=jnp.int32)[None, :] < lengths[:, None]
    skip_rows = lax.all_to_all(skip_store, "seq", split_axis=1, concat_axis=2, tiled=True)
    joined = jnp.concatenate([latents, skip_rows], -1).reshape(row_count, 2 * model_width)
    base = simple(joined, skip_matrix) + skip_offset.astype(jnp.float32)
    first_normed = layer_norm(base, gain_first, shift_first).astype(jnp.bfloat16)
    qkv_vals = simple(first_normed, inward_matrix).astype(jnp.bfloat16)
    qkv_split = qkv_vals.reshape(item_count, slot_dev, 3, head_count, head_width)
    queries = qkv_split[:, :, 0]
    keys_all, values_all = (
        lax.all_gather(qkv_split[:, :, 1], "seq", axis=1, tiled=True),
        lax.all_gather(qkv_split[:, :, 2], "seq", axis=1, tiled=True),
    )
    mixed, log_total = attend(queries, keys_all, values_all, key_valid, score_scale)
    mixed_rows = mixed.reshape(row_count, model_width)
    middle = base + simple(mixed_rows, outward_matrix) + outward_offset.astype(jnp.float32)
    second_normed = layer_norm(middle, gain_second, shift_second).astype(jnp.bfloat16)
    upper = simple(second_normed, expand_matrix) + expand_offset.astype(jnp.float32)
    activated = exact_gelu(upper).astype(jnp.bfloat16)
    result = middle + simple(activated, contract_matrix) + contract_offset.astype(jnp.float32)
    output = result.astype(jnp.bfloat16).reshape(item_count, slot_dev, model_width)
    grad_out = cotangent.reshape(row_count, model_width)
    grad_result = grad_out.astype(jnp.float32)
    grad_contract = across(activated, grad_out)
    grad_contract_off = jnp.sum(grad_result, 0)
    grad_act = against(grad_out, contract_matrix)
    unused_value, gelu_back = jax.vjp(exact_gelu, upper)
    grad_upper = gelu_back(grad_act)[0].astype(jnp.bfloat16)
    grad_expand = across(second_normed, grad_upper)
    grad_expand_off = jnp.sum(grad_upper.astype(jnp.float32), 0)
    grad_second = against(grad_upper, expand_matrix)
    unused_norm, second_back = jax.vjp(layer_norm, middle, gain_second, shift_second)
    grad_mid_ln, grad_gain_two, grad_shift_two = second_back(grad_second)
    grad_middle = grad_result + grad_mid_ln
    grad_branch = grad_middle.astype(jnp.bfloat16)
    grad_outward = across(mixed_rows, grad_branch)
    grad_outward_off = jnp.sum(grad_branch.astype(jnp.float32), 0)
    grad_mixed = against(grad_branch, outward_matrix).astype(jnp.bfloat16)
    grad_heads = grad_mixed.reshape(item_count, slot_dev, head_count, head_width)
    grad_query, grad_key, grad_value = attend_back(
        queries, keys_all, values_all, key_valid, score_scale, log_total, grad_heads
    )
    key_local, value_local = (
        lax.psum_scatter(
            grad_key.astype(jnp.bfloat16), "seq", scatter_dimension=1, tiled=True
        ).astype(jnp.float32),
        lax.psum_scatter(
            grad_value.astype(jnp.bfloat16), "seq", scatter_dimension=1, tiled=True
        ).astype(jnp.float32),
    )
    grad_qkv = jnp.stack([grad_query, key_local, value_local], 2).astype(jnp.bfloat16)
    grad_qkv = grad_qkv.reshape(row_count, 3 * model_width)
    grad_inward = across(first_normed, grad_qkv)
    grad_first = against(grad_qkv, inward_matrix)
    unused_first, first_back = jax.vjp(layer_norm, base, gain_first, shift_first)
    grad_base_ln, grad_gain_one, grad_shift_one = first_back(grad_first)
    grad_base = (grad_middle + grad_base_ln).astype(jnp.bfloat16)
    grad_skipw = across(joined, grad_base)
    grad_skip_off = jnp.sum(grad_base.astype(jnp.float32), 0)
    grad_joined = against(grad_base, skip_matrix)
    grad_latents = grad_joined[:, :model_width].reshape(item_count, slot_dev, model_width)
    grad_skip_rows = (
        grad_joined[:, model_width:].astype(jnp.bfloat16).reshape(item_count, slot_dev, model_width)
    )
    grad_skip = lax.all_to_all(grad_skip_rows, "seq", split_axis=2, concat_axis=1, tiled=True)
    grad_terms = (
        grad_skipw,
        grad_skip_off,
        grad_gain_one,
        grad_shift_one,
        grad_inward,
        grad_outward,
        grad_outward_off,
        grad_gain_two,
        grad_shift_two,
        grad_expand,
        grad_expand_off,
        grad_contract,
        grad_contract_off,
    )
    grad_parts = (
        lax.psum_scatter(
            grad_terms[0].astype(jnp.bfloat16), "seq", scatter_dimension=0, tiled=True
        ).astype(jnp.float32),
        lax.psum_scatter(
            grad_terms[1].astype(jnp.bfloat16), "seq", scatter_dimension=0, tiled=True
        ).astype(jnp.float32),
        lax.psum_scatter(
            grad_terms[2].astype(jnp.bfloat16), "seq", scatter_dimension=0, tiled=True
        ).astype(jnp.float32),
        lax.psum_scatter(
            grad_terms[3].astype(jnp.bfloat16), "seq", scatter_dimension=0, tiled=True
        ).astype(jnp.float32),
        lax.psum_scatter(
            grad_terms[4].astype(jnp.bfloat16), "seq", scatter_dimension=0, tiled=True
        ).astype(jnp.float32),
        lax.psum_scatter(
            grad_terms[5].astype(jnp.bfloat16), "seq", scatter_dimension=0, tiled=True
        ).astype(jnp.float32),
        lax.psum_scatter(
            grad_terms[6].astype(jnp.bfloat16), "seq", scatter_dimension=0, tiled=True
        ).astype(jnp.float32),
        lax.psum_scatter(
            grad_terms[7].astype(jnp.bfloat16), "seq", scatter_dimension=0, tiled=True
        ).astype(jnp.float32),
        lax.psum_scatter(
            grad_terms[8].astype(jnp.bfloat16), "seq", scatter_dimension=0, tiled=True
        ).astype(jnp.float32),
        lax.psum_scatter(
            grad_terms[9].astype(jnp.bfloat16), "seq", scatter_dimension=0, tiled=True
        ).astype(jnp.float32),
        lax.psum_scatter(
            grad_terms[10].astype(jnp.bfloat16), "seq", scatter_dimension=0, tiled=True
        ).astype(jnp.float32),
        lax.psum_scatter(
            grad_terms[11].astype(jnp.bfloat16), "seq", scatter_dimension=0, tiled=True
        ).astype(jnp.float32),
        lax.psum_scatter(
            grad_terms[12].astype(jnp.bfloat16), "seq", scatter_dimension=0, tiled=True
        ).astype(jnp.float32),
    )
    (
        sum_skipw,
        sum_skipb,
        sum_gain1,
        sum_shift1,
        sum_inward,
        sum_outward,
        sum_outb,
        sum_gain2,
        sum_shift2,
        sum_expand,
        sum_expandb,
        sum_contract,
        sum_contractb,
    ) = (
        lax.psum(grad_parts[0].astype(jnp.bfloat16), "wide").astype(jnp.float32),
        lax.psum(grad_parts[1].astype(jnp.bfloat16), "wide").astype(jnp.float32),
        lax.psum(grad_parts[2].astype(jnp.bfloat16), "wide").astype(jnp.float32),
        lax.psum(grad_parts[3].astype(jnp.bfloat16), "wide").astype(jnp.float32),
        lax.psum(grad_parts[4].astype(jnp.bfloat16), "wide").astype(jnp.float32),
        lax.psum(grad_parts[5].astype(jnp.bfloat16), "wide").astype(jnp.float32),
        lax.psum(grad_parts[6].astype(jnp.bfloat16), "wide").astype(jnp.float32),
        lax.psum(grad_parts[7].astype(jnp.bfloat16), "wide").astype(jnp.float32),
        lax.psum(grad_parts[8].astype(jnp.bfloat16), "wide").astype(jnp.float32),
        lax.psum(grad_parts[9].astype(jnp.bfloat16), "wide").astype(jnp.float32),
        lax.psum(grad_parts[10].astype(jnp.bfloat16), "wide").astype(jnp.float32),
        lax.psum(grad_parts[11].astype(jnp.bfloat16), "wide").astype(jnp.float32),
        lax.psum(grad_parts[12].astype(jnp.bfloat16), "wide").astype(jnp.float32),
    )
    return (
        output,
        grad_latents,
        grad_skip,
        sum_skipw,
        sum_skipb,
        sum_gain1,
        sum_shift1,
        sum_inward,
        sum_outward,
        sum_outb,
        sum_gain2,
        sum_shift2,
        sum_expand,
        sum_expandb,
        sum_contract,
        sum_contractb,
    )


def solution(mesh):
    return jax.shard_map(
        per_device,
        mesh=mesh,
        in_specs=(
            P("wide", "seq", None),
            P("wide", None, "seq"),
            P("wide"),
            P("wide", "seq", None),
            P("seq", None),
            P("seq"),
            P("seq"),
            P("seq"),
            P("seq", None),
            P("seq", None),
            P("seq"),
            P("seq"),
            P("seq"),
            P("seq", None),
            P("seq"),
            P("seq", None),
            P("seq"),
        ),
        out_specs=(
            P("wide", "seq", None),
            P("wide", "seq", None),
            P("wide", None, "seq"),
            P("seq", None),
            P("seq"),
            P("seq"),
            P("seq"),
            P("seq", None),
            P("seq", None),
            P("seq"),
            P("seq"),
            P("seq"),
            P("seq", None),
            P("seq"),
            P("seq", None),
            P("seq"),
        ),
        check_vma=False,
    )
```

profile of v0, /device:TPU:0, one launch (start us, length us, event | category | flops | bytes accessed | tf_op | source)
XLA Modules:
  0.0 1866.6 jit_solution(10372359800916407453)
XLA Ops:
  21.0 57.0 %all-reduce.18 = (bf16[1152]{0:T(1024)(128)(2,1)S(1)}, bf16[1152]{0:T(1024)(128)(2,1)S(1)}, bf16[1152]{0:T(1024)(128)(2,1)S(1)}, bf16[1152]{0:T(1024)(128)(2,1)S...) all-reduce(bf16[1152]{0:T(1024)(128)(2,1)S(1)} %dynamic-update-slic, ...), channel_id=1, replica_groups=mesh['wide'=16,'seq'=2] {'seq'}, use_global_device_ids=true, to_apply=%add | all-reduce | flops 6912 | bytes 27648
  86.4 21.0 %all-gather.11.cloned.1.call-done = bf16[2304,1152]{1,0:T(8,128)(2,1)} async-done(((bf16[1152,1152]{1,0:T(8,128)(2,1)}), bf16[2304,1152]{1,0:T(8,128)(2,1)}) %all-gather.11.cloned.1.call-update) | async-done | bytes 5308432 | tf_op jit(solution)/shard_map/all_gather | solution.py:132
  118.8 89.9 %all-gather.13.cloned.1.call-done = bf16[1152,3456]{1,0:T(8,128)(2,1)} async-done(((bf16[576,3456]{1,0:T(8,128)(2,1)}), bf16[1152,3456]{1,0:T(8,128)(2,1)}) %all-gather.13.cloned.1.call-update) | async-done | bytes 7962640 | tf_op jit(solution)/shard_map/all_gather | solution.py:136
  222.7 21.1 %reshape.156 = bf16[13,64,3,16,72]{4,3,2,1,0:T(8,128)(2,1)} reshape(bf16[832,3456]{1,0:T(8,128)(2,1)} %convolution_convert_fusion.5) | data formatting | bytes 11501568 | tf_op jit(solution)/shard_map/reshape | solution.py:163
  264.6 74.7 %all-gather.21.cloned.1.call-done = bf16[13,128,1,16,72]{4,3,2,0,1:T(8,128)(2,1)} async-done(((bf16[13,64,1,16,72]{4,3,2,0,1:T(8,128)(2,1)}), bf16[13,128,1,16,72]{4,3,2,0,1:T(8,128)(2,1)}) %all-gather.21.cloned.1.call-update) | async-done | bytes 3833872 | tf_op jit(solution)/shard_map/all_gather | solution.py:167
  349.0 78.6 %all-gather.23.cloned.1.call-done = bf16[13,128,1,16,72]{4,3,2,0,1:T(8,128)(2,1)} async-done(((bf16[13,64,1,16,72]{4,3,2,0,1:T(8,128)(2,1)}), bf16[13,128,1,16,72]{4,3,2,0,1:T(8,128)(2,1)}) %all-gather.23.cloned.1.call-update) | async-done | bytes 3833872 | tf_op jit(solution)/shard_map/all_gather | solution.py:166
  477.6 123.1 %all-gather.17.cloned.1.call-done = bf16[1152,4608]{1,0:T(8,128)(2,1)} async-done(((bf16[576,4608]{1,0:T(8,128)(2,1)}), bf16[1152,4608]{1,0:T(8,128)(2,1)}) %all-gather.17.cloned.1.call-update) | async-done | bytes 10616848 | tf_op jit(solution)/shard_map/all_gather | solution.py:141
  600.8 17.7 fusion.45
  618.5 114.8 %all-gather.19.cloned.1.call-done = bf16[4608,1152]{1,0:T(8,128)(2,1)} async-done(((bf16[2304,1152]{1,0:T(8,128)(2,1)}), bf16[4608,1152]{1,0:T(8,128)(2,1)}) %all-gather.19.cloned.1.call-update) | async-done | bytes 10616848 | tf_op jit(solution)/shard_map/all_gather | solution.py:143
  733.3 50.0 %fusion.46 = (bf16[4608]{0:T(1024)(128)(2,1)}, bf16[832,4608]{1,0:T(8,128)(2,1)}, f32[832,4608]{1,0:T(8,128)}) fusion(f32[832,4608]{1,0:T(8,128)} %fusion.45, f32[4608]{0:T(1024)S(1)} %reshape.188, bf16[832,1152]{1,0:T(8,128)(2,1)S(1)} %bitcast.93, bf16[4608,1152]{1,0:T(8,128)(2,1)} %all-gather.19.cloned.1.call-done), kind=kOutput, calls=%fused_computation.97 | convolution fusion | flops 9116905472 | bytes 50899968 | tf_op jit(solution)/shard_map/dot_general | solution.py:20
  874.2 50.7 %reduce-scatter.8.cloned.1.call-done = bf16[13,64,16,72]{3,2,0,1:T(8,128)(2,1)} async-done(((bf16[13,128,16,72]{3,2,0,1:T(8,128)(2,1)}), bf16[13,64,16,72]{3,2,0,1:T(8,128)(2,1)}) %reduce-scatter.8.cloned.1.call-update) | async-done | bytes 1916944 | tf_op jit(solution)/shard_map/reduce_scatter | solution.py:199
  927.8 82.9 %reduce-scatter.10.cloned.1.call-done = bf16[13,64,16,72]{3,2,0,1:T(8,128)(2,1)} async-done(((bf16[13,128,16,72]{3,2,0,1:T(8,128)(2,1)}), bf16[13,64,16,72]{3,2,0,1:T(8,128)(2,1)}) %reduce-scatter.10.cloned.1.call-update) | async-done | bytes 1916944 | tf_op jit(solution)/shard_map/reduce_scatter | solution.py:202
  1024.8 16.5 copy.116
  1041.3 16.8 convert_element_type.214
  1058.1 14.3 multiply_reduce_fusion.2
  1086.1 17.7 convolution_convert_fusion.1
  1117.8 14.4 convolution_convert_fusion
  1133.0 14.5 convolution_convert_fusion.2
  1152.0 126.1 %reduce-scatter.18.cloned.1.call-done = bf16[576,4608]{1,0:T(8,128)(2,1)} async-done(((bf16[1152,4608]{1,0:T(8,128)(2,1)}), bf16[576,4608]{1,0:T(8,128)(2,1)}) %reduce-scatter.18.cloned.1.call-update) | async-done | bytes 5308432 | tf_op jit(solution)/shard_map/reduce_scatter | solution.py:264
  1278.1 126.3 %reduce-scatter.20.cloned.1.call-done = bf16[2304,1152]{1,0:T(8,128)(2,1)} async-done(((bf16[4608,1152]{1,0:T(8,128)(2,1)}), bf16[2304,1152]{1,0:T(8,128)(2,1)}) %reduce-scatter.20.cloned.1.call-update) | async-done | bytes 5308432 | tf_op jit(solution)/shard_map/reduce_scatter | solution.py:270
  1404.3 97.4 %reduce-scatter.14.cloned.1.call-done = bf16[576,3456]{1,0:T(8,128)(2,1)} async-done(((bf16[1152,3456]{1,0:T(8,128)(2,1)}), bf16[576,3456]{1,0:T(8,128)(2,1)}) %reduce-scatter.14.cloned.1.call-update) | async-done | bytes 3981328 | tf_op jit(solution)/shard_map/reduce_scatter | solution.py:249
  1538.6 17.5 fusion.19
  1561.0 61.8 %all-reduce.15 = (bf16[576]{0:T(1024)(128)(2,1)S(1)}, bf16[576]{0:T(1024)(128)(2,1)S(1)}, bf16[576]{0:T(1024)(128)(2,1)S(1)}, bf16[576]{0:T(1024)(128)(2,1)S(1)}...) all-reduce(bf16[576]{0:T(1024)(128)(2,1)S(1)} %dynamic-slice.8, ...), channel_id=1, replica_groups=mesh['wide'=16,'seq'=2] {'wide'}, use_global_device_ids=true, to_apply=%region_17.18 | all-reduce | flops 6336 | bytes 25344 | tf_op jit(solution)/shard_map/psum | solution.py:293
  1645.8 191.3 %all-reduce.21.cloned.1.call-done = (bf16[1152,1152]{1,0:T(8,128)(2,1)}, bf16[576,3456]{1,0:T(8,128)(2,1)}, bf16[576,1152]{1,0:T(8,128)(2,1)}, bf16[576,4608]{1,0:T(8,128)(2,1)}, bf16[2304,1152]{1,0:T(8,128)(2,1)}) async-done(((bf16[1152,1152]{1,0:T(8,128)(2,1)}, bf16[576,3456]{1,0:T(8,128)(2,1)}, bf16[576,1152]{1,0:T(8,128)(2,1)}, bf16[576,4608]{1,0:T(8,128)(2,1)}, bf16[2304,1152]{1,0:T(8,128)(2,1)}), ...) | async-done | bytes 18579472 | tf_op jit(solution)/shard_map/psum | solution.py:292
  (292 shorter events, 353.5 us)
Async XLA Ops:
  7.2 100.2 %all-gather.11.cloned.1.call-start = ((), (), s32[]{:S(2)}) async-start(), calls=%async_computation.9 | async-start | bytes 7962624 | tf_op jit(solution)/shard_map/all_gather | solution.py:132
  7.9 200.8 %all-gather.13.cloned.1.call-start = ((), (), s32[]{:S(2)}) async-start(), calls=%async_computation.10 | async-start | bytes 11943936 | tf_op jit(solution)/shard_map/all_gather | solution.py:136
  13.9 64.1 %all-to-all-start = ((bf16[13,128,576]{2,0,1:T(8,128)(2,1)}), bf16[13,128,576]{2,0,1:T(8,128)(2,1)S(1)}, u32[]{:S(2)}, u32[]{:S(2)}) async-start(bf16[13,128,576]{2,0,1:T(8,128)(2,1)} %copy.101), calls=%async_computation | async-start | bytes 5242880 | tf_op jit(solution)/shard_map/all_to_all | solution.py:158
  18.2 321.1 %all-gather.21.cloned.1.call-start = ((), (), s32[]{:S(2)}) async-start(), calls=%async_computation.21 | async-start | bytes 10223616 | tf_op jit(solution)/shard_map/all_gather | solution.py:167
  250.1 187.1 %copy-start.3 = (bf16[13,64,1,16,72]{4,3,2,1,0:T(8,128)(2,1)}, bf16[13,64,1,16,72]{4,3,2,1,0:T(8,128)(2,1)S(1)}, u32[]{:S(2)}) copy-start(bf16[13,64,1,16,72]{4,3,2,1,0:T(8,128)(2,1)S(1)} %get-tuple-element.143) | copy-start | bytes 5750788
  252.8 174.7 %all-gather.23.cloned.1.call-start = ((), (), s32[]{:S(2)}) async-start(), calls=%async_computation.22 | async-start | bytes 10223616 | tf_op jit(solution)/shard_map/all_gather | solution.py:166
  257.4 211.0 %all-gather.15.cloned.1.call-start = ((), (), s32[]{:S(2)}) async-start(), calls=%async_computation.11 | async-start | bytes 3981312 | tf_op jit(solution)/shard_map/all_gather | solution.py:137
  258.0 342.8 %all-gather.17.cloned.1.call-start = ((), (), s32[]{:S(2)}) async-start(), calls=%async_computation.12 | async-start | bytes 15925248 | tf_op jit(solution)/shard_map/all_gather | solution.py:141
  258.6 474.8 %all-gather.19.cloned.1.call-start = ((), (), s32[]{:S(2)}) async-start(), calls=%async_computation.13 | async-start | bytes 15925248 | tf_op jit(solution)/shard_map/all_gather | solution.py:143
  259.3 665.6 %reduce-scatter.8.cloned.1.call-start = ((), (), s32[]{:S(2)}) async-start(), calls=%async_computation.14 | async-start | bytes 10223616 | tf_op jit(solution)/shard_map/reduce_scatter | solution.py:199
  259.4 341.4 %copy-start.39 = (f32[1152]{0:T(1024)}, f32[1152]{0:T(1024)S(1)}, u32[]{:S(2)}) copy-start(f32[1152]{0:T(1024)S(1)} %convert_element_type.197) | copy-start | bytes 13828
  259.4 341.4 %copy-start.50 = (f32[1152]{0:T(1024)}, f32[1152]{0:T(1024)S(1)}, u32[]{:S(2)}) copy-start(f32[1152]{0:T(1024)S(1)} %convert_element_type.198) | copy-start | bytes 13828
  264.6 181.4 %copy-start.27 = (pred[13,128]{1,0:T(8,128)(4,1)}, pred[13,128]{1,0:T(8,128)(4,1)S(1)}, u32[]{:S(2)}) copy-start(pred[13,128]{1,0:T(8,128)(4,1)S(1)} %iota_compare_fusion) | copy-start | bytes 4996
  474.9 143.6 %copy-start.31 = (f32[832]{0:T(1024)}, f32[832]{0:T(1024)S(1)}, u32[]{:S(2)}) copy-start(f32[832]{0:T(1024)S(1)} %broadcast_multiply_fusion) | copy-start | bytes 9988
  477.0 141.6 %copy-start.43 = (f32[832]{0:T(1024)}, f32[832]{0:T(1024)S(1)}, u32[]{:S(2)}) copy-start(f32[832]{0:T(1024)S(1)} %fusion.38) | copy-start | bytes 9988
  477.6 255.7 %copy-start.7 = (bf16[13,64,1152]{2,1,0:T(8,128)(2,1)S(1)}, bf16[13,64,1152]{2,1,0:T(8,128)(2,1)}, u32[]{:S(2)}) copy-start(bf16[13,64,1152]{2,1,0:T(8,128)(2,1)} %param.20) | copy-start | bytes 5750788
  842.0 168.7 %reduce-scatter.10.cloned.1.call-start = ((), (), s32[]{:S(2)}) async-start(), calls=%async_computation.15 | async-start | bytes 10223616 | tf_op jit(solution)/shard_map/reduce_scatter | solution.py:202
  860.8 286.8 %reduce-scatter.16.cloned.1.call-start = ((), (), s32[]{:S(2)}) async-start(), calls=%async_computation.18 | async-start | bytes 3981312 | tf_op jit(solution)/shard_map/reduce_scatter | solution.py:252
  867.9 284.1 %reduce-scatter.12.cloned.1.call-start = ((), (), s32[]{:S(2)}) async-start(), calls=%async_computation.16 | async-start | bytes 7962624 | tf_op jit(solution)/shard_map/reduce_scatter | solution.py:237
  1085.4 192.6 %reduce-scatter.18.cloned.1.call-start = ((), (), s32[]{:S(2)}) async-start(), calls=%async_computation.19 | async-start | bytes 15925248 | tf_op jit(solution)/shard_map/reduce_scatter | solution.py:264
  1103.9 300.5 %reduce-scatter.20.cloned.1.call-start = ((), (), s32[]{:S(2)}) async-start(), calls=%async_computation.20 | async-start | bytes 15925248 | tf_op jit(solution)/shard_map/reduce_scatter | solution.py:270
  1132.3 369.5 %reduce-scatter.14.cloned.1.call-start = ((), (), s32[]{:S(2)}) async-start(), calls=%async_computation.17 | async-start | bytes 11943936 | tf_op jit(solution)/shard_map/reduce_scatter | solution.py:249
  1147.5 689.6 %all-reduce.21.cloned.1.call-start = ((), (), s32[]{:S(2)}) async-start(), calls=%async_computation.23 | async-start | bytes 37158912 | tf_op jit(solution)/shard_map/psum | solution.py:292
  1534.9 92.7 %all-to-all-start.1 = ((bf16[2,2,239616]{2,1,0:T(2,128)(2,1)}), bf16[2,2,239616]{2,1,0:T(2,128)(2,1)S(1)}, u32[]{:S(2)}, u32[]{:S(2)}) async-start(bf16[2,2,239616]{2,1,0:T(2,128)(2,1)} %reshape.212), calls=%async_computation.3 | async-start | bytes 3833856 | tf_op jit(solution)/shard_map/all_to_all | solution.py:220
  (66 other events, 1088.3 us)
Sparse Core Ops, SparseCore 0:
  9.6 97.7 all-gather.10
  108.9 99.7 all-gather.12
  252.9 86.2 all-gather.20
  341.2 86.2 all-gather.22
  428.9 39.3 all-gather.14
  469.8 130.9 all-gather.16
  602.3 130.9 all-gather.18
  842.1 82.7 reduce-scatter.7
  927.9 82.7 reduce-scatter.9
  1013.4 37.9 reduce-scatter.15
  1085.6 66.3 reduce-scatter.11
  1154.7 123.2 reduce-scatter.17
  1281.0 123.2 reduce-scatter.19
  1407.1 94.6 reduce-scatter.13
  1507.4 329.5 all-reduce.20
where the time goes:
time: 1870 us
  waiting for transfers between devices  1190 us (64%)
  matrix products  252 us (13%)
  local copies, waits for them, and re-layouts  202 us (11%)
  blocking collectives  131 us (7%)
  other arithmetic  62.3 us (3%)
    psum x1, waiting for transfers between devices, per_device(): lax.psum(grad_parts[0].astype(jnp.bfloat16), 'wide').astype(jnp.float32)  191 us
    reduce_scatter x1, waiting for transfers between devices, per_device(): lax.psum_scatter(grad_terms[11].astype(jnp.bfloat16), 'seq', scatter_dime...  126 us
    reduce_scatter x1, waiting for transfers between devices, per_device(): lax.psum_scatter(grad_terms[9].astype(jnp.bfloat16), 'seq', scatter_dimen...  126 us
    all_gather x1, waiting for transfers between devices, per_device(): lax.all_gather(shards[9], 'seq', axis=0, tiled=True)  123 us
    all_gather x1, waiting for transfers between devices, per_device(): lax.all_gather(shards[11], 'seq', axis=0, tiled=True)  115 us
    reduce_scatter x1, waiting for transfers between devices, per_device(): lax.psum_scatter(grad_terms[4].astype(jnp.bfloat16), 'seq', scatter_dimen...  97.4 us
    dot_general x5, matrix products, against(): lax.dot_general(left_side, right_side, (((1,), (1,)), ((), ())), preferre...  92 us
    all_gather x1, waiting for transfers between devices, per_device(): lax.all_gather(shards[4], 'seq', axis=0, tiled=True)  89.9 us
  transfers between devices with their start and end apart: 17, of which 14 were waited for; matrix products, arithmetic and copies ran while one was open for 17% of the time, Pallas kernels for 0%

commit v1 on v0

v1 whole, which is shorter than its diff:
```python
import jax
import jax.numpy as jnp
from jax import lax
from jax.sharding import Mesh
from jax.sharding import PartitionSpec as P

HEAD_DIM = 72

EPS = 1e-05
NEG = -1e30
WIDE = ("z", "x", "c")
BF16 = jnp.bfloat16
F32 = jnp.float32


def across(left_side, right_side):
    return lax.dot_general(
        left_side, right_side, (((0,), (0,)), ((), ())), preferred_element_type=F32
    )


def against(left_side, right_side):
    return lax.dot_general(
        left_side, right_side, (((1,), (1,)), ((), ())), preferred_element_type=F32
    )


def simple(left_side, right_side):
    return jnp.dot(left_side, right_side, preferred_element_type=F32)


def pick(array, index, size, axis=0):
    return lax.dynamic_slice_in_dim(array, index * size, size, axis)


def flip(array, axis):
    return lax.ppermute(array, axis, [(0, 1), (1, 0)])


def ordered(mine, other, index, axis=0):
    return jnp.where(
        index == 0,
        jnp.concatenate([mine, other], axis),
        jnp.concatenate([other, mine], axis),
    )


def fast_mesh():
    return lax.axis_size("seq") == 2 and lax.axis_size("z") == 4


def gather_weight(shard):
    if not fast_mesh():
        return lax.all_gather(shard, "seq", axis=0, tiled=True)
    place = lax.axis_index("x") * 2 + lax.axis_index("c")
    quarter = pick(shard, place, shard.shape[0] // 4)
    other = lax.all_gather(flip(quarter, "seq"), ("x", "c"), axis=0, tiled=True)
    return ordered(shard, other, lax.axis_index("seq"))


def reduce_weight(grad, after=None):
    if not fast_mesh():
        part = lax.psum_scatter(
            grad.astype(BF16), "seq", scatter_dimension=0, tiled=True
        )
        return lax.psum(part, WIDE).astype(F32)
    rows, columns = grad.shape
    core, side = lax.axis_index("c"), lax.axis_index("seq")
    blocks = grad.astype(BF16).reshape(2, 2, rows // 4, columns)

    def block(array, index, axis):
        return lax.dynamic_index_in_dim(array, index, axis, keepdims=False)

    def add(left, right):
        return (left.astype(F32) + right.astype(F32)).astype(BF16)

    chip = add(block(blocks, core, 1), flip(block(blocks, 1 - core, 1), "c"))
    part = add(block(chip, side, 0), flip(block(chip, 1 - side, 0), "seq"))
    if after is not None:
        part, after = lax.optimization_barrier((part, after))
    part = lax.psum(part, ("z", "x"))
    return ordered(part, flip(part, "c"), core).astype(F32)


def gather_vectors(vectors):
    joined = jnp.concatenate(vectors)
    count = joined.shape[0]
    if fast_mesh():
        mine = joined.reshape(1, count)
        everything = ordered(mine, flip(mine, "seq"), lax.axis_index("seq"))
    else:
        everything = lax.all_gather(joined.reshape(1, count), "seq", axis=0, tiled=True)
    out, start = [], 0
    for vector in vectors:
        size = vector.shape[0]
        out.append(everything[:, start : start + size].reshape(-1).astype(F32))
        start += size
    return out


def reduce_vectors(vectors):
    ways = lax.axis_size("seq")
    side = lax.axis_index("seq")
    joined = jnp.concatenate(vectors)
    if fast_mesh():
        joined = jnp.concatenate([joined, jnp.zeros((-joined.shape[0]) % 16384, F32)])
        parts = lax.all_gather(joined.reshape(-1, 1024), WIDE + ("seq",), axis=0)
        total = jnp.sum(parts, 0).reshape(-1)
    else:
        total = lax.psum(joined, WIDE + ("seq",))
    out, start = [], 0
    for vector in vectors:
        size = vector.shape[0] // ways
        out.append(lax.dynamic_slice_in_dim(total, start + side * size, size, 0))
        start += vector.shape[0]
    return out


def share_items(array, per, axis):
    ways, side = lax.axis_size("seq"), lax.axis_index("seq")
    items, size = array.shape[0], array.shape[axis]
    array = jnp.pad(array, [(0, per * ways - items)] + [(0, 0)] * (array.ndim - 1))
    shape = list(array.shape)
    shape[0], shape[axis] = per, size * ways
    whole = jnp.zeros(shape, array.dtype)
    for hop in range(ways):
        piece = pick(array, (side + hop) % ways, per)
        if hop:
            piece = lax.ppermute(
                piece, "seq", [(i, (i + hop) % ways) for i in range(ways)]
            )
        source = (side - hop) % ways
        whole = lax.dynamic_update_slice_in_dim(whole, piece, source * size, axis)
    return whole


def return_items(whole, items, axis):
    ways, side = lax.axis_size("seq"), lax.axis_index("seq")
    per, size = whole.shape[0], whole.shape[axis] // ways
    shape = list(whole.shape)
    shape[0], shape[axis] = per * ways, size
    array = jnp.zeros(shape, whole.dtype)
    for hop in range(ways):
        piece = pick(whole, (side + hop) % ways, size, axis)
        if hop:
            piece = lax.ppermute(
                piece, "seq", [(i, (i + hop) % ways) for i in range(ways)]
            )
        source = (side - hop) % ways
        array = lax.dynamic_update_slice_in_dim(array, piece, source * per, 0)
    return array[:items]


def normalize(hidden):
    mean_val = jnp.mean(hidden, -1, keepdims=True)
    centred = hidden - mean_val
    scale = lax.rsqrt(jnp.mean(centred * centred, -1, keepdims=True) + EPS)
    return centred * scale, scale


def norm_back(grad, hidden, gain):
    xhat, scale = normalize(hidden)
    inner = grad * gain
    back = scale * (
        inner
        - jnp.mean(inner, -1, keepdims=True)
        - xhat * jnp.mean(inner * xhat, -1, keepdims=True)
    )
    return back, jnp.sum(grad * xhat, 0), jnp.sum(grad, 0)


def masked_scores(queries, keys_all, key_valid, score_scale):
    scores = (
        jnp.einsum("iqhd,ikhd->ihqk", queries, keys_all, preferred_element_type=F32)
        * score_scale
    )
    return jnp.where(key_valid[:, None, None, :], scores, NEG)


def attend(queries, keys_all, values_all, key_valid, score_scale):
    scores = masked_scores(queries, keys_all, key_valid, score_scale)
    peak = jnp.max(scores, -1, keepdims=True)
    raised = jnp.exp(scores - peak)
    total = jnp.sum(raised, -1, keepdims=True)
    probs = (raised / total).astype(BF16)
    mixed = jnp.einsum("ihqk,ikhd->iqhd", probs, values_all, preferred_element_type=F32)
    return (mixed.astype(BF16), peak + jnp.log(total))


def attend_back(queries, keys_all, values_all, key_valid, score_scale, log_total, grad_mixed):
    scores = masked_scores(queries, keys_all, key_valid, score_scale)
    probs = jnp.exp(scores - log_total)
    grad_probs = jnp.einsum(
        "iqhd,ikhd->ihqk", grad_mixed, values_all, preferred_element_type=F32
    )
    grad_scores = probs * (grad_probs - jnp.sum(grad_probs * probs, -1, keepdims=True))
    grad_scores = grad_scores.astype(BF16)
    grad_query = (
        jnp.einsum("ihqk,ikhd->iqhd", grad_scores, keys_all, preferred_element_type=F32)
        * score_scale
    )
    grad_key = (
        jnp.einsum("ihqk,iqhd->ikhd", grad_scores, queries, preferred_element_type=F32)
        * score_scale
    )
    grad_value = jnp.einsum(
        "ihqk,iqhd->ikhd", probs.astype(BF16), grad_mixed, preferred_element_type=F32
    )
    return (grad_query, grad_key, grad_value)


def gelu_pair(upper):
    below = 0.5 * (1.0 + lax.erf(upper * 0.7071067811865476))
    bell = jnp.exp(-0.5 * upper * upper) * 0.3989422804014327
    return (upper * below).astype(BF16), (below + upper * bell).astype(BF16)


def per_device(
    latents,
    skip_store,
    lengths,
    cotangent,
    skip_weight,
    skip_bias,
    first_gain,
    first_shift,
    inward_weight,
    outward_weight,
    outward_bias,
    second_gain,
    second_shift,
    expand_weight,
    expand_bias,
    contract_weight,
    contract_bias,
):
    items, slot_dev, width = latents.shape
    ways, side = lax.axis_size("seq"), lax.axis_index("seq")
    slots = slot_dev * ways
    per = -(-items // ways)
    rows = per * slots
    heads = width // HEAD_DIM
    score_scale = HEAD_DIM ** (-0.5)

    live = jnp.pad(lengths, (0, per * ways - items), constant_values=slots)
    live = pick(live, side, per)
    key_valid = jnp.arange(slots, dtype=jnp.int32)[None, :] < live[:, None]

    skip_rows = share_items(skip_store, per, 2)
    latent_rows = share_items(latents, per, 1)
    skip_matrix = gather_weight(skip_weight)
    (
        skip_offset,
        gain_first,
        shift_first,
        outward_offset,
        gain_second,
        shift_second,
        expand_offset,
        contract_offset,
    ) = gather_vectors(
        (
            skip_bias,
            first_gain,
            first_shift,
            outward_bias,
            second_gain,
            second_shift,
            expand_bias,
            contract_bias,
        )
    )
    inward_matrix = gather_weight(inward_weight)
    outward_matrix = gather_weight(outward_weight)
    expand_matrix = gather_weight(expand_weight)
    contract_matrix = gather_weight(contract_weight)
    grad_out = share_items(cotangent, per, 1).reshape(rows, width)

    joined = jnp.concatenate([latent_rows, skip_rows], -1).reshape(rows, 2 * width)
    base = simple(joined, skip_matrix) + skip_offset
    first_normed = (normalize(base)[0] * gain_first + shift_first).astype(BF16)
    qkv_vals = simple(first_normed, inward_matrix).astype(BF16)
    qkv_split = qkv_vals.reshape(per, slots, 3, heads, HEAD_DIM)
    queries, keys_all, values_all = (qkv_split[:, :, i] for i in range(3))
    mixed, log_total = attend(queries, keys_all, values_all, key_valid, score_scale)
    mixed_rows = mixed.reshape(rows, width)
    middle = base + simple(mixed_rows, outward_matrix) + outward_offset
    second_normed = (normalize(middle)[0] * gain_second + shift_second).astype(BF16)
    upper = simple(second_normed, expand_matrix) + expand_offset
    activated, slope = lax.optimization_barrier(gelu_pair(upper))
    result = middle + simple(activated, contract_matrix) + contract_offset
    output = return_items(result.astype(BF16).reshape(per, slots, width), items, 1)

    sum_contract = reduce_weight(across(activated, grad_out))
    grad_result = grad_out.astype(F32)
    grad_contract_off = jnp.sum(grad_result, 0)
    grad_act = against(grad_out, contract_matrix)
    grad_upper = (grad_act * slope.astype(F32)).astype(BF16)
    sum_expand = reduce_weight(across(second_normed, grad_upper), sum_contract)
    grad_expand_off = jnp.sum(grad_upper.astype(F32), 0)
    grad_second = against(grad_upper, expand_matrix)
    grad_mid_ln, grad_gain_two, grad_shift_two = norm_back(
        grad_second, middle, gain_second
    )
    grad_middle = grad_result + grad_mid_ln
    grad_branch = grad_middle.astype(BF16)
    sum_outward = reduce_weight(across(mixed_rows, grad_branch), sum_expand)
    grad_outward_off = jnp.sum(grad_branch.astype(F32), 0)
    grad_mixed = against(grad_branch, outward_matrix).astype(BF16)
    grad_heads = grad_mixed.reshape(per, slots, heads, HEAD_DIM)
    grad_qkv = jnp.stack(
        attend_back(
            queries, keys_all, values_all, key_valid, score_scale, log_total, grad_heads
        ),
        2,
    ).astype(BF16)
    grad_qkv = grad_qkv.reshape(rows, 3 * width)
    sum_inward = reduce_weight(across(first_normed, grad_qkv), sum_outward)
    grad_first = against(grad_qkv, inward_matrix)
    grad_base_ln, grad_gain_one, grad_shift_one = norm_back(
        grad_first, base, gain_first
    )
    grad_base = (grad_middle + grad_base_ln).astype(BF16)
    sum_skipw = reduce_weight(across(joined, grad_base), sum_inward)
    grad_skip_off = jnp.sum(grad_base.astype(F32), 0)
    grad_joined = against(grad_base, skip_matrix).astype(BF16)
    grad_joined = grad_joined.reshape(per, slots, 2 * width)
    grad_latents = return_items(grad_joined[:, :, :width], items, 1).astype(F32)
    grad_skip = return_items(grad_joined[:, :, width:], items, 2)
    (
        sum_skipb,
        sum_gain1,
        sum_shift1,
        sum_outb,
        sum_gain2,
        sum_shift2,
        sum_expandb,
        sum_contractb,
    ) = reduce_vectors(
        (
            grad_skip_off,
            grad_gain_one,
            grad_shift_one,
            grad_outward_off,
            grad_gain_two,
            grad_shift_two,
            grad_expand_off,
            grad_contract_off,
        )
    )
    return (
        output,
        grad_latents,
        grad_skip,
        sum_skipw,
        sum_skipb,
        sum_gain1,
        sum_shift1,
        sum_inward,
        sum_outward,
        sum_outb,
        sum_gain2,
        sum_shift2,
        sum_expand,
        sum_expandb,
        sum_contract,
        sum_contractb,
    )


def solution(mesh):
    wide, seq = mesh.shape["wide"], mesh.shape["seq"]
    devices = mesh.devices.reshape(wide // 4, 2, 2, seq)
    return jax.shard_map(
        per_device,
        mesh=Mesh(devices, WIDE + ("seq",)),
        in_specs=(
            P(WIDE, "seq", None),
            P(WIDE, None, "seq"),
            P(WIDE),
            P(WIDE, "seq", None),
            P("seq", None),
            P("seq"),
            P("seq"),
            P("seq"),
            P("seq", None),
            P("seq", None),
            P("seq"),
            P("seq"),
            P("seq"),
            P("seq", None),
            P("seq"),
            P("seq", None),
            P("seq"),
        ),
        out_specs=(
            P(WIDE, "seq", None),
            P(WIDE, "seq", None),
            P(WIDE, None, "seq"),
            P("seq", None),
            P("seq"),
            P("seq"),
            P("seq"),
            P("seq", None),
            P("seq", None),
            P("seq"),
            P("seq"),
            P("seq"),
            P("seq", None),
            P("seq"),
            P("seq", None),
            P("seq"),
        ),
        check_vma=False,
    )
```

time: 1870 us -> 1150 us (0.61)
  waiting for transfers between devices: 1190 us -> 577 us
  blocking collectives: 131 us -> 0 us
  other arithmetic: 62.3 us -> 90.9 us
  matrix products: 252 us -> 232 us
    reduce_scatter x7 -> x0, waiting for transfers between devices: 488 us -> none  [the longest x1 126 us: per_device(): lax.psum_scatter(grad_terms[11].astype(jnp.bfloat16), 'seq', scatter_dime...]
    all_gather x7 -> x6, waiting for transfers between devices: 512 us -> 47.6 us  [the longest x1 47.6 us: reduce_vectors(): parts = lax.all_gather(joined.reshape(-1, 1024), WIDE + ('seq',), axis=0)]
    psum x1 -> x5, waiting for transfers between devices: 191 us -> 387 us  [reduce_weight(): part = lax.psum(part, ('z', 'x'))]
    ppermute x0 -> x27, waiting for transfers between devices: none -> 142 us  [the longest x21 103 us: flip(): return lax.ppermute(array, axis, [(0, 1), (1, 0)])]
    unnamed x2 -> x0, blocking collectives: 64.4 us -> none
    psum x1 -> x0, blocking collectives: 61.8 us -> none  [per_device(): lax.psum(grad_parts[1].astype(jnp.bfloat16), 'wide').astype(jnp.float32)]
    dynamic_update_slice x0 -> x8, local copies, waits for them, and re-layouts: none -> 42.5 us  [the longest x4 36.2 us: share_items(): whole = lax.dynamic_update_slice_in_dim(whole, piece, source * size, axis)]
    convert_element_type x5 -> x9, local copies, waits for them, and re-layouts: 38.3 us -> 1.93 us  [the longest x1 1.37 us: attend(): return (mixed.astype(BF16), peak + jnp.log(total))]
  transfers between devices with their start and end apart: 17 -> 38, of which waited for: 14 -> 12; matrix products, arithmetic and copies ran while one was open for 17% -> 43% of each run, Pallas kernels for 0% -> 0%
where the time goes in v1:
time: 1150 us; the launch traced here: 1140 us
  waiting for transfers between devices  577 us (50%)
  matrix products  232 us (20%)
  local copies, waits for them, and re-layouts  203 us (18%)
  other arithmetic  90.9 us (8%)
  starting transfers between devices  24.9 us (2%)
  between operations  15.2 us (1%)
    psum x5, waiting for transfers between devices, reduce_weight(): part = lax.psum(part, ('z', 'x'))  387 us
    ppermute x21, waiting for transfers between devices, flip(): return lax.ppermute(array, axis, [(0, 1), (1, 0)])  103 us
    dot_general x5, matrix products, simple(): return jnp.dot(left_side, right_side, preferred_element_type=F32)  79.9 us
    dot_general x5, matrix products, against(): lax.dot_general(left_side, right_side, (((1,), (1,)), ((), ())), preferre...  74.9 us
    dot_general x5, matrix products, across(): lax.dot_general(left_side, right_side, (((0,), (0,)), ((), ())), preferre...  59.4 us
    all_gather x1, waiting for transfers between devices, reduce_vectors(): parts = lax.all_gather(joined.reshape(-1, 1024), WIDE + ('seq',), axis=0)  47.6 us
    unnamed x150, local copies, waits for them, and re-layouts  44.9 us
    ppermute x3, waiting for transfers between devices, share_items(): lax.ppermute(piece, 'seq', [(i, (i + hop) % ways) for i in range(ways)])  39.5 us
  transfers between devices with their start and end apart: 38, of which 12 were waited for; matrix products, arithmetic and copies ran while one was open for 43% of the time, Pallas kernels for 0%

profile of v1, /device:TPU:0, one launch (start us, length us, event | category | flops | bytes accessed | tf_op | source)
XLA Modules:
  0.0 1142.8 jit_solution(4648149488377396882)
XLA Ops:
  11.4 14.9 %collective-permute-done.2 = bf16[288,1152]{1,0:T(8,128)(2,1)S(1)} collective-permute-done((bf16[288,1152]{1,0:T(8,128)(2,1)S(1)}, bf16[288,1152]{1,0:T(8,128)(2,1)S(1)}, u32[]{:S(2)}, u32[]{:S(2)}) %collective-permute-start.2) | collective-permute-done | bytes 663584 | tf_op jit(solution)/shard_map/ppermute | solution.py:37
  30.4 21.5 %collective-permute-done.4 = bf16[144,3456]{1,0:T(8,128)(2,1)S(1)} collective-permute-done((bf16[144,3456]{1,0:T(8,128)(2,1)S(1)}, bf16[144,3456]{1,0:T(8,128)(2,1)S(1)}, u32[]{:S(2)}, u32[]{:S(2)}) %collective-permute-start.4) | collective-permute-done | bytes 995360 | tf_op jit(solution)/shard_map/ppermute | solution.py:37
  65.7 27.4 %collective-permute-done.6 = bf16[144,4608]{1,0:T(8,128)(2,1)S(1)} collective-permute-done((bf16[144,4608]{1,0:T(8,128)(2,1)S(1)}, bf16[144,4608]{1,0:T(8,128)(2,1)S(1)}, u32[]{:S(2)}, u32[]{:S(2)}) %collective-permute-start.6) | collective-permute-done | bytes 1327136 | tf_op jit(solution)/shard_map/ppermute | solution.py:37
  114.6 15.8 %dynamic_update_slice.38 = bf16[7,128,1152]{2,1,0:T(8,128)(2,1)} dynamic-update-slice(bf16[7,128,1152]{2,1,0:T(8,128)(2,1)} %broadcast.103.clone, bf16[7,128,576]{2,1,0:T(8,128)(2,1)S(1)} %copy.71, s32[]{:T(128)} %constant.182.clone.1, s32[]{:T(128)} %constant.182.clone.1, s32[]{:T(128)S(6)} %select_n.271) | dynamic-update-slice | bytes 2064388 | tf_op jit(solution)/shard_map/dynamic_update_slice | solution.py:133
  133.7 16.6 %dynamic_update_slice.39 = bf16[7,128,1152]{2,1,0:T(8,128)(2,1)} dynamic-update-slice(bf16[7,128,1152]{2,1,0:T(8,128)(2,1)} %dynamic_update_slice.38, bf16[7,128,576]{2,1,0:T(8,128)(2,1)S(1)} %copy.72, s32[]{:T(128)} %constant.182.clone.1, s32[]{:T(128)} %constant.182.clone.1, s32[]{:T(128)S(6)} %select_n.272) | dynamic-update-slice | bytes 2064388 | tf_op jit(solution)/shard_map/dynamic_update_slice | solution.py:133
  152.7 39.5 %collective-permute-done.9 = bf16[7,64,1152]{2,1,0:T(8,128)(2,1)} collective-permute-done((bf16[7,64,1152]{2,1,0:T(8,128)(2,1)}, bf16[7,64,1152]{2,1,0:T(8,128)(2,1)}, u32[]{:S(2)}, u32[]{:S(2)}) %collective-permute-start.9) | collective-permute-done | bytes 1032224 | tf_op jit(solution)/shard_map/ppermute | solution.py:129
  198.5 10.8 fusion.80
  211.9 15.5 %convolution_convert_fusion.5 = bf16[896,3456]{1,0:T(8,128)(2,1)} fusion(bf16[576,3456]{1,0:T(8,128)(2,1)} %all-gather.9.cloned.1.call-done, bf16[576,3456]{1,0:T(8,128)(2,1)} %param.25, pred[]{:T(512)S(6)} %eq.40, f32[896,1152]{1,0:T(8,128)} %copy-done.13, f32[1152]{0:T(1024)S(1)} %reshape.245, f32[1152]{0:T(1024)S(1)} %reshape.244, ...), kind=kOutput, calls=%fused_computation.30 | convolution fusion | flops 7178600448 | bytes 18300928 | tf_op jit(solution)/shard_map/dot_general | solution.py:29
  227.5 21.1 %reshape.261 = bf16[7,128,3,16,72]{4,3,2,1,0:T(8,128)(2,1)} reshape(bf16[896,3456]{1,0:T(8,128)(2,1)} %convolution_convert_fusion.5) | data formatting | bytes 12386304 | tf_op jit(solution)/shard_map/reshape | solution.py:283
  296.5 24.4 %fusion.4 = (bf16[896,4608]{1,0:T(8,128)(2,1)}, bf16[896,4608]{1,0:T(8,128)(2,1)}) fusion(f32[4608]{0:T(1024)S(1)} %reshape.249, bf16[576,4608]{1,0:T(8,128)(2,1)} %all-gather.13.cloned.1.call-done, bf16[576,4608]{1,0:T(8,128)(2,1)} %param.30, pred[]{:T(512)S(6)} %eq.40, f32[896,1152]{1,0:T(8,128)} %copy-done.12, f32[1152]{0:T(1024)S(1)} %reshape.248, ...), kind=kOutput, calls=%fused_computation.7 | convolution fusion | flops 9615163392 | bytes 31295488 | tf_op jit(solution)/shard_map/dot_general | solution.py:29
  321.0 14.6 %convolution_convert_fusion = bf16[4608,1152]{1,0:T(8,128)(2,1)S(1)} fusion(bf16[896,4608]{1,0:T(8,128)(2,1)} %get-tuple-element.22, bf16[896,1152]{1,0:T(8,128)(2,1)S(1)} %bitcast.154), kind=kOutput, calls=%fused_computation.1 | convolution fusion | flops 9517989888 | bytes 20938752 | tf_op jit(solution)/shard_map/dot_general | solution.py:17
  341.3 19.9 %convert_reduce_fusion = (f32[4608]{0:T(1024)}, bf16[896,4608]{1,0:T(8,128)(2,1)}) fusion(bf16[896,4608]{1,0:T(8,128)(2,1)} %get-tuple-element.23, bf16[896,1152]{1,0:T(8,128)(2,1)S(1)} %bitcast.155, bf16[2304,1152]{1,0:T(8,128)(2,1)} %all-gather.15.cloned.1.call-done, bf16[2304,1152]{1,0:T(8,128)(2,1)} %param.32, pred[]{:T(512)S(6)} %eq.40), kind=kOutput, calls=%fused_computation.8 | convolution fusion | flops 9581096960 | bytes 29214720 | tf_op jit(solution)/shard_map/dot_general | solution.py:23
  361.1 22.0 %multiply_reduce_fusion.1 = (f32[1152]{0:T(1024)}, f32[896]{0:T(1024)S(1)}, f32[896]{0:T(1024)S(1)}, f32[1152]{0:T(1024)}, f32[896,1152]{1,0:T(8,128)}) fusion(f32[896,1152]{1,0:T(8,128)} %copy-done.12, f32[896]{0:T(1024)S(1)} %add_rsqrt_fusion, f32[896]{0:T(1024)S(1)} %broadcast_multiply_fusion.4, f32[1152]{0:T(1024)S(1)} %reshape.247, ...), kind=kOutput, calls=%fused_computation.60 | convolution fusion | flops 9569742848 | bytes 27160064 | tf_op jit(solution)/shard_map/dot_general | solution.py:23
  406.9 18.1 %convolution_convert_fusion.1 = bf16[1152,4608]{1,0:T(8,128)(2,1)} fusion(bf16[896,4608]{1,0:T(8,128)(2,1)} %get-tuple-element.84, f32[896,1152]{1,0:T(8,128)} %copy-done.12, f32[1152]{0:T(1024)S(1)} %reshape.248, f32[1152]{0:T(1024)S(1)} %reshape.247, f32[896]{0:T(1024)S(1)} %add_rsqrt_fusion, f32[896]{0:T(1024)S(1)} %broadcast_multiply_fusion.4), kind=kOutput, calls=%fused_computation.2 | convolution fusion | flops 9523150848 | bytes 23019520 | tf_op jit(solution)/shard_map/dot_general | solution.py:17
  465.8 32.3 %collective-permute-done.21 = bf16[1152,1152]{1,0:T(8,128)(2,1)} collective-permute-done((bf16[1152,1152]{1,0:T(8,128)(2,1)}, bf16[1152,1152]{1,0:T(8,128)(2,1)}, u32[]{:S(2)}, u32[]{:S(2)}) %collective-permute-start.21) | collective-permute-done | bytes 2654240 | tf_op jit(solution)/shard_map/ppermute | solution.py:37
  513.0 15.1 %convolution_convert_fusion.2 = bf16[1152,3456]{1,0:T(8,128)(2,1)} fusion(bf16[432,8,7,128]{3,2,1,0:T(8,128)(2,1)} %bitcast.162, f32[896,1152]{1,0:T(8,128)S(1)} %copy-done.14, f32[1152]{0:T(1024)S(1)} %copy-done.53, f32[1152]{0:T(1024)S(1)} %copy-done.43, f32[896]{0:T(1024)S(1)} %copy-done.49, f32[896]{0:T(1024)S(1)} %copy-done.40), kind=kOutput, calls=%fused_computation.12 | convolution fusion | flops 7143653376 | bytes 18300928 | tf_op jit(solution)/shard_map/dot_general | solution.py:17
  528.1 90.3 %all-reduce.10.cloned.1.call-done = bf16[1152,1152]{1,0:T(8,128)(2,1)} async-done(((bf16[1152,1152]{1,0:T(8,128)(2,1)}), bf16[1152,1152]{1,0:T(8,128)(2,1)}) %all-reduce.10.cloned.1.call-update) | async-done | bytes 2654224 | tf_op jit(solution)/shard_map/psum | solution.py:81
  640.5 20.3 %multiply_reduce_fusion.2 = (f32[1152]{0:T(1024)S(1)}, f32[896]{0:T(1024)S(1)}, f32[896]{0:T(1024)S(1)}, f32[1152]{0:T(1024)S(1)}, f32[896,1152]{1,0:T(8,128)}) fusion(f32[896,1152]{1,0:T(8,128)} %copy-done.13, f32[896]{0:T(1024)S(1)} %copy-done.49, f32[896]{0:T(1024)S(1)} %copy-done.40, f32[1152]{0:T(1024)S(1)} %copy-done.43, ...), kind=kOutput, calls=%fused_computation.62 | convolution fusion | flops 7179628544 | bytes 22441472 | tf_op jit(solution)/shard_map/dot_general | solution.py:23
  664.5 91.6 %all-reduce.12.cloned.1.call-done = bf16[288,4608]{1,0:T(8,128)(2,1)} async-done(((bf16[288,4608]{1,0:T(8,128)(2,1)}), bf16[288,4608]{1,0:T(8,128)(2,1)}) %all-reduce.12.cloned.1.call-update) | async-done | bytes 2654224 | tf_op jit(solution)/shard_map/psum | solution.py:81
  793.2 59.7 %all-reduce.14.cloned.1.call-done = bf16[288,1152]{1,0:T(8,128)(2,1)} async-done(((bf16[288,1152]{1,0:T(8,128)(2,1)}), bf16[288,1152]{1,0:T(8,128)(2,1)}) %all-reduce.14.cloned.1.call-update) | async-done | bytes 663568 | tf_op jit(solution)/shard_map/psum | solution.py:81
  865.5 91.9 %all-reduce.16.cloned.1.call-done = bf16[288,3456]{1,0:T(8,128)(2,1)} async-done(((bf16[288,3456]{1,0:T(8,128)(2,1)}), bf16[288,3456]{1,0:T(8,128)(2,1)}) %all-reduce.16.cloned.1.call-update) | async-done | bytes 1990672 | tf_op jit(solution)/shard_map/psum | solution.py:81
  957.5 20.8 %fusion.28 = bf16[896,1152]{1,0:T(8,128)(2,1)} fusion(f32[896,1152]{1,0:T(8,128)} %copy-done.12, bf16[896,4608]{1,0:T(8,128)(2,1)} %get-tuple-element.22, f32[1152]{0:T(1024)S(1)} %reshape.250, bf16[2304,1152]{1,0:T(8,128)(2,1)} %all-gather.15.cloned.1.call-done, bf16[2304,1152]{1,0:T(8,128)(2,1)} %param.32, pred[]{:T(512)S(6)} %eq.40), kind=kOutput, calls=%fused_computation.86 | convolution fusion | flops 9563553792 | bytes 25072128 | tf_op jit(solution)/shard_map/dot_general | solution.py:29
  1017.0 53.5 %all-reduce.18.cloned.1.call-done = bf16[576,1152]{1,0:T(8,128)(2,1)} async-done(((bf16[576,1152]{1,0:T(8,128)(2,1)}), bf16[576,1152]{1,0:T(8,128)(2,1)}) %all-reduce.18.cloned.1.call-update) | async-done | bytes 1327120 | tf_op jit(solution)/shard_map/psum | solution.py:81
  1082.2 47.6 %all-gather.17.cloned.1.call-done = f32[32,16,1024]{2,1,0:T(8,128)} async-done(((f32[1,16,1024]{2,1,0:T(8,128)}), f32[32,16,1024]{2,1,0:T(8,128)}) %all-gather.17.cloned.1.call-update) | async-done | bytes 2097168 | tf_op jit(solution)/shard_map/all_gather | solution.py:107
  (336 shorter events, 322.5 us)
Async XLA Ops:
  7.2 191.3 %all-gather.7.cloned.1.call-start = ((), (), s32[]{:S(2)}) async-start(), calls=%async_computation | async-start | bytes 3317760 | tf_op jit(solution)/shard_map/all_gather | solution.py:57
  27.3 184.6 %all-gather.9.cloned.1.call-start = ((), (), s32[]{:S(2)}) async-start(), calls=%async_computation.1 | async-start | bytes 4976640 | tf_op jit(solution)/shard_map/all_gather | solution.py:57
  52.9 232.8 %all-gather.11.cloned.1.call-start = ((), (), s32[]{:S(2)}) async-start(), calls=%async_computation.2 | async-start | bytes 1658880 | tf_op jit(solution)/shard_map/all_gather | solution.py:57
  62.9 233.6 %all-gather.13.cloned.1.call-start = ((), (), s32[]{:S(2)}) async-start(), calls=%async_computation.3 | async-start | bytes 6635520 | tf_op jit(solution)/shard_map/all_gather | solution.py:57
  94.2 247.1 %all-gather.15.cloned.1.call-start = ((), (), s32[]{:S(2)}) async-start(), calls=%async_computation.4 | async-start | bytes 6635520 | tf_op jit(solution)/shard_map/all_gather | solution.py:57
  105.8 92.4 %collective-permute-start.7 = (bf16[576,1152]{1,0:T(8,128)(2,1)}, bf16[576,1152]{1,0:T(8,128)(2,1)}, u32[]{:S(2)}, u32[]{:S(2)}) collective-permute-start(bf16[576,1152]{1,0:T(8,128)(2,1)} %constant_dynamic-slice_fusion.4), channel_id=1, source_target_pairs={{0,1},{1,0},{2,3},{3,2},{4,5},{5,4},{6,7},{7,6},{8,9},{9,8},{10,11... | collective-permute-start | bytes 3981320 | tf_op jit(solution)/shard_map/ppermute | solution.py:37
  110.0 82.2 %collective-permute-start.9 = (bf16[7,64,1152]{2,1,0:T(8,128)(2,1)}, bf16[7,64,1152]{2,1,0:T(8,128)(2,1)}, u32[]{:S(2)}, u32[]{:S(2)}) collective-permute-start(bf16[7,64,1152]{2,1,0:T(8,128)(2,1)} %get-tuple-element.53), channel_id=1, source_target_pairs={{0,1},{1,0},{2,3},{3,2},{4,5},{5,4},{6,7},{7,6},{8,9},{9,8},{10,11... | collective-permute-start | bytes 3096584 | tf_op jit(solution)/shard_map/ppermute | solution.py:129
  198.2 420.1 %all-reduce.10.cloned.1.call-start = ((), (), s32[]{:S(2)}) async-start(), calls=%async_computation.5 | async-start | bytes 5308416 | tf_op jit(solution)/shard_map/psum | solution.py:81
  341.3 89.7 %collective-permute-start.20 = (bf16[2,1152,1152]{2,1,0:T(8,128)(2,1)}, bf16[2,1152,1152]{2,1,0:T(8,128)(2,1)}, u32[]{:S(2)}, u32[]{:S(2)}) collective-permute-start(bf16[2,1152,1152]{2,1,0:T(8,128)(2,1)} %dynamic-slice_bitcast_fusion), channel_id=1, source_target_pairs={{0,2},{2,0},{1,3},{3,1},{4,6},{6,4},{5,7},{7,5},{8,10},{10,8},{9,1... | collective-permute-start | bytes 15925256 | tf_op jit(solution)/shard_map/ppermute | solution.py:37
  430.5 71.5 %collective-permute-start.18 = (bf16[2,288,4608]{2,1,0:T(8,128)(2,1)}, bf16[2,288,4608]{2,1,0:T(8,128)(2,1)}, u32[]{:S(2)}, u32[]{:S(2)}) collective-permute-start(bf16[2,288,4608]{2,1,0:T(8,128)(2,1)} %dynamic-slice_bitcast_fusion.1), channel_id=1, source_target_pairs={{0,2},{2,0},{1,3},{3,1},{4,6},{6,4},{5,7},{7,5},{8,10},{10,8},{9,1... | collective-permute-start | bytes 15925256 | tf_op jit(solution)/shard_map/ppermute | solution.py:37
  502.0 254.2 %all-reduce.12.cloned.1.call-start = ((), (), s32[]{:S(2)}) async-start(), calls=%async_computation.6 | async-start | bytes 5308416 | tf_op jit(solution)/shard_map/psum | solution.py:81
  511.5 118.0 %collective-permute-start.19 = (bf16[288,4608]{1,0:T(8,128)(2,1)}, bf16[288,4608]{1,0:T(8,128)(2,1)}, u32[]{:S(2)}, u32[]{:S(2)}) collective-permute-start(bf16[288,4608]{1,0:T(8,128)(2,1)} %dynamic-slice_bitcast_fusion.4), channel_id=1, source_target_pairs={{0,1},{1,0},{2,3},{3,2},{4,5},{5,4},{6,7},{7,6},{8,9},{9,8},{10,11... | collective-permute-start | bytes 7962632 | tf_op jit(solution)/shard_map/ppermute | solution.py:37
  622.9 141.2 %collective-permute-start.14 = (bf16[2,288,3456]{2,1,0:T(8,128)(2,1)}, bf16[2,288,3456]{2,1,0:T(8,128)(2,1)}, u32[]{:S(2)}, u32[]{:S(2)}) collective-permute-start(bf16[2,288,3456]{2,1,0:T(8,128)(2,1)} %dynamic-slice_bitcast_fusion.2), channel_id=1, source_target_pairs={{0,2},{2,0},{1,3},{3,1},{4,6},{6,4},{5,7},{7,5},{8,10},{10,8},{9,1... | collective-permute-start | bytes 11943944 | tf_op jit(solution)/shard_map/ppermute | solution.py:37
  640.4 212.4 %all-reduce.14.cloned.1.call-start = ((), (), s32[]{:S(2)}) async-start(), calls=%async_computation.7 | async-start | bytes 1327104 | tf_op jit(solution)/shard_map/psum | solution.py:81
  663.4 98.2 %collective-permute-start.17 = (bf16[288,1152]{1,0:T(8,128)(2,1)}, bf16[288,1152]{1,0:T(8,128)(2,1)}, u32[]{:S(2)}, u32[]{:S(2)}) collective-permute-start(bf16[288,1152]{1,0:T(8,128)(2,1)} %dynamic-slice_bitcast_fusion.9), channel_id=1, source_target_pairs={{0,1},{1,0},{2,3},{3,2},{4,5},{5,4},{6,7},{7,6},{8,9},{9,8},{10,11... | collective-permute-start | bytes 1990664 | tf_op jit(solution)/shard_map/ppermute | solution.py:37
  771.8 81.1 %collective-permute-start.15 = (bf16[288,3456]{1,0:T(8,128)(2,1)}, bf16[288,3456]{1,0:T(8,128)(2,1)}, u32[]{:S(2)}, u32[]{:S(2)}) collective-permute-start(bf16[288,3456]{1,0:T(8,128)(2,1)} %dynamic-slice_bitcast_fusion.6), channel_id=1, source_target_pairs={{0,1},{1,0},{2,3},{3,2},{4,5},{5,4},{6,7},{7,6},{8,9},{9,8},{10,11... | collective-permute-start | bytes 5971976 | tf_op jit(solution)/shard_map/ppermute | solution.py:37
  780.7 176.8 %all-reduce.16.cloned.1.call-start = ((), (), s32[]{:S(2)}) async-start(), calls=%async_computation.8 | async-start | bytes 3981312 | tf_op jit(solution)/shard_map/psum | solution.py:81
  793.0 66.7 %collective-permute-start.12 = (bf16[2,576,1152]{2,1,0:T(8,128)(2,1)}, bf16[2,576,1152]{2,1,0:T(8,128)(2,1)}, u32[]{:S(2)}, u32[]{:S(2)}) collective-permute-start(bf16[2,576,1152]{2,1,0:T(8,128)(2,1)} %dynamic-slice_bitcast_fusion.5), channel_id=1, source_target_pairs={{0,2},{2,0},{1,3},{3,1},{4,6},{6,4},{5,7},{7,5},{8,10},{10,8},{9,1... | collective-permute-start | bytes 7962632 | tf_op jit(solution)/shard_map/ppermute | solution.py:37
  858.6 211.9 %all-reduce.18.cloned.1.call-start = ((), (), s32[]{:S(2)}) async-start(), calls=%async_computation.9 | async-start | bytes 2654208 | tf_op jit(solution)/shard_map/psum | solution.py:81
  864.1 114.2 %collective-permute-start.13 = (bf16[576,1152]{1,0:T(8,128)(2,1)}, bf16[576,1152]{1,0:T(8,128)(2,1)}, u32[]{:S(2)}, u32[]{:S(2)}) collective-permute-start(bf16[576,1152]{1,0:T(8,128)(2,1)} %dynamic-slice_bitcast_fusion.8), channel_id=1, source_target_pairs={{0,1},{1,0},{2,3},{3,2},{4,5},{5,4},{6,7},{7,6},{8,9},{9,8},{10,11... | collective-permute-start | bytes 3981320 | tf_op jit(solution)/shard_map/ppermute | solution.py:37
  987.2 142.6 %all-gather.17.cloned.1.call-start = ((), (), s32[]{:S(2)}) async-start(), calls=%async_computation.10 | async-start | bytes 2162688 | tf_op jit(solution)/shard_map/all_gather | solution.py:107
  992.0 78.5 %collective-permute-start.8 = (bf16[7,64,1152]{2,1,0:T(8,128)(2,1)}, bf16[7,64,1152]{2,1,0:T(8,128)(2,1)}, u32[]{:S(2)}, u32[]{:S(2)}) collective-permute-start(bf16[7,64,1152]{2,1,0:T(8,128)(2,1)} %get-tuple-element.51), channel_id=1, source_target_pairs={{0,1},{1,0},{2,3},{3,2},{4,5},{5,4},{6,7},{7,6},{8,9},{9,8},{10,11... | collective-permute-start | bytes 3096584 | tf_op jit(solution)/shard_map/ppermute | solution.py:146
  1008.8 67.0 %collective-permute-start.11 = (bf16[7,128,576]{1,2,0:T(8,128)(2,1)}, bf16[7,128,576]{1,2,0:T(8,128)(2,1)}, u32[]{:S(2)}, u32[]{:S(2)}) collective-permute-start(bf16[7,128,576]{1,2,0:T(8,128)(2,1)} %copy.105), channel_id=1, source_target_pairs={{0,1},{1,0},{2,3},{3,2},{4,5},{5,4},{6,7},{7,6},{8,9},{9,8},{10,11... | collective-permute-start | bytes 3096584 | tf_op jit(solution)/shard_map/ppermute | solution.py:146
  1012.1 66.5 %collective-permute-start.10 = (bf16[7,64,1152]{2,1,0:T(8,128)(2,1)}, bf16[7,64,1152]{2,1,0:T(8,128)(2,1)}, u32[]{:S(2)}, u32[]{:S(2)}) collective-permute-start(bf16[7,64,1152]{2,1,0:T(8,128)(2,1)} %get-tuple-element.49), channel_id=1, source_target_pairs={{0,1},{1,0},{2,3},{3,2},{4,5},{5,4},{6,7},{7,6},{8,9},{9,8},{10,11... | collective-permute-start | bytes 3096584 | tf_op jit(solution)/shard_map/ppermute | solution.py:146
  (82 other events, 1816.0 us)
Sparse Core Ops, SparseCore 0:
  27.3 27.2 all-gather.6
  56.7 33.2 all-gather.8
  91.6 18.2 all-gather.10
  111.9 40.8 all-gather.12
  198.4 40.9 all-gather.14
  502.1 116.2 all-reduce.9
  640.5 115.5 all-reduce.11
  780.8 72.0 all-reduce.13
  858.7 98.6 all-reduce.15
  987.3 83.1 all-reduce.17
  1074.1 55.6 all-gather.16

commit v2 on v1

--- a/solution.py
+++ b/solution.py
@@ -1,6 +1,8 @@
 import jax
 import jax.numpy as jnp
 from jax import lax
+from jax.experimental import pallas as pl
+from jax.experimental.pallas import tpu as pltpu
 from jax.sharding import Mesh
 from jax.sharding import PartitionSpec as P
 
@@ -58,28 +60,47 @@
     return ordered(shard, other, lax.axis_index("seq"))
 
 
-def reduce_weight(grad, after=None):
+def swap(array, axis, step):
+    ways = lax.axis_size(axis)
+    return lax.ppermute(array, axis, [(i, i ^ step) for i in range(ways)])
+
+
+def add(left, right):
+    return (left.astype(F32) + right.astype(F32)).astype(BF16)
+
+
+def block(array, index, axis):
+    return lax.dynamic_index_in_dim(array, index, axis, keepdims=False)
+
+
+def fold(blocks, axis):
+    index = lax.axis_index(axis)
+    return add(block(blocks, index, 0), flip(block(blocks, 1 - index, 0), axis))
+
+
+def spread(part, axis):
+    return ordered(part, flip(part, axis), lax.axis_index(axis))
+
+
+def reduce_weight(grad, offload=False):
     if not fast_mesh():
         part = lax.psum_scatter(
             grad.astype(BF16), "seq", scatter_dimension=0, tiled=True
         )
         return lax.psum(part, WIDE).astype(F32)
     rows, columns = grad.shape
-    core, side = lax.axis_index("c"), lax.axis_index("seq")
+    core = lax.axis_index("c")
     blocks = grad.astype(BF16).reshape(2, 2, rows // 4, columns)
-
-    def block(array, index, axis):
-        return lax.dynamic_index_in_dim(array, index, axis, keepdims=False)
-
-    def add(left, right):
-        return (left.astype(F32) + right.astype(F32)).astype(BF16)
-
     chip = add(block(blocks, core, 1), flip(block(blocks, 1 - core, 1), "c"))
-    part = add(block(chip, side, 0), flip(block(chip, 1 - side, 0), "seq"))
-    if after is not None:
-        part, after = lax.optimization_barrier((part, after))
-    part = lax.psum(part, ("z", "x"))
-    return ordered(part, flip(part, "c"), core).astype(F32)
+    part = fold(chip, "seq")
+    if offload:
+        part = lax.psum(part, ("z", "x"))
+    else:
+        part = fold(part.reshape(2, rows // 8, columns), "x")
+        part = add(part, swap(part, "z", 1))
+        part = add(part, swap(part, "z", 2))
+        part = spread(part, "x")
+    return spread(part, "c").astype(F32)
 
 
 def gather_vectors(vectors):
@@ -120,6 +141,10 @@
     ways, side = lax.axis_size("seq"), lax.axis_index("seq")
     items, size = array.shape[0], array.shape[axis]
     array = jnp.pad(array, [(0, per * ways - items)] + [(0, 0)] * (array.ndim - 1))
+    if ways == 2:
+        return ordered(
+            pick(array, side, per), flip(pick(array, 1 - side, per), "seq"), side, axis
+        )
     shape = list(array.shape)
     shape[0], shape[axis] = per, size * ways
     whole = jnp.zeros(shape, array.dtype)
@@ -137,6 +162,10 @@
 def return_items(whole, items, axis):
     ways, side = lax.axis_size("seq"), lax.axis_index("seq")
     per, size = whole.shape[0], whole.shape[axis] // ways
+    if ways == 2:
+        mine = pick(whole, side, size, axis)
+        other = flip(pick(whole, 1 - side, size, axis), "seq")
+        return ordered(mine, other, side)[:items]
     shape = list(whole.shape)
     shape[0], shape[axis] = per * ways, size
     array = jnp.zeros(shape, whole.dtype)
@@ -169,44 +198,149 @@
     return back, jnp.sum(grad * xhat, 0), jnp.sum(grad, 0)
 
 
-def masked_scores(queries, keys_all, key_valid, score_scale):
-    scores = (
-        jnp.einsum("iqhd,ikhd->ihqk", queries, keys_all, preferred_element_type=F32)
-        * score_scale
-    )
-    return jnp.where(key_valid[:, None, None, :], scores, NEG)
-
-
-def attend(queries, keys_all, values_all, key_valid, score_scale):
-    scores = masked_scores(queries, keys_all, key_valid, score_scale)
-    peak = jnp.max(scores, -1, keepdims=True)
-    raised = jnp.exp(scores - peak)
-    total = jnp.sum(raised, -1, keepdims=True)
-    probs = (raised / total).astype(BF16)
-    mixed = jnp.einsum("ihqk,ikhd->iqhd", probs, values_all, preferred_element_type=F32)
-    return (mixed.astype(BF16), peak + jnp.log(total))
-
-
-def attend_back(queries, keys_all, values_all, key_valid, score_scale, log_total, grad_mixed):
-    scores = masked_scores(queries, keys_all, key_valid, score_scale)
-    probs = jnp.exp(scores - log_total)
-    grad_probs = jnp.einsum(
-        "iqhd,ikhd->ihqk", grad_mixed, values_all, preferred_element_type=F32
-    )
-    grad_scores = probs * (grad_probs - jnp.sum(grad_probs * probs, -1, keepdims=True))
-    grad_scores = grad_scores.astype(BF16)
-    grad_query = (
-        jnp.einsum("ihqk,ikhd->iqhd", grad_scores, keys_all, preferred_element_type=F32)
-        * score_scale
-    )
-    grad_key = (
-        jnp.einsum("ihqk,iqhd->ikhd", grad_scores, queries, preferred_element_type=F32)
-        * score_scale
-    )
-    grad_value = jnp.einsum(
-        "ihqk,iqhd->ikhd", probs.astype(BF16), grad_mixed, preferred_element_type=F32
-    )
-    return (grad_query, grad_key, grad_value)
+LANES = 128
+
+
+def head_window(head):
+    start = head * HEAD_DIM
+    first = start // LANES * LANES
+    size = LANES if start + HEAD_DIM <= first + LANES else 2 * LANES
+    return first, size, start - first
+
+
+def head_mask(size, offset):
+    lane = lax.broadcasted_iota(jnp.int32, (1, size), 1)
+    return (lane >= offset) & (lane < offset + HEAD_DIM)
+
+
+def head_groups(width, slots):
+    heads = [(head,) + head_window(head) for head in range(width // HEAD_DIM)]
+    count = max(1, 2048 // slots)
+    return [heads[i : i + count] for i in range(0, len(heads), count)]
+
+
+def masked(ref, first, size, offset):
+    return jnp.where(head_mask(size, offset), ref[:, first : first + size], 0)
+
+
+def place(ref, start, size, offset, result):
+    result = result.astype(BF16)
+    if offset:
+        result = jnp.where(
+            head_mask(size, offset), result, ref[:, start : start + size]
+        )
+    ref[:, start : start + size] = result
+
+
+def attend_kernel(lengths, qkv, mixed, probs_out):
+    slots, width = mixed.shape
+    live = lax.broadcasted_iota(jnp.int32, (1, slots), 1) < lengths[pl.program_id(0)]
+    for group in head_groups(width, slots):
+        scores = [
+            against(
+                masked(qkv, first, size, offset),
+                qkv[:, width + first : width + first + size],
+            )
+            for _, first, size, offset in group
+        ]
+        scores = [jnp.where(live, s * HEAD_DIM ** (-0.5), NEG) for s in scores]
+        raised = [jnp.exp(s - jnp.max(s, -1, keepdims=True)) for s in scores]
+        probs = [
+            (r * (1.0 / jnp.sum(r, -1, keepdims=True))).astype(BF16) for r in raised
+        ]
+        results = [
+            simple(p, qkv[:, 2 * width + first : 2 * width + first + size])
+            for p, (_, first, size, _) in zip(probs, group)
+        ]
+        for p, result, (head, first, size, offset) in zip(probs, results, group):
+            probs_out[head * slots : (head + 1) * slots, :] = p
+            place(mixed, first, size, offset, result)
+
+
+def attend(qkv, lengths):
+    per = lengths.shape[0]
+    rows, width = qkv.shape[0], qkv.shape[1] // 3
+    slots, heads = rows // per, width // HEAD_DIM
+    return pl.pallas_call(
+        attend_kernel,
+        out_shape=(
+            jax.ShapeDtypeStruct((rows, width), BF16),
+            jax.ShapeDtypeStruct((rows * heads, slots), BF16),
+        ),
+        grid_spec=pltpu.PrefetchScalarGridSpec(
+            num_scalar_prefetch=1,
+            grid=(per,),
+            in_specs=[pl.BlockSpec((slots, 3 * width), lambda i, _: (i, 0))],
+            out_specs=(
+                pl.BlockSpec((slots, width), lambda i, _: (i, 0)),
+                pl.BlockSpec((heads * slots, slots), lambda i, _: (i, 0)),
+            ),
+        ),
+        compiler_params=pltpu.CompilerParams(vmem_limit_bytes=56 << 20),
+        cost_estimate=pl.CostEstimate(
+            flops=4 * rows * slots * width,
+            transcendentals=rows * slots * heads,
+            bytes_accessed=8 * rows * width + 2 * rows * heads * slots,
+        ),
+        name="attend",
+    )(lengths, qkv)
+
+
+def attend_back_kernel(qkv, probs_in, grad_mixed, grad_qkv):
+    slots, width = grad_mixed.shape
+    scale = HEAD_DIM ** (-0.5)
+    for group in head_groups(width, slots):
+        grads = [masked(grad_mixed, *window) for _, *window in group]
+        grad_probs = [
+            against(g, qkv[:, 2 * width + first : 2 * width + first + size])
+            for g, (_, first, size, _) in zip(grads, group)
+        ]
+        probs = [
+            probs_in[head * slots : (head + 1) * slots, :] for head, _, _, _ in group
+        ]
+        grad_values = [across(p, g) for p, g in zip(probs, grads)]
+        probs = [p.astype(F32) for p in probs]
+        sums = [
+            jnp.sum(g * p, -1, keepdims=True) for g, p in zip(grad_probs, probs)
+        ]
+        scores = [
+            (p * (g - total)).astype(BF16)
+            for p, g, total in zip(probs, grad_probs, sums)
+        ]
+        grad_queries = [
+            simple(s, qkv[:, width + first : width + first + size]) * scale
+            for s, (_, first, size, _) in zip(scores, group)
+        ]
+        grad_keys = [
+            across(s, qkv[:, first : first + size]) * scale
+            for s, (_, first, size, _) in zip(scores, group)
+        ]
+        for part, results in enumerate((grad_queries, grad_keys, grad_values)):
+            for result, (_, first, size, offset) in zip(results, group):
+                place(grad_qkv, part * width + first, size, offset, result)
+
+
+def attend_back(qkv, probs, grad_mixed, per):
+    rows, width = grad_mixed.shape
+    slots, heads = rows // per, width // HEAD_DIM
+    return pl.pallas_call(
+        attend_back_kernel,
+        out_shape=jax.ShapeDtypeStruct((rows, 3 * width), BF16),
+        grid=(per,),
+        in_specs=[
+            pl.BlockSpec((slots, 3 * width), lambda i: (i, 0)),
+            pl.BlockSpec((heads * slots, slots), lambda i: (i, 0)),
+            pl.BlockSpec((slots, width), lambda i: (i, 0)),
+        ],
+        out_specs=pl.BlockSpec((slots, 3 * width), lambda i: (i, 0)),
+        compiler_params=pltpu.CompilerParams(vmem_limit_bytes=56 << 20),
+        cost_estimate=pl.CostEstimate(
+            flops=8 * rows * slots * width,
+            transcendentals=0,
+            bytes_accessed=14 * rows * width + 2 * rows * heads * slots,
+        ),
+        name="attend_back",
+    )(qkv, probs, grad_mixed)
 
 
 def gelu_pair(upper):
@@ -239,12 +373,9 @@
     slots = slot_dev * ways
     per = -(-items // ways)
     rows = per * slots
-    heads = width // HEAD_DIM
-    score_scale = HEAD_DIM ** (-0.5)
 
     live = jnp.pad(lengths, (0, per * ways - items), constant_values=slots)
     live = pick(live, side, per)
-    key_valid = jnp.arange(slots, dtype=jnp.int32)[None, :] < live[:, None]
 
     skip_rows = share_items(skip_store, per, 2)
     latent_rows = share_items(latents, per, 1)
@@ -270,6 +401,9 @@
             contract_bias,
         )
     )
+    inward_weight, skip_rows, latent_rows = lax.optimization_barrier(
+        (inward_weight, skip_rows, latent_rows)
+    )
     inward_matrix = gather_weight(inward_weight)
     outward_matrix = gather_weight(outward_weight)
     expand_matrix = gather_weight(expand_weight)
@@ -280,10 +414,7 @@
     base = simple(joined, skip_matrix) + skip_offset
     first_normed = (normalize(base)[0] * gain_first + shift_first).astype(BF16)
     qkv_vals = simple(first_normed, inward_matrix).astype(BF16)
-    qkv_split = qkv_vals.reshape(per, slots, 3, heads, HEAD_DIM)
-    queries, keys_all, values_all = (qkv_split[:, :, i] for i in range(3))
-    mixed, log_total = attend(queries, keys_all, values_all, key_valid, score_scale)
-    mixed_rows = mixed.reshape(rows, width)
+    mixed_rows, probs = attend(qkv_vals, live)
     middle = base + simple(mixed_rows, outward_matrix) + outward_offset
     second_normed = (normalize(middle)[0] * gain_second + shift_second).astype(BF16)
     upper = simple(second_normed, expand_matrix) + expand_offset
@@ -291,12 +422,12 @@
     result = middle + simple(activated, contract_matrix) + contract_offset
     output = return_items(result.astype(BF16).reshape(per, slots, width), items, 1)
 
-    sum_contract = reduce_weight(across(activated, grad_out))
+    sum_contract = reduce_weight(across(activated, grad_out), True)
     grad_result = grad_out.astype(F32)
     grad_contract_off = jnp.sum(grad_result, 0)
     grad_act = against(grad_out, contract_matrix)
     grad_upper = (grad_act * slope.astype(F32)).astype(BF16)
-    sum_expand = reduce_weight(across(second_normed, grad_upper), sum_contract)
+    sum_expand = reduce_weight(across(second_normed, grad_upper))
     grad_expand_off = jnp.sum(grad_upper.astype(F32), 0)
     grad_second = against(grad_upper, expand_matrix)
     grad_mid_ln, grad_gain_two, grad_shift_two = norm_back(
@@ -304,24 +435,17 @@
     )
     grad_middle = grad_result + grad_mid_ln
     grad_branch = grad_middle.astype(BF16)
-    sum_outward = reduce_weight(across(mixed_rows, grad_branch), sum_expand)
+    sum_outward = reduce_weight(across(mixed_rows, grad_branch))
     grad_outward_off = jnp.sum(grad_branch.astype(F32), 0)
     grad_mixed = against(grad_branch, outward_matrix).astype(BF16)
-    grad_heads = grad_mixed.reshape(per, slots, heads, HEAD_DIM)
-    grad_qkv = jnp.stack(
-        attend_back(
-            queries, keys_all, values_all, key_valid, score_scale, log_total, grad_heads
-        ),
-        2,
-    ).astype(BF16)
-    grad_qkv = grad_qkv.reshape(rows, 3 * width)
-    sum_inward = reduce_weight(across(first_normed, grad_qkv), sum_outward)
+    grad_qkv = attend_back(qkv_vals, probs, grad_mixed, per)
+    sum_inward = reduce_weight(across(first_normed, grad_qkv))
     grad_first = against(grad_qkv, inward_matrix)
     grad_base_ln, grad_gain_one, grad_shift_one = norm_back(
         grad_first, base, gain_first
     )
     grad_base = (grad_middle + grad_base_ln).astype(BF16)
-    sum_skipw = reduce_weight(across(joined, grad_base), sum_inward)
+    sum_skipw = reduce_weight(across(joined, grad_base))
     grad_skip_off = jnp.sum(grad_base.astype(F32), 0)
     grad_joined = against(grad_base, skip_matrix).astype(BF16)
     grad_joined = grad_joined.reshape(per, slots, 2 * width)

time: 1150 us -> 963 us (0.84)
  local copies, waits for them, and re-layouts: 203 us -> 65 us
  waiting for transfers between devices: 577 us -> 498 us
  matrix products: 232 us -> 208 us
  Pallas kernels: 0 us -> 23.7 us
  starting transfers between devices: 24.9 us -> 47.2 us
    psum x5 -> x1, waiting for transfers between devices: 387 us -> 0.01 us  [reduce_weight(): part = lax.psum(part, ('z', 'x'))]
    ppermute x21 -> x35, waiting for transfers between devices: 103 us -> 353 us  [flip(): return lax.ppermute(array, axis, [(0, 1), (1, 0)])]
    ppermute x6 -> x8, waiting for transfers between devices: 39.5 us -> 145 us  [swap(): return lax.ppermute(array, axis, [(i, i ^ step) for i in range(ways)])]
    all_gather x1, waiting for transfers between devices: 47.6 us -> 0.01 us  [reduce_vectors(): parts = lax.all_gather(joined.reshape(-1, 1024), WIDE + ('seq',), axis=0)]
    dynamic_update_slice x8 -> x0, local copies, waits for them, and re-layouts: 42.5 us -> none  [the longest x4 36.2 us: share_items(): whole = lax.dynamic_update_slice_in_dim(whole, piece, source * size, axis)]
    reshape x3 -> x0, local copies, waits for them, and re-layouts: 34.4 us -> none  [the longest x1 21.1 us: per_device(): qkv_split = qkv_vals.reshape(per, slots, 3, heads, HEAD_DIM)]
    pallas_call x0 -> x2, Pallas kernels: none -> 23.7 us  [the longest x1 12.9 us: attend_back(): pl.pallas_call(attend_back_kernel, out_shape=jax.ShapeDtypeStruct((rows,...]
    unnamed x150 -> x102, local copies, waits for them, and re-layouts: 44.9 us -> 25.5 us
  transfers between devices with their start and end apart: 38 -> 50, of which waited for: 12 -> 20; matrix products, arithmetic and copies ran while one was open for 43% -> 27% of each run, Pallas kernels for 0% -> 1%
where the time goes in v2:
time: 963 us; the launch traced here: 956 us
  waiting for transfers between devices  498 us (52%)
  matrix products  208 us (22%)
  other arithmetic  99.4 us (10%)
  local copies, waits for them, and re-layouts  65 us (7%)
  starting transfers between devices  47.2 us (5%)
  Pallas kernels  23.7 us (2%)
  between operations  15.3 us (2%)
    ppermute x35, waiting for transfers between devices, flip(): return lax.ppermute(array, axis, [(0, 1), (1, 0)])  353 us
    ppermute x8, waiting for transfers between devices, swap(): return lax.ppermute(array, axis, [(i, i ^ step) for i in range(ways)])  145 us
    dot_general x5, matrix products, simple(): return jnp.dot(left_side, right_side, preferred_element_type=F32)  78.1 us
    dot_general x5, matrix products, against(): lax.dot_general(left_side, right_side, (((1,), (1,)), ((), ())), preferre...  74.2 us
    dot_general x5, matrix products, across(): lax.dot_general(left_side, right_side, (((0,), (0,)), ((), ())), preferre...  55.6 us
    convert_element_type x22, other arithmetic, add(): return (left.astype(F32) + right.astype(F32)).astype(BF16)  32.6 us
    ppermute x35, starting transfers between devices, flip(): return lax.ppermute(array, axis, [(0, 1), (1, 0)])  32 us
    unnamed x102, local copies, waits for them, and re-layouts  25.5 us
  transfers between devices with their start and end apart: 50, of which 20 were waited for; matrix products, arithmetic and copies ran while one was open for 27% of the time, Pallas kernels for 1%

profile of v2, /device:TPU:0, one launch (start us, length us, event | category | flops | bytes accessed | tf_op | source)
XLA Modules:
  0.0 956.5 jit_solution(17912345930899455225)
XLA Ops:
  11.4 14.9 %collective-permute-done.2 = bf16[288,1152]{1,0:T(8,128)(2,1)S(1)} collective-permute-done((bf16[288,1152]{1,0:T(8,128)(2,1)S(1)}, bf16[288,1152]{1,0:T(8,128)(2,1)S(1)}, u32[]{:S(2)}, u32[]{:S(2)}) %collective-permute-start.2) | collective-permute-done | bytes 663584 | tf_op jit(solution)/shard_map/ppermute | solution.py:39
  39.3 20.7 %collective-permute-done = bf16[7,128,576]{1,2,0:T(8,128)(2,1)} collective-permute-done((bf16[7,128,576]{1,2,0:T(8,128)(2,1)S(1)}, bf16[7,128,576]{1,2,0:T(8,128)(2,1)}, u32[]{:S(2)}, u32[]{:S(2)}) %collective-permute-start) | collective-permute-done | bytes 1032224 | tf_op jit(solution)/shard_map/ppermute | solution.py:39
  64.8 15.5 %collective-permute-done.1 = bf16[7,64,1152]{2,1,0:T(8,128)(2,1)} collective-permute-done((bf16[7,64,1152]{2,1,0:T(8,128)(2,1)}, bf16[7,64,1152]{2,1,0:T(8,128)(2,1)}, u32[]{:S(2)}, u32[]{:S(2)}) %collective-permute-start.1) | collective-permute-done | bytes 1032224 | tf_op jit(solution)/shard_map/ppermute | solution.py:39
  86.7 20.9 %collective-permute-done.4 = bf16[144,3456]{1,0:T(8,128)(2,1)S(1)} collective-permute-done((bf16[144,3456]{1,0:T(8,128)(2,1)S(1)}, bf16[144,3456]{1,0:T(8,128)(2,1)S(1)}, u32[]{:S(2)}, u32[]{:S(2)}) %collective-permute-start.4) | collective-permute-done | bytes 995360 | tf_op jit(solution)/shard_map/ppermute | solution.py:39
  120.3 26.4 %collective-permute-done.6 = bf16[144,4608]{1,0:T(8,128)(2,1)S(1)} collective-permute-done((bf16[144,4608]{1,0:T(8,128)(2,1)S(1)}, bf16[144,4608]{1,0:T(8,128)(2,1)S(1)}, u32[]{:S(2)}, u32[]{:S(2)}) %collective-permute-start.6) | collective-permute-done | bytes 1327136 | tf_op jit(solution)/shard_map/ppermute | solution.py:39
  156.5 42.9 %collective-permute-done.9 = bf16[7,64,1152]{2,1,0:T(8,128)(2,1)S(1)} collective-permute-done((bf16[7,64,1152]{2,1,0:T(8,128)(2,1)}, bf16[7,64,1152]{2,1,0:T(8,128)(2,1)S(1)}, u32[]{:S(2)}, u32[]{:S(2)}) %collective-permute-start.9) | collective-permute-done | bytes 1032224 | tf_op jit(solution)/shard_map/ppermute | solution.py:39
  221.6 15.6 %convolution_convert_fusion.5.qkv = bf16[896,3456]{1,0:T(8,128)(2,1)} fusion(bf16[576,3456]{1,0:T(8,128)(2,1)} %all-gather.9.cloned.1.call-done, bf16[576,3456]{1,0:T(8,128)(2,1)} %param.25, pred[]{:T(512)S(6)} %eq.6, f32[896,1152]{1,0:T(8,128)} %copy-done.3, f32[1152]{0:T(1024)S(1)} %reshape.227, f32[1152]{0:T(1024)S(1)} %reshape.226, ...), kind=kOutput, calls=%fused_computation.24 | convolution fusion | flops 7178600448 | bytes 18300928 | tf_op jit(solution)/shard_map/dot_general | solution.py:31
  257.6 24.6 %fusion.4 = (bf16[896,4608]{1,0:T(8,128)(2,1)}, bf16[896,4608]{1,0:T(8,128)(2,1)}) fusion(f32[4608]{0:T(1024)S(1)} %reshape.231, bf16[576,4608]{1,0:T(8,128)(2,1)} %all-gather.13.cloned.1.call-done, bf16[576,4608]{1,0:T(8,128)(2,1)} %param.30, pred[]{:T(512)S(6)} %eq.6, f32[896,1152]{1,0:T(8,128)} %copy-done.2, f32[1152]{0:T(1024)S(1)} %reshape.230, ...), kind=kOutput, calls=%fused_computation.7 | convolution fusion | flops 9615163392 | bytes 31295488 | tf_op jit(solution)/shard_map/dot_general | solution.py:31
  282.2 19.1 %convert_reduce_fusion = (f32[4608]{0:T(1024)S(1)}, bf16[896,4608]{1,0:T(8,128)(2,1)}) fusion(bf16[896,4608]{1,0:T(8,128)(2,1)} %get-tuple-element.28, bf16[896,1152]{1,0:T(8,128)(2,1)S(1)} %bitcast.109, bf16[2304,1152]{1,0:T(8,128)(2,1)} %all-gather.15.cloned.1.call-done, bf16[2304,1152]{1,0:T(8,128)(2,1)} %param.32, pred[]{:T(512)S(6)} %eq.6), kind=kOutput, calls=%fused_computation.8 | convolution fusion | flops 9581096960 | bytes 29214720 | tf_op jit(solution)/shard_map/dot_general | solution.py:25
  301.3 21.6 %multiply_reduce_fusion = (f32[1152]{0:T(1024)S(1)}, f32[896]{0:T(1024)S(1)}, f32[896]{0:T(1024)S(1)}, f32[1152]{0:T(1024)S(1)}, f32[896,1152]{1,0:T(8,128)}) fusion(f32[896,1152]{1,0:T(8,128)} %copy-done.2, f32[896]{0:T(1024)S(1)} %add_rsqrt_fusion, f32[896]{0:T(1024)S(1)} %broadcast_multiply_fusion.4, f32[1152]{0:T(1024)S(1)} %reshape.229, ...), kind=kOutput, calls=%fused_computation.46 | convolution fusion | flops 9569742848 | bytes 27160064 | tf_op jit(solution)/shard_map/dot_general | solution.py:25
  331.8 12.9 %attend_back.1 = bf16[896,3456]{1,0:T(8,128)(2,1)} custom-call(bf16[896,3456]{1,0:T(8,128)(2,1)} %convolution_convert_fusion.5.qkv, bf16[14336,128]{1,0:T(8,128)(2,1)} %get-tuple-element.29.probs_in, bf16[896,1152]{1,0:T(8,128)(2,1)} %convolution_convert_fusion.7.grad_mixed), custom_call_target="tpu_custom_call" | custom-call | flops 1056964608 | bytes 18120704 | tf_op jit(solution)/shard_map/attend_back/pallas_call | solution.py:326
  344.6 19.4 %multiply_reduce_fusion.1 = (f32[1152]{0:T(1024)S(1)}, f32[896]{0:T(1024)S(1)}, f32[896]{0:T(1024)S(1)}, f32[1152]{0:T(1024)S(1)}, f32[896,1152]{1,0:T(8,128)}) fusion(f32[896,1152]{1,0:T(8,128)} %copy-done.3, f32[896]{0:T(1024)S(1)} %add_rsqrt_fusion.1, f32[896]{0:T(1024)S(1)} %broadcast_multiply_fusion.5, f32[1152]{0:T(1024)S(1)} %reshape.226, ...), kind=kOutput, calls=%fused_computation.48 | convolution fusion | flops 7179628544 | bytes 22441472 | tf_op jit(solution)/shard_map/dot_general | solution.py:25
  364.0 14.8 %convolution_convert_fusion = bf16[4608,1152]{1,0:T(8,128)(2,1)S(1)} fusion(bf16[896,4608]{1,0:T(8,128)(2,1)} %get-tuple-element.27, bf16[896,1152]{1,0:T(8,128)(2,1)S(1)} %bitcast.110), kind=kOutput, calls=%fused_computation.1 | convolution fusion | flops 9517989888 | bytes 20938752 | tf_op jit(solution)/shard_map/dot_general | solution.py:19
  453.6 37.2 %collective-permute-done.41 = bf16[1152,1152]{1,0:T(8,128)(2,1)S(1)} collective-permute-done((bf16[1152,1152]{1,0:T(8,128)(2,1)S(1)}, bf16[1152,1152]{1,0:T(8,128)(2,1)S(1)}, u32[]{:S(2)}, u32[]{:S(2)}) %collective-permute-start.41) | collective-permute-done | bytes 2654240 | tf_op jit(solution)/shard_map/ppermute | solution.py:39
  493.1 15.7 %convolution_convert_fusion.1 = bf16[1152,4608]{1,0:T(8,128)(2,1)S(1)} fusion(bf16[896,4608]{1,0:T(8,128)(2,1)} %get-tuple-element.81, f32[896,1152]{1,0:T(8,128)} %copy-done.2, f32[1152]{0:T(1024)S(1)} %copy-done.28, f32[1152]{0:T(1024)S(1)} %reshape.229, f32[896]{0:T(1024)S(1)} %add_rsqrt_fusion, f32[896]{0:T(1024)S(1)} %broadcast_multiply_fusion.4), kind=kOutput, calls=%fused_computation.2 | convolution fusion | flops 9523150848 | bytes 23019520 | tf_op jit(solution)/shard_map/dot_general | solution.py:19
  530.6 20.2 %fusion.17 = bf16[896,1152]{1,0:T(8,128)(2,1)S(1)} fusion(f32[896,1152]{1,0:T(8,128)} %copy-done.2, bf16[896,4608]{1,0:T(8,128)(2,1)} %get-tuple-element.27, f32[1152]{0:T(1024)S(1)} %copy-done.26, bf16[2304,1152]{1,0:T(8,128)(2,1)} %all-gather.15.cloned.1.call-done, bf16[2304,1152]{1,0:T(8,128)(2,1)} %param.32, pred[]{:T(512)S(6)} %eq.6), kind=kOutput, calls=%fused_computation.67 | convolution fusion | flops 9563553792 | bytes 25072128 | tf_op jit(solution)/shard_map/dot_general | solution.py:31
  603.0 25.6 %collective-permute-done.13 = bf16[576,1152]{1,0:T(8,128)(2,1)} collective-permute-done((bf16[576,1152]{1,0:T(8,128)(2,1)S(1)}, bf16[576,1152]{1,0:T(8,128)(2,1)}, u32[]{:S(2)}, u32[]{:S(2)}) %collective-permute-start.13) | collective-permute-done | bytes 1327136 | tf_op jit(solution)/shard_map/ppermute | solution.py:39
  631.1 45.3 %collective-permute-done.20 = bf16[288,3456]{1,0:T(8,128)(2,1)} collective-permute-done((bf16[288,3456]{1,0:T(8,128)(2,1)}, bf16[288,3456]{1,0:T(8,128)(2,1)}, u32[]{:S(2)}, u32[]{:S(2)}) %collective-permute-start.20) | collective-permute-done | bytes 1990688 | tf_op jit(solution)/shard_map/ppermute | solution.py:39
  679.3 50.9 %collective-permute-done.34 = bf16[288,4608]{1,0:T(8,128)(2,1)S(1)} collective-permute-done((bf16[288,4608]{1,0:T(8,128)(2,1)S(1)}, bf16[288,4608]{1,0:T(8,128)(2,1)S(1)}, u32[]{:S(2)}, u32[]{:S(2)}) %collective-permute-start.34) | collective-permute-done | bytes 2654240 | tf_op jit(solution)/shard_map/ppermute | solution.py:39
  734.2 25.1 %collective-permute-done.35 = bf16[144,4608]{1,0:T(8,128)(2,1)S(1)} collective-permute-done((bf16[144,4608]{1,0:T(8,128)(2,1)S(1)}, bf16[144,4608]{1,0:T(8,128)(2,1)S(1)}, u32[]{:S(2)}, u32[]{:S(2)}) %collective-permute-start.35) | collective-permute-done | bytes 1327136 | tf_op jit(solution)/shard_map/ppermute | solution.py:39
  764.1 31.8 %collective-permute-done.22 = bf16[144,3456]{1,0:T(8,128)(2,1)S(1)} collective-permute-done((bf16[144,3456]{1,0:T(8,128)(2,1)S(1)}, bf16[144,3456]{1,0:T(8,128)(2,1)S(1)}, u32[]{:S(2)}, u32[]{:S(2)}) %collective-permute-start.22) | collective-permute-done | bytes 995360 | tf_op jit(solution)/shard_map/ppermute | solution.py:65
  798.0 22.5 %collective-permute-done.36 = bf16[144,4608]{1,0:T(8,128)(2,1)S(1)} collective-permute-done((bf16[144,4608]{1,0:T(8,128)(2,1)S(1)}, bf16[144,4608]{1,0:T(8,128)(2,1)S(1)}, u32[]{:S(2)}, u32[]{:S(2)}) %collective-permute-start.36) | collective-permute-done | bytes 1327136 | tf_op jit(solution)/shard_map/ppermute | solution.py:65
  824.2 57.4 %collective-permute-done.23 = bf16[144,3456]{1,0:T(8,128)(2,1)S(1)} collective-permute-done((bf16[144,3456]{1,0:T(8,128)(2,1)S(1)}, bf16[144,3456]{1,0:T(8,128)(2,1)S(1)}, u32[]{:S(2)}, u32[]{:S(2)}) %collective-permute-start.23) | collective-permute-done | bytes 995360 | tf_op jit(solution)/shard_map/ppermute | solution.py:65
  883.7 16.2 %collective-permute-done.37 = bf16[144,4608]{1,0:T(8,128)(2,1)S(1)} collective-permute-done((bf16[144,4608]{1,0:T(8,128)(2,1)S(1)}, bf16[144,4608]{1,0:T(8,128)(2,1)S(1)}, u32[]{:S(2)}, u32[]{:S(2)}) %collective-permute-start.37) | collective-permute-done | bytes 1327136 | tf_op jit(solution)/shard_map/ppermute | solution.py:65
  (301 shorter events, 324.1 us)
Async XLA Ops:
  7.2 201.1 %all-gather.7.cloned.1.call-start = ((), (), s32[]{:S(2)}) async-start(), calls=%async_computation | async-start | bytes 3317760 | tf_op jit(solution)/shard_map/all_gather | solution.py:59
  27.2 194.4 %all-gather.9.cloned.1.call-start = ((), (), s32[]{:S(2)}) async-start(), calls=%async_computation.1 | async-start | bytes 4976640 | tf_op jit(solution)/shard_map/all_gather | solution.py:59
  108.5 139.5 %all-gather.11.cloned.1.call-start = ((), (), s32[]{:S(2)}) async-start(), calls=%async_computation.2 | async-start | bytes 1658880 | tf_op jit(solution)/shard_map/all_gather | solution.py:59
  117.5 140.1 %all-gather.13.cloned.1.call-start = ((), (), s32[]{:S(2)}) async-start(), calls=%async_computation.3 | async-start | bytes 6635520 | tf_op jit(solution)/shard_map/all_gather | solution.py:59
  147.7 134.4 %all-gather.15.cloned.1.call-start = ((), (), s32[]{:S(2)}) async-start(), calls=%async_computation.4 | async-start | bytes 6635520 | tf_op jit(solution)/shard_map/all_gather | solution.py:59
  207.9 696.7 %all-reduce.6.cloned.1.call-start = ((), (), s32[]{:S(2)}) async-start(), calls=%async_computation.6 | async-start | bytes 5308416 | tf_op jit(solution)/shard_map/psum | solution.py:97
  416.3 92.6 %collective-permute-start.26 = (bf16[2,288,1152]{2,1,0:T(8,128)(2,1)}, bf16[2,288,1152]{2,1,0:T(8,128)(2,1)}, u32[]{:S(2)}, u32[]{:S(2)}) collective-permute-start(bf16[2,288,1152]{2,1,0:T(8,128)(2,1)} %dynamic-slice_bitcast_fusion.8), channel_id=1, source_target_pairs={{0,2},{2,0},{1,3},{3,1},{4,6},{6,4},{5,7},{7,5},{8,10},{10,8},{9,1... | collective-permute-start | bytes 3981320 | tf_op jit(solution)/shard_map/ppermute | solution.py:39
  430.4 60.4 %collective-permute-start.41 = (bf16[1152,1152]{1,0:T(8,128)(2,1)S(1)}, bf16[1152,1152]{1,0:T(8,128)(2,1)S(1)}, u32[]{:S(2)}, u32[]{:S(2)}) collective-permute-start(bf16[1152,1152]{1,0:T(8,128)(2,1)S(1)} %dynamic-slice_bitcast_fusion.3), channel_id=1, source_target_pairs={{0,1},{1,0},{2,3},{3,2},{4,5},{5,4},{6,7},{7,6},{8,9},{9,8},{10,11... | collective-permute-start | bytes 7962632 | tf_op jit(solution)/shard_map/ppermute | solution.py:39
  432.9 119.8 %collective-permute-start.10 = (bf16[7,64,1152]{2,1,0:T(8,128)(2,1)}, bf16[7,64,1152]{2,1,0:T(8,128)(2,1)}, u32[]{:S(2)}, u32[]{:S(2)}) collective-permute-start(bf16[7,64,1152]{2,1,0:T(8,128)(2,1)} %get-tuple-element.53), channel_id=1, source_target_pairs={{0,1},{1,0},{2,3},{3,2},{4,5},{5,4},{6,7},{7,6},{8,9},{9,8},{10,11... | collective-permute-start | bytes 3096584 | tf_op jit(solution)/shard_map/ppermute | solution.py:39
  435.4 130.4 %collective-permute-start.12 = (bf16[2,576,1152]{2,1,0:T(8,128)(2,1)}, bf16[2,576,1152]{2,1,0:T(8,128)(2,1)}, u32[]{:S(2)}, u32[]{:S(2)}) collective-permute-start(bf16[2,576,1152]{2,1,0:T(8,128)(2,1)} %dynamic-slice_bitcast_fusion.5), channel_id=1, source_target_pairs={{0,2},{2,0},{1,3},{3,1},{4,6},{6,4},{5,7},{7,5},{8,10},{10,8},{9,1... | collective-permute-start | bytes 7962632 | tf_op jit(solution)/shard_map/ppermute | solution.py:39
  453.1 130.6 %collective-permute-start.19 = (bf16[2,288,3456]{2,1,0:T(8,128)(2,1)}, bf16[2,288,3456]{2,1,0:T(8,128)(2,1)}, u32[]{:S(2)}, u32[]{:S(2)}) collective-permute-start(bf16[2,288,3456]{2,1,0:T(8,128)(2,1)} %dynamic-slice_bitcast_fusion.2), channel_id=1, source_target_pairs={{0,2},{2,0},{1,3},{3,1},{4,6},{6,4},{5,7},{7,5},{8,10},{10,8},{9,1... | collective-permute-start | bytes 11943944 | tf_op jit(solution)/shard_map/ppermute | solution.py:39
  493.0 419.2 %all-gather.17.cloned.1.call-start = ((), (), s32[]{:S(2)}) async-start(), calls=%async_computation.5 | async-start | bytes 2162688 | tf_op jit(solution)/shard_map/all_gather | solution.py:128
  515.7 74.4 %collective-permute-start.33 = (bf16[2,288,4608]{2,1,0:T(8,128)(2,1)}, bf16[2,288,4608]{2,1,0:T(8,128)(2,1)}, u32[]{:S(2)}, u32[]{:S(2)}) collective-permute-start(bf16[2,288,4608]{2,1,0:T(8,128)(2,1)} %dynamic-slice_bitcast_fusion.1), channel_id=1, source_target_pairs={{0,2},{2,0},{1,3},{3,1},{4,6},{6,4},{5,7},{7,5},{8,10},{10,8},{9,1... | collective-permute-start | bytes 15925256 | tf_op jit(solution)/shard_map/ppermute | solution.py:39
  564.3 340.3 %collective-permute-start.11 = (bf16[7,128,576]{1,2,0:T(8,128)(2,1)}, bf16[7,128,576]{1,2,0:T(8,128)(2,1)}, u32[]{:S(2)}, u32[]{:S(2)}) collective-permute-start(bf16[7,128,576]{1,2,0:T(8,128)(2,1)} %copy.49), channel_id=1, source_target_pairs={{0,1},{1,0},{2,3},{3,2},{4,5},{5,4},{6,7},{7,6},{8,9},{9,8},{10,11... | collective-permute-start | bytes 3096584 | tf_op jit(solution)/shard_map/ppermute | solution.py:39
  590.1 86.3 %collective-permute-start.20 = (bf16[288,3456]{1,0:T(8,128)(2,1)}, bf16[288,3456]{1,0:T(8,128)(2,1)}, u32[]{:S(2)}, u32[]{:S(2)}) collective-permute-start(bf16[288,3456]{1,0:T(8,128)(2,1)} %dynamic-slice_bitcast_fusion.6), channel_id=1, source_target_pairs={{0,1},{1,0},{2,3},{3,2},{4,5},{5,4},{6,7},{7,6},{8,9},{9,8},{10,11... | collective-permute-start | bytes 5971976 | tf_op jit(solution)/shard_map/ppermute | solution.py:39
  596.4 133.8 %collective-permute-start.34 = (bf16[288,4608]{1,0:T(8,128)(2,1)S(1)}, bf16[288,4608]{1,0:T(8,128)(2,1)S(1)}, u32[]{:S(2)}, u32[]{:S(2)}) collective-permute-start(bf16[288,4608]{1,0:T(8,128)(2,1)S(1)} %dynamic-slice_bitcast_fusion.4), channel_id=1, source_target_pairs={{0,1},{1,0},{2,3},{3,2},{4,5},{5,4},{6,7},{7,6},{8,9},{9,8},{10,11... | collective-permute-start | bytes 7962632 | tf_op jit(solution)/shard_map/ppermute | solution.py:39
  603.0 305.6 %collective-permute-start.32 = (bf16[288,1152]{1,0:T(8,128)(2,1)}, bf16[288,1152]{1,0:T(8,128)(2,1)}, u32[]{:S(2)}, u32[]{:S(2)}) collective-permute-start(bf16[288,1152]{1,0:T(8,128)(2,1)} %maximum_select_fusion.24), channel_id=1, source_target_pairs={{0,2},{2,0},{1,3},{3,1},{4,6},{6,4},{5,7},{7,5},{8,10},{10,8},{9,1... | collective-permute-start | bytes 1990664 | tf_op jit(solution)/shard_map/ppermute | solution.py:39
  630.3 101.3 %collective-permute-start.14 = (bf16[288,1152]{1,0:T(8,128)(2,1)S(1)}, bf16[288,1152]{1,0:T(8,128)(2,1)S(1)}, u32[]{:S(2)}, u32[]{:S(2)}) collective-permute-start(bf16[288,1152]{1,0:T(8,128)(2,1)S(1)} %dynamic-slice_bitcast_fusion.12), channel_id=1, source_target_pairs={{0,4},{4,0},{1,5},{5,1},{2,6},{6,2},{3,7},{7,3},{8,12},{12,8},{9,1... | collective-permute-start | bytes 1990664 | tf_op jit(solution)/shard_map/ppermute | solution.py:39
  733.7 62.2 %collective-permute-start.22 = (bf16[144,3456]{1,0:T(8,128)(2,1)S(1)}, bf16[144,3456]{1,0:T(8,128)(2,1)S(1)}, u32[]{:S(2)}, u32[]{:S(2)}) collective-permute-start(bf16[144,3456]{1,0:T(8,128)(2,1)S(1)} %fusion.22), channel_id=1, source_target_pairs={{0,8},{8,0},{16,24},{24,16},{1,9},{9,1},{17,25},{25,17},{2,10},{10... | collective-permute-start | bytes 2985992 | tf_op jit(solution)/shard_map/ppermute | solution.py:65
  759.7 60.9 %collective-permute-start.36 = (bf16[144,4608]{1,0:T(8,128)(2,1)S(1)}, bf16[144,4608]{1,0:T(8,128)(2,1)S(1)}, u32[]{:S(2)}, u32[]{:S(2)}) collective-permute-start(bf16[144,4608]{1,0:T(8,128)(2,1)S(1)} %fusion.19), channel_id=1, source_target_pairs={{0,8},{8,0},{16,24},{24,16},{1,9},{9,1},{17,25},{25,17},{2,10},{10... | collective-permute-start | bytes 3981320 | tf_op jit(solution)/shard_map/ppermute | solution.py:65
  761.4 60.8 %collective-permute-start.16 = (bf16[288,1152]{1,0:T(8,128)(2,1)S(1)}, bf16[288,1152]{1,0:T(8,128)(2,1)S(1)}, u32[]{:S(2)}, u32[]{:S(2)}) collective-permute-start(bf16[288,1152]{1,0:T(8,128)(2,1)S(1)} %add_convert_fusion.8), channel_id=1, source_target_pairs={{0,16},{8,24},{16,0},{24,8},{1,17},{9,25},{17,1},{25,9},{2,18},{10... | collective-permute-start | bytes 1990664 | tf_op jit(solution)/shard_map/ppermute | solution.py:65
  796.3 85.3 %collective-permute-start.23 = (bf16[144,3456]{1,0:T(8,128)(2,1)S(1)}, bf16[144,3456]{1,0:T(8,128)(2,1)S(1)}, u32[]{:S(2)}, u32[]{:S(2)}) collective-permute-start(bf16[144,3456]{1,0:T(8,128)(2,1)S(1)} %add_convert_fusion.6), channel_id=1, source_target_pairs={{0,16},{8,24},{16,0},{24,8},{1,17},{9,25},{17,1},{25,9},{2,18},{10... | collective-permute-start | bytes 2985992 | tf_op jit(solution)/shard_map/ppermute | solution.py:65
  820.9 79.0 %collective-permute-start.37 = (bf16[144,4608]{1,0:T(8,128)(2,1)S(1)}, bf16[144,4608]{1,0:T(8,128)(2,1)S(1)}, u32[]{:S(2)}, u32[]{:S(2)}) collective-permute-start(bf16[144,4608]{1,0:T(8,128)(2,1)S(1)} %add_convert_fusion.4), channel_id=1, source_target_pairs={{0,16},{8,24},{16,0},{24,8},{1,17},{9,25},{17,1},{25,9},{2,18},{10... | collective-permute-start | bytes 3981320 | tf_op jit(solution)/shard_map/ppermute | solution.py:65
  822.4 80.6 %collective-permute-start.17 = (bf16[288,1152]{1,0:T(8,128)(2,1)S(1)}, bf16[288,1152]{1,0:T(8,128)(2,1)S(1)}, u32[]{:S(2)}, u32[]{:S(2)}) collective-permute-start(bf16[288,1152]{1,0:T(8,128)(2,1)S(1)} %add_convert_fusion.7), channel_id=1, source_target_pairs={{0,4},{4,0},{1,5},{5,1},{2,6},{6,2},{3,7},{7,3},{8,12},{12,8},{9,1... | collective-permute-start | bytes 1990664 | tf_op jit(solution)/shard_map/ppermute | solution.py:39
  (71 other events, 1832.6 us)
Sparse Core Ops, SparseCore 0:
  27.3 27.2 all-gather.6
  108.6 34.0 all-gather.8
  144.9 18.2 all-gather.10
  165.2 40.7 all-gather.12
  208.0 41.0 all-gather.14
  493.1 123.4 all-reduce.5
  619.7 58.6 all-gather.16

commit v3 on v2

v3 whole, which is shorter than its diff:
```python
import functools

import jax
import jax.numpy as jnp
from jax import lax
from jax.experimental import pallas as pl
from jax.experimental.pallas import tpu as pltpu
from jax.sharding import Mesh
from jax.sharding import PartitionSpec as P

HEAD_DIM = 72
WIDTH = 16 * HEAD_DIM

EPS = 1e-05
NEG = -1e30
PLANE = ("z", "x", "c")
WIDE = ("w",) + PLANE
BF16 = jnp.bfloat16
F32 = jnp.float32
LANES = 128

def across(left_side, right_side):
    return lax.dot_general(
        left_side, right_side, (((0,), (0,)), ((), ())), preferred_element_type=F32
    )


def against(left_side, right_side):
    return lax.dot_general(
        left_side, right_side, (((1,), (1,)), ((), ())), preferred_element_type=F32
    )


def simple(left_side, right_side):
    return jnp.dot(left_side, right_side, preferred_element_type=F32)


def pick(array, index, size, axis=0):
    return lax.dynamic_slice_in_dim(array, index * size, size, axis)


def flip(array, axis):
    return lax.ppermute(array, axis, [(0, 1), (1, 0)])


def ordered(mine, other, index, axis=0):
    return jnp.where(
        index == 0,
        jnp.concatenate([mine, other], axis),
        jnp.concatenate([other, mine], axis),
    )


class Chain:
    def __init__(self):
        self.last = ()

    def enter(self, *values):
        values = lax.optimization_barrier(values + self.last)[: len(values)]
        return values

    def leave(self, *values):
        self.last = values[:1]
        return values if len(values) > 1 else values[0]

    def run(self, function, *values):
        out = function(*self.enter(*values))
        self.last = tuple(out)[:1] if isinstance(out, (tuple, list)) else (out,)
        return out


def fast_mesh():
    return lax.axis_size("seq") == 2 and lax.axis_size("w") == 2


def added(parts):
    if len(parts) == 1:
        return parts[0]
    return (parts[0].astype(F32) + parts[1].astype(F32)).astype(BF16)


def block(array, index, axis):
    return lax.dynamic_index_in_dim(array, index, axis, keepdims=False)


def eighth(shard):
    place = lax.axis_index("z") * 4 + lax.axis_index("x") * 2 + lax.axis_index("c")
    return pick(shard, place, shard.shape[0] // 8)


def share(piece):
    return lax.all_gather(piece, PLANE, axis=0, tiled=True)


class Reduction:
    def __init__(self, chain, name, lefts, rights):
        self.chain = chain
        if fast_mesh():
            core = lax.axis_index("c").reshape(1)
            count = len(lefts)
            sent, keep = chain.run(
                lambda *a: core_gradients(name, core, a[:count], a[count:]),
                *lefts,
                *rights,
            )
            shape = (2, 2, 2) + sent.shape[1:]
            self.parts = (keep.reshape(shape), flip(sent.reshape(shape), "c"))
            self.names = ["seq", "z", "x", "w", None]
        else:
            axis = int(len(rights) > 1)
            pairs = zip(lefts, rights) if axis else ((a, rights[0]) for a in lefts)
            grad = jnp.concatenate([across(*p).astype(BF16) for p in pairs], axis)
            part = lax.psum_scatter(grad, "seq", scatter_dimension=0, tiled=True)
            self.total, self.names = lax.psum(part, WIDE), []

    def step(self):
        if not self.names:
            return
        name = self.names.pop(0)
        parts = self.chain.enter(*self.parts)
        if name is None:
            self.total = share(self.chain.leave(added(parts)))
        elif name == "w":
            sent = self.chain.leave(added(parts))
            self.parts = (sent, flip(sent, name))
        else:
            index = lax.axis_index(name)
            sent = added([block(part, 1 - index, 0) for part in parts])
            keep = added([block(part, index, 0) for part in parts])
            sent, keep = self.chain.leave(sent, keep)
            self.parts = (keep, flip(sent, name))

    def finish(self):
        assert not self.names
        return self.chain.run(lambda a: a.astype(F32), self.total)


def gather_vectors(vectors):
    joined = jnp.concatenate(vectors)
    count = joined.shape[0]
    if fast_mesh():
        mine = joined.reshape(1, count)
        everything = ordered(mine, flip(mine, "seq"), lax.axis_index("seq"))
    else:
        everything = lax.all_gather(joined.reshape(1, count), "seq", axis=0, tiled=True)
    out, start = [], 0
    for vector in vectors:
        size = vector.shape[0]
        out.append(everything[:, start : start + size].reshape(-1).astype(F32))
        start += size
    return out


class VectorReduction:
    def __init__(self, chain, vectors):
        self.chain, self.sizes = chain, [vector.shape[1] for vector in vectors]
        self.total = chain.run(lambda *a: jnp.concatenate(a, 1), *vectors)
        self.names = ["seq", "c", "z", "x", "w"]
        if fast_mesh():
            self.got = flip(self.total, self.names.pop(0))
        else:
            self.total, self.names = lax.psum(self.total, WIDE + ("seq",)), []

    def step(self):
        if fast_mesh():
            self.total = self.chain.run(jnp.add, self.total, self.got)
            if self.names:
                self.got = flip(self.total, self.names.pop(0))

    def finish(self):
        assert not self.names
        ways, side = lax.axis_size("seq"), lax.axis_index("seq")
        out, start = [], 0
        for whole in self.sizes:
            size = whole // ways
            shards = self.total[:, start : start + whole].reshape(ways, size)
            out.append(block(shards, side, 0))
            start += whole
        return out


def start_items(array, per):
    ways, side = lax.axis_size("seq"), lax.axis_index("seq")
    padding = [(0, per * ways - array.shape[0])] + [(0, 0)] * (array.ndim - 1)
    array = jnp.pad(array, padding)
    pieces = [pick(array, side, per)]
    for hop in range(1, ways):
        piece = pick(array, (side + hop) % ways, per)
        pieces.append(
            lax.ppermute(piece, "seq", [(i, (i + hop) % ways) for i in range(ways)])
        )
    return tuple(pieces)


def joined_pieces(pieces, axis):
    ways, side = lax.axis_size("seq"), lax.axis_index("seq")
    if ways == 2:
        return ordered(pieces[0], pieces[1], side, axis)
    size = pieces[0].shape[axis]
    shape = list(pieces[0].shape)
    shape[axis] = size * ways
    whole = jnp.zeros(shape, pieces[0].dtype)
    for hop, piece in enumerate(pieces):
        source = (side - hop) % ways
        whole = lax.dynamic_update_slice_in_dim(whole, piece, source * size, axis)
    return whole


def return_items(whole, axis):
    ways, side = lax.axis_size("seq"), lax.axis_index("seq")
    size = whole.shape[axis] // ways
    pieces = [pick(whole, side, size, axis)]
    for hop in range(1, ways):
        piece = pick(whole, (side + hop) % ways, size, axis)
        pieces.append(
            lax.ppermute(piece, "seq", [(i, (i + hop) % ways) for i in range(ways)])
        )
    return tuple(pieces)


HINT = pl.CostEstimate(flops=10**13, transcendentals=0, bytes_accessed=10**9)


def block_loader(parts, offset, blocks, side, sems):
    count, size, _ = blocks.shape
    rows, columns = parts[0].shape
    first = pl.program_id(0) == 0
    copies = []
    for b in range(count):
        copies.append([])
        if len(parts) == 1:
            row, column = divmod(b, columns // size)
            source = parts[0].at[pl.ds(row * size, size), pl.ds(column * size, size)]
            copy = pltpu.make_async_copy(source, blocks.at[b], sems.at[0, b])
            copies[b].append((first, copy))
        elif rows >= size:
            half, place = divmod(b, rows // size)
            for p, part in enumerate(parts):
                mine = side == half if p == 0 else side != half
                source = part.at[pl.ds(place * size, size), :]
                copy = pltpu.make_async_copy(source, blocks.at[b], sems.at[0, b])
                copies[b].append((jnp.logical_and(first, mine), copy))
        else:
            for p, part in enumerate(parts):
                start = pl.multiple_of((side if p == 0 else 1 - side) * rows, 16)
                column = (b + (offset if p else 0)) * size
                copy = pltpu.make_async_copy(
                    part.at[:, pl.ds(column, size)],
                    blocks.at[b, pl.ds(start, rows), :],
                    sems.at[p, b],
                )
                copies[b].append((first, copy))
    for pair in copies:
        for when, copy in pair:
            pl.when(when)(copy.start)

    def wait(b):
        for when, copy in copies[b]:
            pl.when(when)(copy.wait)

    return wait


def dense(name, body, rows_in, vectors, weight, outs, sums=(), steps=2):
    rows = rows_in[0].shape[0]
    tile = rows // steps
    count, offset, parts = weight
    cuts = [len(rows_in), len(vectors), len(parts), len(outs), len(sums)]

    def kernel(side, *refs):
        groups = []
        for size in cuts:
            groups.append(refs[:size])
            refs = refs[size:]
        blocks, sems = refs
        wait = block_loader(groups[2], offset, blocks, side[0], sems)
        if sums:

            @pl.when(pl.program_id(0) == 0)
            def _():
                for ref in groups[4]:
                    ref[...] = jnp.zeros_like(ref)

        body(wait, blocks, groups[0], groups[1], groups[3], groups[4])

    return pl.pallas_call(
        kernel,
        out_shape=tuple(jax.ShapeDtypeStruct((rows, c), d) for c, d in outs)
        + tuple(jax.ShapeDtypeStruct((1, c), F32) for c in sums),
        grid_spec=pltpu.PrefetchScalarGridSpec(
            num_scalar_prefetch=1,
            grid=(steps,),
            in_specs=[
                pl.BlockSpec((tile, a.shape[1]), lambda i, _: (i, 0)) for a in rows_in
            ]
            + [pl.BlockSpec(a.shape, lambda i, _: (0, 0)) for a in vectors]
            + [pl.BlockSpec(memory_space=pl.ANY) for _ in parts],
            out_specs=tuple(pl.BlockSpec((tile, c), lambda i, _: (i, 0)) for c, _ in outs)
            + tuple(pl.BlockSpec((1, c), lambda i, _: (0, 0)) for c in sums),
            scratch_shapes=[
                pltpu.VMEM((count, WIDTH, WIDTH), BF16),
                pltpu.SemaphoreType.DMA((2, count)),
            ],
        ),
        compiler_params=pltpu.CompilerParams(vmem_limit_bytes=60 << 20),
        cost_estimate=HINT,
        name=name,
    )(lax.axis_index("seq").reshape(1), *rows_in, *vectors, *parts)


def normalize(hidden):
    mean_val = jnp.mean(hidden, -1, keepdims=True)
    centred = hidden - mean_val
    scale = lax.rsqrt(jnp.mean(centred * centred, -1, keepdims=True) + EPS)
    return centred * scale, scale


def add_sum(ref, values):
    ref[...] += jnp.sum(values, 0, keepdims=True)


def columns_of(b):
    return slice(b * WIDTH, (b + 1) * WIDTH)


def base_body(wait, blocks, rows, vectors, outs, sums):
    wait(0)
    total = simple(rows[0][...], blocks[0])
    wait(1)
    total = total + simple(rows[1][...], blocks[1]) + vectors[0][...]
    outs[0][...] = total
    outs[1][...] = (normalize(total)[0] * vectors[1][...] + vectors[2][...]).astype(
        BF16
    )


def wide_body(wait, blocks, rows, vectors, outs, sums):
    for b in range(blocks.shape[0]):
        wait(b)
        outs[0][:, columns_of(b)] = simple(rows[0][...], blocks[b]).astype(BF16)


def middle_body(wait, blocks, rows, vectors, outs, sums):
    wait(0)
    total = simple(rows[0][...], blocks[0]) + rows[1][...] + vectors[0][...]
    outs[0][...] = total
    outs[1][...] = (normalize(total)[0] * vectors[1][...] + vectors[2][...]).astype(
        BF16
    )


def expand_body(wait, blocks, rows, vectors, outs, sums):
    for b in range(blocks.shape[0]):
        wait(b)
        upper = simple(rows[0][...], blocks[b]) + vectors[0][:, columns_of(b)]
        below = 0.5 * (1.0 + lax.erf(upper * 0.7071067811865476))
        bell = jnp.exp(-0.5 * upper * upper) * 0.3989422804014327
        outs[0][:, columns_of(b)] = (upper * below).astype(BF16)
        outs[1][:, columns_of(b)] = (below + upper * bell).astype(BF16)


def contract_body(wait, blocks, rows, vectors, outs, sums):
    total = rows[1][...] + vectors[0][...]
    for b in range(blocks.shape[0]):
        wait(b)
        total = total + simple(rows[0][:, columns_of(b)], blocks[b])
    outs[0][...] = total.astype(BF16)


def upper_back_body(wait, blocks, rows, vectors, outs, sums):
    grad = rows[0][...]
    add_sum(sums[1], grad.astype(F32))
    for b in range(blocks.shape[0]):
        wait(b)
        upper = against(grad, blocks[b]) * rows[1][:, columns_of(b)].astype(F32)
        upper = upper.astype(BF16)
        outs[0][:, columns_of(b)] = upper
        add_sum(sums[0].at[:, columns_of(b)], upper.astype(F32))


def norm_back_body(wait, blocks, rows, vectors, outs, sums):
    grad = None
    for b in range(blocks.shape[0]):
        wait(b)
        part = against(rows[0][:, columns_of(b)], blocks[b])
        grad = part if grad is None else grad + part
    xhat, scale = normalize(rows[1][...])
    inner = grad * vectors[0][...]
    back = scale * (
        inner
        - jnp.mean(inner, -1, keepdims=True)
        - xhat * jnp.mean(inner * xhat, -1, keepdims=True)
    )
    total = rows[2][...].astype(F32) + back
    rounded = total.astype(BF16)
    outs[0][...] = rounded
    if len(outs) > 1:
        outs[1][...] = total
    add_sum(sums[0], grad * xhat)
    add_sum(sums[1], grad)
    add_sum(sums[2], rounded.astype(F32))


def against_body(wait, blocks, rows, vectors, outs, sums):
    for b in range(blocks.shape[0]):
        wait(b)
        result = against(rows[0][...], blocks[b]).astype(BF16)
        size = outs[b].shape[1]
        outs[b][...] = result[:, :size]
        if size < WIDTH:
            outs[b + 1][...] = result[:, size:]


def core_gradients(name, core, lefts, rights):
    rows = rights[0].shape[0]
    columns = sum(right.shape[1] for right in rights)
    stacked = len(rights) == 1
    depth = sum(left.shape[1] for left in lefts) if stacked else WIDTH
    tiles, unit = depth // WIDTH, depth // 16
    per = WIDTH // unit // 2
    count = len(lefts)
    ends = [0]
    for array in lefts if stacked else rights:
        ends.append(ends[-1] + array.shape[1] // WIDTH)

    def kernel(core_ref, *refs):
        left, right = refs[:count], refs[count : count + len(rights)]
        sent, keep = refs[count + len(rights) :]

        def run(left_ref, right_ref):
            grad = across(left_ref[...], right_ref[...]).astype(BF16)
            for mine in range(2):

                @pl.when(core_ref[0] == mine)
                def _():
                    for j in range(per):
                        own, other = 2 * j + mine, 2 * j + 1 - mine
                        keep[j] = grad[own * unit : (own + 1) * unit]
                        sent[j] = grad[other * unit : (other + 1) * unit]

        if count == 1:
            run(left[0], right[0])
        else:
            place = pl.program_id(0 if stacked else 1)
            for k in range(count):
                here = jnp.logical_and(place >= ends[k], place < ends[k + 1])
                pl.when(here)(
                    functools.partial(run, left[k], right[0 if stacked else k])
                )

    def clipped(index, k, blocks):
        return jnp.clip(index - ends[k], 0, blocks - 1)

    def left_spec(k, left):
        blocks = left.shape[1] // WIDTH
        if stacked:
            return pl.BlockSpec(
                (rows, WIDTH), lambda i, n, _: (0, clipped(i, k, blocks))
            )
        return pl.BlockSpec((rows, WIDTH), lambda i, n, _: (0, 0))

    def right_spec(k, right):
        blocks = right.shape[1] // WIDTH
        if stacked:
            return pl.BlockSpec((rows, WIDTH), lambda i, n, _: (0, n))
        return pl.BlockSpec((rows, WIDTH), lambda i, n, _: (0, clipped(n, k, blocks)))

    half = jax.ShapeDtypeStruct((8, unit, columns), BF16)
    return pl.pallas_call(
        kernel,
        out_shape=(half, half),
        grid_spec=pltpu.PrefetchScalarGridSpec(
            num_scalar_prefetch=1,
            grid=(tiles, columns // WIDTH),
            in_specs=[left_spec(k, left) for k, left in enumerate(lefts)]
            + [right_spec(k, right) for k, right in enumerate(rights)],
            out_specs=(pl.BlockSpec((per, unit, WIDTH), lambda i, n, _: (i, 0, n)),) * 2,
        ),
        compiler_params=pltpu.CompilerParams(vmem_limit_bytes=60 << 20),
        cost_estimate=HINT,
        name=name,
    )(core, *lefts, *rights)


def head_window(head):
    start = head * HEAD_DIM
    first = start // LANES * LANES
    size = LANES if start + HEAD_DIM <= first + LANES else 2 * LANES
    return first, size, start - first


def head_mask(size, offset):
    lane = lax.broadcasted_iota(jnp.int32, (1, size), 1)
    return (lane >= offset) & (lane < offset + HEAD_DIM)


def head_groups(width, slots):
    heads = [(head,) + head_window(head) for head in range(width // HEAD_DIM)]
    count = max(1, 2048 // slots)
    return [heads[i : i + count] for i in range(0, len(heads), count)]


def masked(ref, first, size, offset):
    return jnp.where(head_mask(size, offset), ref[:, first : first + size], 0)


def place(ref, start, size, offset, result):
    result = result.astype(BF16)
    if offset:
        result = jnp.where(
            head_mask(size, offset), result, ref[:, start : start + size]
        )
    ref[:, start : start + size] = result


def attend_kernel(lengths, qkv, mixed, probs_out):
    slots, width = mixed.shape
    live = lax.broadcasted_iota(jnp.int32, (1, slots), 1) < lengths[pl.program_id(0)]
    for group in head_groups(width, slots):
        scores = [
            against(
                masked(qkv, first, size, offset),
                qkv[:, width + first : width + first + size],
            )
            for _, first, size, offset in group
        ]
        scores = [jnp.where(live, s * HEAD_DIM ** (-0.5), NEG) for s in scores]
        raised = [jnp.exp(s - jnp.max(s, -1, keepdims=True)) for s in scores]
        probs = [
            (r * (1.0 / jnp.sum(r, -1, keepdims=True))).astype(BF16) for r in raised
        ]
        results = [
            simple(p, qkv[:, 2 * width + first : 2 * width + first + size])
            for p, (_, first, size, _) in zip(probs, group)
        ]
        for p, result, (head, first, size, offset) in zip(probs, results, group):
            probs_out[head * slots : (head + 1) * slots, :] = p
            place(mixed, first, size, offset, result)


def attend(qkv, lengths):
    per = lengths.shape[0]
    rows, width = qkv.shape[0], qkv.shape[1] // 3
    slots, heads = rows // per, width // HEAD_DIM
    return pl.pallas_call(
        attend_kernel,
        out_shape=(
            jax.ShapeDtypeStruct((rows, width), BF16),
            jax.ShapeDtypeStruct((rows * heads, slots), BF16),
        ),
        grid_spec=pltpu.PrefetchScalarGridSpec(
            num_scalar_prefetch=1,
            grid=(per,),
            in_specs=[pl.BlockSpec((slots, 3 * width), lambda i, _: (i, 0))],
            out_specs=(
                pl.BlockSpec((slots, width), lambda i, _: (i, 0)),
                pl.BlockSpec((heads * slots, slots), lambda i, _: (i, 0)),
            ),
        ),
        compiler_params=pltpu.CompilerParams(vmem_limit_bytes=56 << 20),
        cost_estimate=HINT,
        name="attend",
    )(lengths, qkv)


def attend_back_kernel(qkv, probs_in, grad_mixed, grad_qkv):
    slots, width = grad_mixed.shape
    scale = HEAD_DIM ** (-0.5)
    for group in head_groups(width, slots):
        grads = [masked(grad_mixed, *window) for _, *window in group]
        grad_probs = [
            against(g, qkv[:, 2 * width + first : 2 * width + first + size])
            for g, (_, first, size, _) in zip(grads, group)
        ]
        probs = [
            probs_in[head * slots : (head + 1) * slots, :] for head, _, _, _ in group
        ]
        grad_values = [across(p, g) for p, g in zip(probs, grads)]
        probs = [p.astype(F32) for p in probs]
        sums = [
            jnp.sum(g * p, -1, keepdims=True) for g, p in zip(grad_probs, probs)
        ]
        scores = [
            (p * (g - total)).astype(BF16)
            for p, g, total in zip(probs, grad_probs, sums)
        ]
        grad_queries = [
            simple(s, qkv[:, width + first : width + first + size]) * scale
            for s, (_, first, size, _) in zip(scores, group)
        ]
        grad_keys = [
            across(s, qkv[:, first : first + size]) * scale
            for s, (_, first, size, _) in zip(scores, group)
        ]
        for part, results in enumerate((grad_queries, grad_keys, grad_values)):
            for result, (_, first, size, offset) in zip(results, group):
                place(grad_qkv, part * width + first, size, offset, result)


def attend_back(qkv, probs, grad_mixed, per):
    rows, width = grad_mixed.shape
    slots, heads = rows // per, width // HEAD_DIM
    return pl.pallas_call(
        attend_back_kernel,
        out_shape=jax.ShapeDtypeStruct((rows, 3 * width), BF16),
        grid=(per,),
        in_specs=[
            pl.BlockSpec((slots, 3 * width), lambda i: (i, 0)),
            pl.BlockSpec((heads * slots, slots), lambda i: (i, 0)),
            pl.BlockSpec((slots, width), lambda i: (i, 0)),
        ],
        out_specs=pl.BlockSpec((slots, 3 * width), lambda i: (i, 0)),
        compiler_params=pltpu.CompilerParams(vmem_limit_bytes=56 << 20),
        cost_estimate=HINT,
        name="attend_back",
    )(qkv, probs, grad_mixed)


def per_device(
    latents,
    skip_store,
    lengths,
    cotangent,
    skip_weight,
    skip_bias,
    first_gain,
    first_shift,
    inward_weight,
    outward_weight,
    outward_bias,
    second_gain,
    second_shift,
    expand_weight,
    expand_bias,
    contract_weight,
    contract_bias,
):
    items, slot_dev, width = latents.shape
    ways, side = lax.axis_size("seq"), lax.axis_index("seq")
    slots = slot_dev * ways
    per = -(-items // ways)
    rows = per * slots
    fast = fast_mesh()
    chain = Chain()

    live = jnp.pad(lengths, (0, per * ways - items), constant_values=slots)
    live = pick(live, side, per)

    (
        skip_offset,
        gain_first,
        shift_first,
        outward_offset,
        gain_second,
        shift_second,
        expand_offset,
        contract_offset,
    ) = (
        vector.reshape(1, -1)
        for vector in gather_vectors(
            (
                skip_bias,
                first_gain,
                first_shift,
                outward_bias,
                second_gain,
                second_shift,
                expand_bias,
                contract_bias,
            )
        )
    )
    if fast:
        skip_piece = flip(chain.run(eighth, skip_weight), "seq")
        skip_parts = (skip_weight, share(skip_piece))
        attention_piece = flip(
            chain.run(
                lambda a, b: jnp.concatenate([eighth(a), eighth(b)], 1),
                inward_weight,
                outward_weight,
            ),
            "seq",
        )
        attention_other = share(attention_piece)
        inward_parts = (inward_weight, attention_other)
        outward_parts = (outward_weight, attention_other)
        skip_pieces = chain.run(lambda a: start_items(a, per), skip_store)
        latent_pieces = chain.run(lambda a: start_items(a, per), latents)
        skip_rows, latent_rows = chain.run(
            lambda a, b: (
                joined_pieces(a, 2).reshape(rows, width),
                joined_pieces(b, 1).reshape(rows, width),
            ),
            skip_pieces,
            latent_pieces,
        )
        expand_piece = flip(chain.run(eighth, expand_weight), "seq")
        contract_piece = flip(chain.run(eighth, contract_weight), "seq")
        grad_pieces = chain.run(lambda a: start_items(a, per), cotangent)
    else:
        skip_parts, inward_parts, outward_parts, expand_parts, contract_parts = (
            (lax.all_gather(shard, "seq", axis=0, tiled=True),)
            for shard in (
                skip_weight,
                inward_weight,
                outward_weight,
                expand_weight,
                contract_weight,
            )
        )
        skip_rows = joined_pieces(start_items(skip_store, per), 2)
        latent_rows = joined_pieces(start_items(latents, per), 1)
        grad_pieces = start_items(cotangent, per)
    skip_matrix, inward_matrix = (2, 0, skip_parts), (3, 0, inward_parts)
    outward_matrix = (1, 3, outward_parts)
    skip_rows, latent_rows = (a.reshape(rows, width) for a in (skip_rows, latent_rows))
    one, both = [(width, BF16)], [(width, F32), (width, BF16)]

    base, first_normed = chain.run(
        lambda a, b, *w: dense(
            "base",
            base_body,
            (a, b),
            (skip_offset, gain_first, shift_first),
            (2, 0, w),
            both,
        ),
        latent_rows,
        skip_rows,
        *skip_parts,
    )
    if fast:
        expand_parts = (expand_weight, share(*chain.enter(expand_piece)))
    (qkv_vals,) = chain.run(
        lambda a: dense("inward", wide_body, (a,), (), inward_matrix, [(3 * width, BF16)]),
        first_normed,
    )
    if fast:
        contract_parts = (contract_weight, share(*chain.enter(contract_piece)))
    expand_matrix, contract_matrix = (4, 0, expand_parts), (4, 0, contract_parts)
    mixed_rows, probs = chain.run(lambda a: attend(a, live), qkv_vals)
    middle, second_normed = dense(
        "middle",
        middle_body,
        (mixed_rows, base),
        (outward_offset, gain_second, shift_second),
        outward_matrix,
        both,
    )
    activated, slope = dense(
        "expand",
        expand_body,
        (second_normed,),
        (expand_offset,),
        expand_matrix,
        [(expand_offset.shape[1], BF16)] * 2,
    )
    chain.leave(activated)
    grad_out = chain.run(
        lambda *a: joined_pieces(a, 1).reshape(rows, width), *grad_pieces
    )
    contract_sum = Reduction(chain, "contract_grad", (activated,), (grad_out,))
    grad_upper, grad_expand_off, grad_contract_off = chain.run(
        lambda *a: dense(
            "upper_back",
            upper_back_body,
            a,
            (),
            contract_matrix,
            [(expand_offset.shape[1], BF16)],
            [expand_offset.shape[1], width],
        ),
        grad_out,
        slope,
    )
    contract_sum.step()
    expand_sum = Reduction(chain, "expand_grad", (second_normed,), (grad_upper,))
    grad_branch, grad_middle, grad_gain_two, grad_shift_two, grad_outward_off = chain.run(
        lambda *a: dense(
            "middle_back",
            norm_back_body,
            a,
            (gain_second,),
            expand_matrix,
            both[::-1],
            [width] * 3,
        ),
        grad_upper,
        middle,
        grad_out,
    )
    expand_sum.step()
    (grad_mixed,) = chain.run(
        lambda a: dense("mixed_back", against_body, (a,), (), outward_matrix, one),
        grad_branch,
    )
    grad_qkv = attend_back(qkv_vals, probs, grad_mixed, per)
    chain.leave(grad_qkv)
    contract_sum.step()
    attention_sum = Reduction(
        chain,
        "attention_grad",
        (first_normed, mixed_rows),
        (grad_qkv, grad_branch),
    )
    grad_base, grad_gain_one, grad_shift_one, grad_skip_off = chain.run(
        lambda *a: dense(
            "base_back", norm_back_body, a, (gain_first,), inward_matrix, one, [width] * 3
        ),
        grad_qkv,
        base,
        grad_middle,
    )
    vector_sum = VectorReduction(
        chain,
        (
            grad_skip_off,
            grad_gain_one,
            grad_shift_one,
            grad_outward_off,
            grad_gain_two,
            grad_shift_two,
            grad_expand_off,
            grad_contract_off,
        ),
    )
    attention_sum.step()
    contract_sum.step()
    expand_sum.step()
    skip_sum = Reduction(chain, "skip_grad", (latent_rows, skip_rows), (grad_base,))
    contract_sum.step()
    vector_sum.step()
    halves = ways == 2
    columns = [width] + ([width // 2] * 2 if halves else [width])
    grad_latents, *grad_skip = chain.run(
        lambda a: dense(
            "joined_back",
            against_body,
            (a,),
            (),
            skip_matrix,
            [(size, BF16) for size in columns],
        ),
        grad_base,
    )
    skip_sum.step()
    contract_sum.step()
    expand_sum.step()
    vector_sum.step()
    latent_pieces = chain.run(
        lambda a: return_items(a.reshape(per, slots, width), 1), grad_latents
    )
    if halves:
        skip_pieces = chain.run(
            lambda a, b: (jnp.where(side == 0, a, b), jnp.where(side == 0, b, a)),
            *grad_skip,
        )
        skip_pieces = [a.reshape(per, slots, width // 2) for a in skip_pieces]
        skip_pieces[1] = flip(skip_pieces[1], "seq")
    else:
        skip_pieces = return_items(grad_skip[0].reshape(per, slots, width), 2)
    (result,) = chain.run(
        lambda *a: dense(
            "contract", contract_body, a, (contract_offset,), contract_matrix, one
        ),
        activated,
        middle,
    )
    expand_sum.step()
    output_pieces = chain.run(
        lambda a: return_items(a.reshape(per, slots, width), 1), result
    )
    attention_sum.step()
    vector_sum.step()
    expand_sum.step()
    vector_sum.step()
    skip_sum.step()
    sum_contract = contract_sum.finish()
    attention_sum.step()
    vector_sum.step()
    attention_sum.step()
    skip_sum.step()
    skip_sum.step()
    attention_sum.step()
    skip_sum.step()
    sum_expand = expand_sum.finish()
    grad_latents = chain.run(
        lambda *a: joined_pieces(a, 0)[:items].astype(F32), *latent_pieces
    )
    grad_skip = chain.run(lambda *a: joined_pieces(a, 0)[:items], *skip_pieces)
    output = chain.run(lambda *a: joined_pieces(a, 0)[:items], *output_pieces)
    sum_attention = attention_sum.finish()
    sum_inward, sum_outward = jnp.split(sum_attention, [3 * width], 1)
    sum_skipw = skip_sum.finish()
    (
        sum_skipb,
        sum_gain1,
        sum_shift1,
        sum_outb,
        sum_gain2,
        sum_shift2,
        sum_expandb,
        sum_contractb,
    ) = vector_sum.finish()
    return (
        output,
        grad_latents,
        grad_skip,
        sum_skipw,
        sum_skipb,
        sum_gain1,
        sum_shift1,
        sum_inward,
        sum_outward,
        sum_outb,
        sum_gain2,
        sum_shift2,
        sum_expand,
        sum_expandb,
        sum_contract,
        sum_contractb,
    )


def solution(mesh):
    wide, seq = mesh.shape["wide"], mesh.shape["seq"]
    devices = mesh.devices.reshape(wide // 8, 2, 2, 2, seq)
    return jax.shard_map(
        per_device,
        mesh=Mesh(devices, WIDE + ("seq",)),
        in_specs=(
            P(WIDE, "seq", None),
            P(WIDE, None, "seq"),
            P(WIDE),
            P(WIDE, "seq", None),
            P("seq", None),
            P("seq"),
            P("seq"),
            P("seq"),
            P("seq", None),
            P("seq", None),
            P("seq"),
            P("seq"),
            P("seq"),
            P("seq", None),
            P("seq"),
            P("seq", None),
            P("seq"),
        ),
        out_specs=(
            P(WIDE, "seq", None),
            P(WIDE, "seq", None),
            P(WIDE, None, "seq"),
            P("seq", None),
            P("seq"),
            P("seq"),
            P("seq"),
            P("seq", None),
            P("seq", None),
            P("seq"),
            P("seq"),
            P("seq"),
            P("seq", None),
            P("seq"),
            P("seq", None),
            P("seq"),
        ),
        check_vma=False,
    )
```

time: 963 us -> 695 us (0.72)
  waiting for transfers between devices: 498 us -> 218 us
  Pallas kernels: 23.7 us -> 263 us
  matrix products: 208 us -> 0 us
  local copies, waits for them, and re-layouts: 65 us -> 49.6 us
    pallas_call x0 -> x14, Pallas kernels: none -> 239 us  [the longest x10 173 us: dense(): pl.pallas_call(kernel, out_shape=tuple((jax.ShapeDtypeStruct((rows, c), d...]
    dot_general x15 -> x0, matrix products: 208 us -> none  [the longest x5 78.1 us: simple(): return jnp.dot(left_side, right_side, preferred_element_type=F32)]
    ppermute x35 -> x31, waiting for transfers between devices: 353 us -> 200 us  [flip(): return lax.ppermute(array, axis, [(0, 1), (1, 0)])]
    ppermute x8 -> x5, waiting for transfers between devices: 145 us -> 16 us  [the longest x2 16 us: return_items(): lax.ppermute(piece, 'seq', [(i, (i + hop) % ways) for i in range(ways)])]
    convert_element_type x28 -> x24, other arithmetic: 61.7 us -> 79.5 us  [the longest x20 55.9 us: added(): return (parts[0].astype(F32) + parts[1].astype(F32)).astype(BF16)]
    unnamed x102 -> x84, local copies, waits for them, and re-layouts: 25.5 us -> 8.84 us
    reduce_sum x6 -> x0, other arithmetic: 13.8 us -> none  [the longest x1 4.33 us: per_device(): grad_outward_off = jnp.sum(grad_branch.astype(F32), 0)]
    squeeze x14 -> x0, local copies, waits for them, and re-layouts: 13.1 us -> none  [block(): return lax.dynamic_index_in_dim(array, index, axis, keepdims=False)]
  transfers between devices with their start and end apart: 50 -> 44, of which waited for: 20 -> 18; matrix products, arithmetic and copies ran while one was open for 27% -> 19% of each run, Pallas kernels for 1% -> 38%
where the time goes in v3:
time: 695 us; the launch traced here: 687 us
  Pallas kernels  263 us (38%)
  waiting for transfers between devices  218 us (31%)
  other arithmetic  102 us (15%)
  local copies, waits for them, and re-layouts  49.6 us (7%)
  starting transfers between devices  39.1 us (6%)
  between operations  15.2 us (2%)
    ppermute x31, waiting for transfers between devices, flip(): return lax.ppermute(array, axis, [(0, 1), (1, 0)])  200 us
    pallas_call x10, Pallas kernels, dense(): pl.pallas_call(kernel, out_shape=tuple((jax.ShapeDtypeStruct((rows, c), d...  173 us
    pallas_call x4, Pallas kernels, core_gradients(): pl.pallas_call(kernel, out_shape=(half, half), grid_spec=pltpu.PrefetchSc...  66.1 us
    convert_element_type x20, other arithmetic, added(): return (parts[0].astype(F32) + parts[1].astype(F32)).astype(BF16)  55.9 us
    ppermute x31, starting transfers between devices, flip(): return lax.ppermute(array, axis, [(0, 1), (1, 0)])  34.2 us
    convert_element_type x3, other arithmetic, finish(): return self.chain.run(lambda a: a.astype(F32), self.total)  19.9 us
    select_n x6, other arithmetic, ordered(): jnp.where(index == 0, jnp.concatenate([mine, other], axis), jnp.concatena...  16.2 us
    dynamic_slice x11, local copies, waits for them, and re-layouts, pick(): return lax.dynamic_slice_in_dim(array, index * size, size, axis)  16.2 us
  transfers between devices with their start and end apart: 44, of which 18 were waited for; matrix products, arithmetic and copies ran while one was open for 19% of the time, Pallas kernels for 38%

profile of v3, /device:TPU:0, one launch (start us, length us, event | category | flops | bytes accessed | tf_op | source)
XLA Modules:
  0.0 687.5 jit_solution(4541070392256599166)
XLA Ops:
  30.6 53.4 %collective-permute-done.3 = bf16[1,6336]{1,0:T(2,128)(2,1)S(1)} collective-permute-done((bf16[1,6336]{1,0:T(2,128)(2,1)S(1)}, bf16[1,6336]{1,0:T(2,128)(2,1)S(1)}, u32[]{:S(2)}, u32[]{:S(2)}) %collective-permute-start.3) | collective-permute-done | bytes 12704 | tf_op jit(solution)/shard_map/ppermute | solution.py:43
  109.2 13.3 %base.1 = (f32[896,1152]{1,0:T(8,128)}, bf16[896,1152]{1,0:T(8,128)(2,1)}) custom-call(s32[1]{0:T(128)} %bitcast.side, bf16[896,1152]{1,0:T(8,128)(2,1)} %bitcast.78, bf16[896,1152]{1,0:T(8,128)(2,1)} %maximum_select_fusion.1.refs_1_, f32[1,1152]{1,0:T(1,128)} %reshape.359.refs_2_, f32[1,1152]{1,0:T(1,128)} %reshape.360.refs_3_, ...), custom_call_target="tpu_custom_call" | custom-call | flops 9999999827968 | bytes 1000000000 | tf_op jit(solution)/shard_map/base/pallas_call | solution.py:286
  124.8 15.3 %inward.1.qkv = bf16[896,3456]{1,0:T(8,128)(2,1)} custom-call(s32[1]{0:T(128)} %bitcast.side, bf16[896,1152]{1,0:T(8,128)(2,1)} %get-tuple-element.215.refs_0_, bf16[576,3456]{1,0:T(8,128)(2,1)} %refs_4_.3, bf16[576,4608]{1,0:T(8,128)(2,1)} %all-gather.11.cloned.1.call-done.refs_2_.refs_6_.refs_5_), custom_call_target="tpu_custom_call" | custom-call | flops 9999999827968 | bytes 1000000000 | tf_op jit(solution)/shard_map/inward/pallas_call | solution.py:286
  140.1 10.7 %attend.1 = (bf16[896,1152]{1,0:T(8,128)(2,1)}, bf16[14336,128]{1,0:T(8,128)(2,1)}) custom-call(s32[7]{0:T(128)} %pad_dynamic-slice_fusion.6.lengths, bf16[896,3456]{1,0:T(8,128)(2,1)} %inward.1.qkv), custom_call_target="tpu_custom_call" | custom-call | flops 9999999827968 | bytes 1000000000 | tf_op jit(solution)/shard_map/attend/pallas_call | solution.py:545
  150.9 9.5 %middle.1 = (f32[896,1152]{1,0:T(8,128)}, bf16[896,1152]{1,0:T(8,128)(2,1)}) custom-call(s32[1]{0:T(128)} %bitcast.side, bf16[896,1152]{1,0:T(8,128)(2,1)} %get-tuple-element.216.refs_0_.refs_1_, f32[896,1152]{1,0:T(8,128)} %get-tuple-element.221.refs_1_, f32[1,1152]{1,0:T(1,128)} %reshape.362.refs_2_, f32[1,1152]{1,0:T(1,128)} %reshape.363.refs_3_, ...), custom_call_target="tpu_custom_call" | custom-call | flops 9999999827968 | bytes 1000000000 | tf_op jit(solution)/shard_map/middle/pallas_call | solution.py:286
  160.5 25.2 %expand.1 = (bf16[896,4608]{1,0:T(8,128)(2,1)}, bf16[896,4608]{1,0:T(8,128)(2,1)}) custom-call(s32[1]{0:T(128)} %bitcast.side, bf16[896,1152]{1,0:T(8,128)(2,1)} %get-tuple-element.201.refs_0_, f32[1,4608]{1,0:T(1,128)} %bitcast.85, bf16[576,4608]{1,0:T(8,128)(2,1)} %refs_4_.2, bf16[576,4608]{1,0:T(8,128)(2,1)} %all-gather.13.cloned.1.call-done.refs_3_.refs_5_), custom_call_target="tpu_custom_call" | custom-call | flops 9999999827968 | bytes 1000000000 | tf_op jit(solution)/shard_map/expand/pallas_call | solution.py:286
  189.3 17.9 %contract_grad.1 = (bf16[8,288,1152]{2,1,0:T(8,128)(2,1)}, bf16[8,288,1152]{2,1,0:T(8,128)(2,1)}) custom-call(s32[1]{0:T(128)} %bitcast.5.core_ref, bf16[896,4608]{1,0:T(8,128)(2,1)} %get-tuple-element.271.refs_0_, bf16[896,1152]{1,0:T(8,128)(2,1)} %bitcast.81), custom_call_target="tpu_custom_call" | custom-call | flops 9999999827968 | bytes 1000000000 | tf_op jit(solution)/shard_map/contract_grad/pallas_call | solution.py:469
  207.5 22.7 %upper_back.1 = (bf16[896,4608]{1,0:T(8,128)(2,1)}, f32[1,4608]{1,0:T(1,128)}, f32[1,1152]{1,0:T(1,128)}) custom-call(s32[1]{0:T(128)} %bitcast.side, bf16[896,1152]{1,0:T(8,128)(2,1)} %bitcast.82, bf16[896,4608]{1,0:T(8,128)(2,1)} %get-tuple-element.195.refs_1_, bf16[2304,1152]{1,0:T(8,128)(2,1)} %refs_3_.1, ...), custom_call_target="tpu_custom_call" | custom-call | flops 9999999827968 | bytes 1000000000 | tf_op jit(solution)/shard_map/upper_back/pallas_call | solution.py:286
  239.3 17.8 %expand_grad.1 = (bf16[8,72,4608]{2,1,0:T(8,128)(2,1)}, bf16[8,72,4608]{2,1,0:T(8,128)(2,1)}) custom-call(s32[1]{0:T(128)} %bitcast.5.core_ref, bf16[896,1152]{1,0:T(8,128)(2,1)} %get-tuple-element.201.refs_0_, bf16[896,4608]{1,0:T(8,128)(2,1)} %get-tuple-element.204.refs_1_.refs_0_), custom_call_target="tpu_custom_call" | custom-call | flops 9999999827968 | bytes 1000000000 | tf_op jit(solution)/shard_map/expand_grad/pallas_call | solution.py:469
  257.1 24.6 %middle_back.1 = (bf16[896,1152]{1,0:T(8,128)(2,1)}, f32[896,1152]{1,0:T(8,128)}, f32[1,1152]{1,0:T(1,128)}, f32[1,1152]{1,0:T(1,128)}, f32[1,1152]{1,0:T(1,128)}) custom-call(s32[1]{0:T(128)} %bitcast.side, bf16[896,4608]{1,0:T(8,128)(2,1)} %get-tuple-element.204.refs_1_.refs_0_, f32[896,1152]{1,0:T(8,128)} %get-tuple-element.272.refs_1_, ...), custom_call_target="tpu_custom_call" | custom-call | flops 9999999827968 | bytes 1000000000 | tf_op jit(solution)/shard_map/middle_back/pallas_call | solution.py:286
  296.9 13.3 %attend_back.1.refs_2_.refs_0_ = bf16[896,3456]{1,0:T(8,128)(2,1)} custom-call(bf16[896,3456]{1,0:T(8,128)(2,1)} %inward.1.qkv, bf16[14336,128]{1,0:T(8,128)(2,1)} %get-tuple-element.187.probs_in, bf16[896,1152]{1,0:T(8,128)(2,1)} %mixed_back.1.grad_mixed), custom_call_target="tpu_custom_call" | custom-call | flops 9999999827968 | bytes 1000000000 | tf_op jit(solution)/shard_map/attend_back/pallas_call | solution.py:603
  315.9 18.9 %attention_grad.1 = (bf16[8,72,4608]{2,1,0:T(8,128)(2,1)}, bf16[8,72,4608]{2,1,0:T(8,128)(2,1)}) custom-call(s32[1]{0:T(128)} %bitcast.5.core_ref, bf16[896,1152]{1,0:T(8,128)(2,1)} %get-tuple-element.215.refs_0_, bf16[896,1152]{1,0:T(8,128)(2,1)} %get-tuple-element.216.refs_0_.refs_1_, bf16[896,3456]{1,0:T(8,128)(2,1)} %attend_back.1.refs_2_.refs_0_, ...), custom_call_target="tpu_custom_call" | custom-call | flops 9999999827968 | bytes 1000000000 | tf_op jit(solution)/shard_map/attention_grad/pallas_call | solution.py:469
  334.9 20.5 %base_back.1 = (bf16[896,1152]{1,0:T(8,128)(2,1)}, f32[1,1152]{1,0:T(1,128)}, f32[1,1152]{1,0:T(1,128)}, f32[1,1152]{1,0:T(1,128)}) custom-call(s32[1]{0:T(128)} %bitcast.side, bf16[896,3456]{1,0:T(8,128)(2,1)} %attend_back.1.refs_2_.refs_0_, f32[896,1152]{1,0:T(8,128)} %get-tuple-element.221.refs_1_, f32[896,1152]{1,0:T(8,128)} %get-tuple-element.222.refs_2_, ...), custom_call_target="tpu_custom_call" | custom-call | flops 9999999827968 | bytes 1000000000 | tf_op jit(solution)/shard_map/base_back/pallas_call | solution.py:286
  381.1 11.5 %skip_grad.1 = (bf16[8,144,1152]{2,1,0:T(8,128)(2,1)}, bf16[8,144,1152]{2,1,0:T(8,128)(2,1)}) custom-call(s32[1]{0:T(128)} %bitcast.5.core_ref, bf16[896,1152]{1,0:T(8,128)(2,1)} %bitcast.79, bf16[896,1152]{1,0:T(8,128)(2,1)} %maximum_select_fusion.1.refs_1_, bf16[896,1152]{1,0:T(8,128)(2,1)} %get-tuple-element.255.refs_2_.refs_0_), custom_call_target="tpu_custom_call" | custom-call | flops 9999999827968 | bytes 1000000000 | tf_op jit(solution)/shard_map/skip_grad/pallas_call | solution.py:469
  399.1 12.0 %joined_back.1 = (bf16[896,1152]{1,0:T(8,128)(2,1)}, bf16[896,576]{1,0:T(8,128)(2,1)}, bf16[896,576]{1,0:T(8,128)(2,1)}) custom-call(s32[1]{0:T(128)} %bitcast.side, bf16[896,1152]{1,0:T(8,128)(2,1)} %get-tuple-element.255.refs_2_.refs_0_, bf16[1152,1152]{1,0:T(8,128)(2,1)} %refs_1_.5, bf16[1152,1152]{1,0:T(8,128)(2,1)} %all-gather.9.cloned.1.call-done.refs_6_.refs_2_), custom_call_target="tpu_custom_call" | custom-call | flops 9999999827968 | bytes 1000000000 | tf_op jit(solution)/shard_map/joined_back/pallas_call | solution.py:286
  415.0 14.0 %collective-permute-done.18 = bf16[288,1152]{1,0:T(8,128)(2,1)} collective-permute-done((bf16[288,1152]{1,0:T(8,128)(2,1)}, bf16[288,1152]{1,0:T(8,128)(2,1)}, u32[]{:S(2)}, u32[]{:S(2)}) %collective-permute-start.18) | collective-permute-done | bytes 663584 | tf_op jit(solution)/shard_map/ppermute | solution.py:43
  441.0 22.5 %contract.1 = bf16[896,1152]{1,0:T(8,128)(2,1)} custom-call(s32[1]{0:T(128)} %bitcast.side, bf16[896,4608]{1,0:T(8,128)(2,1)} %get-tuple-element.271.refs_0_, f32[896,1152]{1,0:T(8,128)} %get-tuple-element.272.refs_1_, f32[1,1152]{1,0:T(1,128)} %reshape.366.refs_2_, bf16[2304,1152]{1,0:T(8,128)(2,1)} %refs_3_.1, ...), custom_call_target="tpu_custom_call" | custom-call | flops 9999999827968 | bytes 1000000000 | tf_op jit(solution)/shard_map/contract/pallas_call | solution.py:286
  475.4 19.9 %collective-permute-done.24 = bf16[72,4608]{1,0:T(8,128)(2,1)S(1)} collective-permute-done((bf16[72,4608]{1,0:T(8,128)(2,1)S(1)}, bf16[72,4608]{1,0:T(8,128)(2,1)S(1)}, u32[]{:S(2)}, u32[]{:S(2)}) %collective-permute-start.24) | collective-permute-done | bytes 663584 | tf_op jit(solution)/shard_map/ppermute | solution.py:43
  502.2 23.6 %collective-permute-done.27 = bf16[2,2,144,1152]{3,2,1,0:T(8,128)(2,1)S(1)} collective-permute-done((bf16[2,2,144,1152]{3,2,1,0:T(8,128)(2,1)}, bf16[2,2,144,1152]{3,2,1,0:T(8,128)(2,1)S(1)}, u32[]{:S(2)}, u32[]{:S(2)}) %collective-permute-start.27) | collective-permute-done | bytes 1327136 | tf_op jit(solution)/shard_map/ppermute | solution.py:43
  534.3 15.9 %collective-permute-done.30 = bf16[2,72,4608]{2,1,0:T(8,128)(2,1)} collective-permute-done((bf16[2,72,4608]{2,1,0:T(8,128)(2,1)}, bf16[2,72,4608]{2,1,0:T(8,128)(2,1)}, u32[]{:S(2)}, u32[]{:S(2)}) %collective-permute-start.30) | collective-permute-done | bytes 1327136 | tf_op jit(solution)/shard_map/ppermute | solution.py:43
  577.3 19.2 %collective-permute-done.35 = bf16[72,4608]{1,0:T(8,128)(2,1)S(1)} collective-permute-done((bf16[72,4608]{1,0:T(8,128)(2,1)S(1)}, bf16[72,4608]{1,0:T(8,128)(2,1)S(1)}, u32[]{:S(2)}, u32[]{:S(2)}) %collective-permute-start.35) | collective-permute-done | bytes 663584 | tf_op jit(solution)/shard_map/ppermute | solution.py:43
  597.7 10.8 %collective-permute-done.34 = bf16[144,1152]{1,0:T(8,128)(2,1)S(1)} collective-permute-done((bf16[144,1152]{1,0:T(8,128)(2,1)S(1)}, bf16[144,1152]{1,0:T(8,128)(2,1)S(1)}, u32[]{:S(2)}, u32[]{:S(2)}) %collective-permute-start.34) | collective-permute-done | bytes 331808 | tf_op jit(solution)/shard_map/ppermute | solution.py:43
  625.9 9.6 %collective-permute-done.23 = bf16[7,64,1152]{2,1,0:T(8,128)(2,1)} collective-permute-done((bf16[7,64,1152]{2,1,0:T(8,128)(2,1)}, bf16[7,64,1152]{2,1,0:T(8,128)(2,1)}, u32[]{:S(2)}, u32[]{:S(2)}) %collective-permute-start.23) | collective-permute-done | bytes 1032224 | tf_op jit(solution)/shard_map/ppermute | solution.py:216
  639.2 14.5 %collective-permute-done.22 = bf16[7,128,576]{1,2,0:T(8,128)(2,1)} collective-permute-done((bf16[7,128,576]{1,2,0:T(8,128)(2,1)}, bf16[7,128,576]{1,2,0:T(8,128)(2,1)}, u32[]{:S(2)}, u32[]{:S(2)}) %collective-permute-start.22) | collective-permute-done | bytes 1032224 | tf_op jit(solution)/shard_map/ppermute | solution.py:43
  (253 shorter events, 235.5 us)
Async XLA Ops:
  7.2 102.0 %all-gather.9.cloned.1.call-start = ((), (), s32[]{:S(2)}) async-start(), calls=%async_computation | async-start | bytes 2985984 | tf_op jit(solution)/shard_map/all_gather | solution.py:92
  20.0 104.8 %all-gather.11.cloned.1.call-start = ((), (), s32[]{:S(2)}) async-start(), calls=%async_computation.1 | async-start | bytes 5971968 | tf_op jit(solution)/shard_map/all_gather | solution.py:92
  22.9 66.7 %collective-permute-start.4 = (bf16[72,4608]{1,0:T(8,128)(2,1)}, bf16[72,4608]{1,0:T(8,128)(2,1)}, u32[]{:S(2)}, u32[]{:S(2)}) collective-permute-start(bf16[72,4608]{1,0:T(8,128)(2,1)} %pad_maximum_fusion.6), channel_id=1, source_target_pairs={{0,1},{1,0},{2,3},{3,2},{4,5},{5,4},{6,7},{7,6},{8,9},{9,8},{10,11... | collective-permute-start | bytes 1990664 | tf_op jit(solution)/shard_map/ppermute | solution.py:43
  25.9 63.8 %collective-permute-start = (bf16[7,128,576]{1,2,0:T(8,128)(2,1)S(1)}, bf16[7,128,576]{1,2,0:T(8,128)(2,1)}, u32[]{:S(2)}, u32[]{:S(2)}) collective-permute-start(bf16[7,128,576]{1,2,0:T(8,128)(2,1)S(1)} %get-tuple-element.349), channel_id=1, source_target_pairs={{0,1},{1,0},{2,3},{3,2},{4,5},{5,4},{6,7},{7,6},{8,9},{9,8},{10,11... | collective-permute-start | bytes 3096584 | tf_op jit(solution)/shard_map/ppermute | solution.py:190
  27.7 61.9 %collective-permute-start.1 = (bf16[7,64,1152]{2,1,0:T(8,128)(2,1)}, bf16[7,64,1152]{2,1,0:T(8,128)(2,1)}, u32[]{:S(2)}, u32[]{:S(2)}) collective-permute-start(bf16[7,64,1152]{2,1,0:T(8,128)(2,1)} %get-tuple-element.347), channel_id=1, source_target_pairs={{0,1},{1,0},{2,3},{3,2},{4,5},{5,4},{6,7},{7,6},{8,9},{9,8},{10,11... | collective-permute-start | bytes 3096584 | tf_op jit(solution)/shard_map/ppermute | solution.py:190
  29.3 54.7 %collective-permute-start.3 = (bf16[1,6336]{1,0:T(2,128)(2,1)S(1)}, bf16[1,6336]{1,0:T(2,128)(2,1)S(1)}, u32[]{:S(2)}, u32[]{:S(2)}) collective-permute-start(bf16[1,6336]{1,0:T(2,128)(2,1)S(1)} %reshape.337), channel_id=1, source_target_pairs={{0,1},{1,0},{2,3},{3,2},{4,5},{5,4},{6,7},{7,6},{8,9},{9,8},{10,11... | collective-permute-start | bytes 38024 | tf_op jit(solution)/shard_map/ppermute | solution.py:43
  89.6 70.9 %all-gather.13.cloned.1.call-start = ((), (), s32[]{:S(2)}) async-start(), calls=%async_computation.2 | async-start | bytes 5971968 | tf_op jit(solution)/shard_map/all_gather | solution.py:92
  102.1 48.8 %collective-permute-start.7 = (bf16[288,1152]{1,0:T(8,128)(2,1)}, bf16[288,1152]{1,0:T(8,128)(2,1)}, u32[]{:S(2)}, u32[]{:S(2)}) collective-permute-start(bf16[288,1152]{1,0:T(8,128)(2,1)} %constant_dynamic-slice_fusion.12), channel_id=1, source_target_pairs={{0,1},{1,0},{2,3},{3,2},{4,5},{5,4},{6,7},{7,6},{8,9},{9,8},{10,11... | collective-permute-start | bytes 1990664 | tf_op jit(solution)/shard_map/ppermute | solution.py:43
  104.3 81.4 %collective-permute-start.6 = (bf16[7,64,1152]{2,1,0:T(8,128)(2,1)}, bf16[7,64,1152]{2,1,0:T(8,128)(2,1)}, u32[]{:S(2)}, u32[]{:S(2)}) collective-permute-start(bf16[7,64,1152]{2,1,0:T(8,128)(2,1)} %get-tuple-element.345), channel_id=1, source_target_pairs={{0,1},{1,0},{2,3},{3,2},{4,5},{5,4},{6,7},{7,6},{8,9},{9,8},{10,11... | collective-permute-start | bytes 3096584 | tf_op jit(solution)/shard_map/ppermute | solution.py:190
  122.6 84.9 %all-gather.15.cloned.1.call-start = ((), (), s32[]{:S(2)}) async-start(), calls=%async_computation.3 | async-start | bytes 5971968 | tf_op jit(solution)/shard_map/all_gather | solution.py:92
  150.9 376.1 %all-gather.19.cloned.1.call-start = ((), (), s32[]{:S(2)}) async-start(), calls=%async_computation.5 | async-start | bytes 5971968 | tf_op jit(solution)/shard_map/all_gather | solution.py:92
  237.8 72.4 %collective-permute-start.10 = (bf16[2,2,288,1152]{3,2,1,0:T(8,128)(2,1)}, bf16[2,2,288,1152]{3,2,1,0:T(8,128)(2,1)}, u32[]{:S(2)}, u32[]{:S(2)}) collective-permute-start(bf16[2,2,288,1152]{3,2,1,0:T(8,128)(2,1)} %get-tuple-element.322), channel_id=1, source_target_pairs={{0,1},{1,0},{2,3},{3,2},{4,5},{5,4},{6,7},{7,6},{8,9},{9,8},{10,11... | collective-permute-start | bytes 7962632 | tf_op jit(solution)/shard_map/ppermute | solution.py:43
  314.1 57.5 %collective-permute-start.12 = (bf16[2,288,1152]{2,1,0:T(8,128)(2,1)}, bf16[2,288,1152]{2,1,0:T(8,128)(2,1)}, u32[]{:S(2)}, u32[]{:S(2)}) collective-permute-start(bf16[2,288,1152]{2,1,0:T(8,128)(2,1)} %get-tuple-element.330), channel_id=1, source_target_pairs={{0,8},{8,0},{1,9},{9,1},{2,10},{10,2},{3,11},{11,3},{4,12},{12,4},... | collective-permute-start | bytes 3981320 | tf_op jit(solution)/shard_map/ppermute | solution.py:43
  315.4 60.5 %collective-permute-start.15 = (bf16[2,2,72,4608]{3,2,1,0:T(8,128)(2,1)}, bf16[2,2,72,4608]{3,2,1,0:T(8,128)(2,1)}, u32[]{:S(2)}, u32[]{:S(2)}) collective-permute-start(bf16[2,2,72,4608]{3,2,1,0:T(8,128)(2,1)} %get-tuple-element.320), channel_id=1, source_target_pairs={{0,1},{1,0},{2,3},{3,2},{4,5},{5,4},{6,7},{7,6},{8,9},{9,8},{10,11... | collective-permute-start | bytes 7962632 | tf_op jit(solution)/shard_map/ppermute | solution.py:43
  379.8 51.5 %collective-permute-start.17 = (bf16[2,72,4608]{2,1,0:T(8,128)(2,1)}, bf16[2,72,4608]{2,1,0:T(8,128)(2,1)}, u32[]{:S(2)}, u32[]{:S(2)}) collective-permute-start(bf16[2,72,4608]{2,1,0:T(8,128)(2,1)} %get-tuple-element.328), channel_id=1, source_target_pairs={{0,8},{8,0},{1,9},{9,1},{2,10},{10,2},{3,11},{11,3},{4,12},{12,4},... | collective-permute-start | bytes 3981320 | tf_op jit(solution)/shard_map/ppermute | solution.py:43
  380.5 90.4 %collective-permute-start.26 = (bf16[2,2,72,4608]{3,2,1,0:T(8,128)(2,1)}, bf16[2,2,72,4608]{3,2,1,0:T(8,128)(2,1)}, u32[]{:S(2)}, u32[]{:S(2)}) collective-permute-start(bf16[2,2,72,4608]{3,2,1,0:T(8,128)(2,1)} %get-tuple-element.318), channel_id=1, source_target_pairs={{0,1},{1,0},{2,3},{3,2},{4,5},{5,4},{6,7},{7,6},{8,9},{9,8},{10,11... | collective-permute-start | bytes 7962632 | tf_op jit(solution)/shard_map/ppermute | solution.py:43
  396.2 39.4 %collective-permute-start.16 = (f32[1,12672]{1,0:T(1,128)}, f32[1,12672]{1,0:T(1,128)}, u32[]{:S(2)}, u32[]{:S(2)}) collective-permute-start(f32[1,12672]{1,0:T(1,128)} %add.310), channel_id=1, source_target_pairs={{0,2},{2,0},{1,3},{3,1},{4,6},{6,4},{5,7},{7,5},{8,10},{10,8},{9,1... | collective-permute-start | bytes 152072 | tf_op jit(solution)/shard_map/ppermute | solution.py:43
  437.0 37.4 %collective-permute-start.25 = (f32[1,12672]{1,0:T(1,128)}, f32[1,12672]{1,0:T(1,128)}, u32[]{:S(2)}, u32[]{:S(2)}) collective-permute-start(f32[1,12672]{1,0:T(1,128)} %add.315), channel_id=1, source_target_pairs={{0,8},{8,0},{1,9},{9,1},{2,10},{10,2},{3,11},{11,3},{4,12},{12,4},... | collective-permute-start | bytes 152072 | tf_op jit(solution)/shard_map/ppermute | solution.py:43
  437.1 180.6 %all-gather.17.cloned.1.call-start = ((), (), s32[]{:S(2)}) async-start(), calls=%async_computation.4 | async-start | bytes 5971968 | tf_op jit(solution)/shard_map/all_gather | solution.py:92
  496.4 171.4 %all-gather.23.cloned.1.call-start = ((), (), s32[]{:S(2)}) async-start(), calls=%async_computation.7 | async-start | bytes 5971968 | tf_op jit(solution)/shard_map/all_gather | solution.py:92
  498.0 52.2 %collective-permute-start.30 = (bf16[2,72,4608]{2,1,0:T(8,128)(2,1)}, bf16[2,72,4608]{2,1,0:T(8,128)(2,1)}, u32[]{:S(2)}, u32[]{:S(2)}) collective-permute-start(bf16[2,72,4608]{2,1,0:T(8,128)(2,1)} %get-tuple-element.324), channel_id=1, source_target_pairs={{0,8},{8,0},{1,9},{9,1},{2,10},{10,2},{3,11},{11,3},{4,12},{12,4},... | collective-permute-start | bytes 3981320 | tf_op jit(solution)/shard_map/ppermute | solution.py:43
  597.5 78.1 %all-gather.21.cloned.1.call-start = ((), (), s32[]{:S(2)}) async-start(), calls=%async_computation.6 | async-start | bytes 2985984 | tf_op jit(solution)/shard_map/all_gather | solution.py:92
  611.9 41.8 %collective-permute-start.22 = (bf16[7,128,576]{1,2,0:T(8,128)(2,1)}, bf16[7,128,576]{1,2,0:T(8,128)(2,1)}, u32[]{:S(2)}, u32[]{:S(2)}) collective-permute-start(bf16[7,128,576]{1,2,0:T(8,128)(2,1)} %copy.35), channel_id=1, source_target_pairs={{0,1},{1,0},{2,3},{3,2},{4,5},{5,4},{6,7},{7,6},{8,9},{9,8},{10,11... | collective-permute-start | bytes 3096584 | tf_op jit(solution)/shard_map/ppermute | solution.py:43
  613.4 51.3 %collective-permute-start.21 = (bf16[7,64,1152]{2,1,0:T(8,128)(2,1)S(1)}, bf16[7,64,1152]{2,1,0:T(8,128)(2,1)}, u32[]{:S(2)}, u32[]{:S(2)}) collective-permute-start(bf16[7,64,1152]{2,1,0:T(8,128)(2,1)S(1)} %copy-done.21), channel_id=1, source_target_pairs={{0,1},{1,0},{2,3},{3,2},{4,5},{5,4},{6,7},{7,6},{8,9},{9,8},{10,11... | collective-permute-start | bytes 3096584 | tf_op jit(solution)/shard_map/ppermute | solution.py:216
  (58 other events, 912.1 us)
Sparse Core Ops, SparseCore 0:
  20.1 24.5 all-gather.8
  89.7 35.0 all-gather.10
  126.5 33.8 all-gather.12
  161.9 33.8 all-gather.14
  437.2 38.4 all-gather.18
  496.5 53.0 all-gather.16
  597.7 33.7 all-gather.22
  633.0 21.9 all-gather.20

commit v4 on v3

--- a/solution.py
+++ b/solution.py
@@ -73,12 +73,6 @@
     return lax.axis_size("seq") == 2 and lax.axis_size("w") == 2
 
 
-def added(parts):
-    if len(parts) == 1:
-        return parts[0]
-    return (parts[0].astype(F32) + parts[1].astype(F32)).astype(BF16)
-
-
 def block(array, index, axis):
     return lax.dynamic_index_in_dim(array, index, axis, keepdims=False)
 
@@ -93,8 +87,9 @@
 
 
 class Reduction:
-    def __init__(self, chain, name, lefts, rights):
-        self.chain = chain
+    def __init__(self, chain, name, lefts, rights, lanes=1):
+        self.chain, self.lanes = chain, lanes
+        self.cuts = [right.shape[1] for right in rights]
         if fast_mesh():
             core = lax.axis_index("c").reshape(1)
             count = len(lefts)
@@ -103,50 +98,58 @@
                 *lefts,
                 *rights,
             )
-            shape = (2, 2, 2) + sent.shape[1:]
-            self.parts = (keep.reshape(shape), flip(sent.reshape(shape), "c"))
-            self.names = ["seq", "z", "x", "w", None]
+            self.parts = [(keep, flip(sent, "c"))] * lanes
+            self.names = [["seq", "x", "z", "w"] for _ in range(lanes)]
         else:
             axis = int(len(rights) > 1)
             pairs = zip(lefts, rights) if axis else ((a, rights[0]) for a in lefts)
             grad = jnp.concatenate([across(*p).astype(BF16) for p in pairs], axis)
             part = lax.psum_scatter(grad, "seq", scatter_dimension=0, tiled=True)
-            self.total, self.names = lax.psum(part, WIDE), []
-
-    def step(self):
-        if not self.names:
+            self.total, self.names = lax.psum(part, WIDE), None
+
+    def step(self, lane=0):
+        if self.names is None:
             return
-        name = self.names.pop(0)
-        parts = self.chain.enter(*self.parts)
-        if name is None:
-            self.total = share(self.chain.leave(added(parts)))
-        elif name == "w":
-            sent = self.chain.leave(added(parts))
-            self.parts = (sent, flip(sent, name))
+        if not self.names[lane]:
+            self.join()
+            return
+        name, parts = self.names[lane].pop(0), self.parts[lane]
+        if name == "w":
+            sent = self.chain.run(
+                lambda *a: add(*(part.reshape(part.shape[1:]) for part in a)), *parts
+            )
+            self.parts[lane] = (sent, flip(sent, name))
         else:
-            index = lax.axis_index(name)
-            sent = added([block(part, 1 - index, 0) for part in parts])
-            keep = added([block(part, index, 0) for part in parts])
-            sent, keep = self.chain.leave(sent, keep)
-            self.parts = (keep, flip(sent, name))
+            outer = 2 if name == "x" else 1
+            lanes = self.lanes if name == "seq" else 1
+            sent, keep = self.chain.run(
+                functools.partial(fold, name, outer, lane if lanes > 1 else 0, lanes),
+                *parts,
+            )
+            self.parts[lane] = (keep, flip(sent, name))
+
+    def join(self):
+        if self.names is None:
+            return
+        assert not any(self.names)
+        parts = [part for pair in self.parts for part in pair]
+        self.total = share(self.chain.run(add, *parts))
 
     def finish(self):
-        assert not self.names
-        return self.chain.run(lambda a: a.astype(F32), self.total)
-
-
-def gather_vectors(vectors):
-    joined = jnp.concatenate(vectors)
-    count = joined.shape[0]
+        return self.chain.run(functools.partial(widen, self.cuts), self.total)
+
+
+def gather_vectors(chain, vectors):
+    joined = chain.run(lambda *a: jnp.concatenate(a), *vectors)
+    mine = joined.reshape(1, -1)
     if fast_mesh():
-        mine = joined.reshape(1, count)
         everything = ordered(mine, flip(mine, "seq"), lax.axis_index("seq"))
     else:
-        everything = lax.all_gather(joined.reshape(1, count), "seq", axis=0, tiled=True)
+        everything = lax.all_gather(mine, "seq", axis=0, tiled=True)
     out, start = [], 0
     for vector in vectors:
         size = vector.shape[0]
-        out.append(everything[:, start : start + size].reshape(-1).astype(F32))
+        out.append(everything[:, start : start + size].reshape(1, -1).astype(F32))
         start += size
     return out
 
@@ -155,7 +158,7 @@
     def __init__(self, chain, vectors):
         self.chain, self.sizes = chain, [vector.shape[1] for vector in vectors]
         self.total = chain.run(lambda *a: jnp.concatenate(a, 1), *vectors)
-        self.names = ["seq", "c", "z", "x", "w"]
+        self.names = ["c", "x", "z", "w", "seq"]
         if fast_mesh():
             self.got = flip(self.total, self.names.pop(0))
         else:
@@ -163,7 +166,7 @@
 
     def step(self):
         if fast_mesh():
-            self.total = self.chain.run(jnp.add, self.total, self.got)
+            self.total = self.chain.run(add, self.total, self.got)
             if self.names:
                 self.got = flip(self.total, self.names.pop(0))
 
@@ -179,17 +182,30 @@
         return out
 
 
-def start_items(array, per):
+def split_items(array, per):
     ways, side = lax.axis_size("seq"), lax.axis_index("seq")
     padding = [(0, per * ways - array.shape[0])] + [(0, 0)] * (array.ndim - 1)
     array = jnp.pad(array, padding)
-    pieces = [pick(array, side, per)]
-    for hop in range(1, ways):
-        piece = pick(array, (side + hop) % ways, per)
-        pieces.append(
-            lax.ppermute(piece, "seq", [(i, (i + hop) % ways) for i in range(ways)])
-        )
-    return tuple(pieces)
+    return tuple(pick(array, (side + hop) % ways, per) for hop in range(ways))
+
+
+def split_parts(whole, axis):
+    ways, side = lax.axis_size("seq"), lax.axis_index("seq")
+    size = whole.shape[axis] // ways
+    return tuple(pick(whole, (side + hop) % ways, size, axis) for hop in range(ways))
+
+
+def swap_pieces(pieces):
+    ways = lax.axis_size("seq")
+    return pieces[:1] + tuple(
+        lax.ppermute(piece, "seq", [(i, (i + hop) % ways) for i in range(ways)])
+        for hop, piece in enumerate(pieces)
+        if hop
+    )
+
+
+def start_items(array, per):
+    return swap_pieces(split_items(array, per))
 
 
 def joined_pieces(pieces, axis):
@@ -206,39 +222,30 @@
     return whole
 
 
-def return_items(whole, axis):
-    ways, side = lax.axis_size("seq"), lax.axis_index("seq")
-    size = whole.shape[axis] // ways
-    pieces = [pick(whole, side, size, axis)]
-    for hop in range(1, ways):
-        piece = pick(whole, (side + hop) % ways, size, axis)
-        pieces.append(
-            lax.ppermute(piece, "seq", [(i, (i + hop) % ways) for i in range(ways)])
-        )
-    return tuple(pieces)
-
-
 HINT = pl.CostEstimate(flops=10**13, transcendentals=0, bytes_accessed=10**9)
 
 
-def block_loader(parts, offset, blocks, side, sems):
-    count, size, _ = blocks.shape
+def block_loader(parts, offset, blocks, base, count, side, sems):
+    size = blocks.shape[1]
     rows, columns = parts[0].shape
     first = pl.program_id(0) == 0
     copies = []
     for b in range(count):
         copies.append([])
+        target = base + b
         if len(parts) == 1:
             row, column = divmod(b, columns // size)
             source = parts[0].at[pl.ds(row * size, size), pl.ds(column * size, size)]
-            copy = pltpu.make_async_copy(source, blocks.at[b], sems.at[0, b])
+            copy = pltpu.make_async_copy(source, blocks.at[target], sems.at[0, target])
             copies[b].append((first, copy))
         elif rows >= size:
             half, place = divmod(b, rows // size)
             for p, part in enumerate(parts):
                 mine = side == half if p == 0 else side != half
                 source = part.at[pl.ds(place * size, size), :]
-                copy = pltpu.make_async_copy(source, blocks.at[b], sems.at[0, b])
+                copy = pltpu.make_async_copy(
+                    source, blocks.at[target], sems.at[0, target]
+                )
                 copies[b].append((jnp.logical_and(first, mine), copy))
         else:
             for p, part in enumerate(parts):
@@ -246,26 +253,22 @@
                 column = (b + (offset if p else 0)) * size
                 copy = pltpu.make_async_copy(
                     part.at[:, pl.ds(column, size)],
-                    blocks.at[b, pl.ds(start, rows), :],
-                    sems.at[p, b],
+                    blocks.at[target, pl.ds(start, rows), :],
+                    sems.at[p, target],
                 )
                 copies[b].append((first, copy))
     for pair in copies:
         for when, copy in pair:
             pl.when(when)(copy.start)
-
-    def wait(b):
-        for when, copy in copies[b]:
-            pl.when(when)(copy.wait)
-
-    return wait
-
-
-def dense(name, body, rows_in, vectors, weight, outs, sums=(), steps=2):
+    return copies
+
+
+def dense(name, body, rows_in, vectors, weights, outs, sums=(), steps=2):
     rows = rows_in[0].shape[0]
     tile = rows // steps
-    count, offset, parts = weight
-    cuts = [len(rows_in), len(vectors), len(parts), len(outs), len(sums)]
+    total = sum(count for count, _, _ in weights)
+    arrays = [part for _, _, parts in weights for part in parts]
+    cuts = [len(rows_in), len(vectors), len(arrays), len(outs), len(sums)]
 
     def kernel(side, *refs):
         groups = []
@@ -273,7 +276,17 @@
             groups.append(refs[:size])
             refs = refs[size:]
         blocks, sems = refs
-        wait = block_loader(groups[2], offset, blocks, side[0], sems)
+        copies, parts = [], groups[2]
+        for count, offset, used in weights:
+            copies += block_loader(
+                parts[: len(used)], offset, blocks, len(copies), count, side[0], sems
+            )
+            parts = parts[len(used) :]
+
+        def wait(b):
+            for when, copy in copies[b]:
+                pl.when(when)(copy.wait)
+
         if sums:
 
             @pl.when(pl.program_id(0) == 0)
@@ -294,18 +307,123 @@
                 pl.BlockSpec((tile, a.shape[1]), lambda i, _: (i, 0)) for a in rows_in
             ]
             + [pl.BlockSpec(a.shape, lambda i, _: (0, 0)) for a in vectors]
-            + [pl.BlockSpec(memory_space=pl.ANY) for _ in parts],
+            + [pl.BlockSpec(memory_space=pl.ANY) for _ in arrays],
             out_specs=tuple(pl.BlockSpec((tile, c), lambda i, _: (i, 0)) for c, _ in outs)
             + tuple(pl.BlockSpec((1, c), lambda i, _: (0, 0)) for c in sums),
             scratch_shapes=[
-                pltpu.VMEM((count, WIDTH, WIDTH), BF16),
-                pltpu.SemaphoreType.DMA((2, count)),
+                pltpu.VMEM((total, WIDTH, WIDTH), BF16),
+                pltpu.SemaphoreType.DMA((2, total)),
             ],
         ),
         compiler_params=pltpu.CompilerParams(vmem_limit_bytes=60 << 20),
         cost_estimate=HINT,
         name=name,
-    )(lax.axis_index("seq").reshape(1), *rows_in, *vectors, *parts)
+    )(lax.axis_index("seq").reshape(1), *rows_in, *vectors, *arrays)
+
+
+def fold_kernel(index_ref, *refs):
+    (*parts, sent, keep) = refs
+    index = index_ref[0]
+
+    def total(place):
+        values = [part[0, place].astype(F32) for part in parts]
+        return sum(values[1:], values[0]).astype(BF16)
+
+    sent[0] = total(1 - index)
+    keep[0] = total(index)
+
+
+def fold(name, outer, lane, lanes, *parts):
+    index = lax.axis_index(name).reshape(1)
+    count, unit, columns = parts[0].shape
+    inner = count // (2 * outer)
+    size = columns // lanes
+    half = jax.ShapeDtypeStruct((outer, inner, unit, size), BF16)
+    out = pl.pallas_call(
+        fold_kernel,
+        out_shape=(half, half),
+        grid_spec=pltpu.PrefetchScalarGridSpec(
+            num_scalar_prefetch=1,
+            grid=(outer, inner),
+            in_specs=[
+                pl.BlockSpec((1, 2, 1, unit, size), lambda i, j, _: (i, 0, j, 0, lane))
+                for _ in parts
+            ],
+            out_specs=(
+                pl.BlockSpec((1, 1, unit, size), lambda i, j, _: (i, j, 0, 0)),
+            )
+            * 2,
+        ),
+        compiler_params=pltpu.CompilerParams(vmem_limit_bytes=60 << 20),
+        cost_estimate=HINT,
+        name="fold_" + name,
+    )(index, *(part.reshape(outer, 2, inner, unit, columns) for part in parts))
+    return tuple(part.reshape(count // 2, unit, size) for part in out)
+
+
+def add_kernel(*refs):
+    (*parts, out) = refs
+    size = parts[0].shape[1]
+    for k in range(len(parts) // 2):
+        total = parts[2 * k][...].astype(F32) + parts[2 * k + 1][...].astype(F32)
+        out[:, k * size : (k + 1) * size] = total.astype(out.dtype)
+
+
+def add(*parts):
+    rows, columns = parts[0].shape
+    return pl.pallas_call(
+        add_kernel,
+        out_shape=jax.ShapeDtypeStruct((rows, columns * len(parts) // 2), parts[0].dtype),
+        compiler_params=pltpu.CompilerParams(vmem_limit_bytes=60 << 20),
+        cost_estimate=HINT,
+        name="add",
+    )(*parts)
+
+
+def widen_kernel(value, *outs):
+    start = 0
+    for out in outs:
+        out[...] = value[:, start : start + out.shape[1]].astype(F32)
+        start += out.shape[1]
+
+
+def widen(cuts, value):
+    rows, columns = value.shape
+    steps = 4 if rows % 32 == 0 else 2
+    return pl.pallas_call(
+        widen_kernel,
+        out_shape=tuple(jax.ShapeDtypeStruct((rows, size), F32) for size in cuts),
+        grid=(steps,),
+        in_specs=[pl.BlockSpec((rows // steps, columns), lambda i: (i, 0))],
+        out_specs=tuple(
+            pl.BlockSpec((rows // steps, size), lambda i: (i, 0)) for size in cuts
+        ),
+        compiler_params=pltpu.CompilerParams(vmem_limit_bytes=60 << 20),
+        cost_estimate=HINT,
+        name="widen",
+    )(value)
+
+
+def eighth_copy_kernel(place, shard, out):
+    out[...] = shard[...]
+
+
+def eighth_copy(shard):
+    rows, columns = shard.shape[0] // 8, shard.shape[1]
+    place = lax.axis_index("z") * 4 + lax.axis_index("x") * 2 + lax.axis_index("c")
+    return pl.pallas_call(
+        eighth_copy_kernel,
+        out_shape=jax.ShapeDtypeStruct((rows, columns), BF16),
+        grid_spec=pltpu.PrefetchScalarGridSpec(
+            num_scalar_prefetch=1,
+            grid=(1,),
+            in_specs=[pl.BlockSpec((rows, columns), lambda i, place: (place[0], 0))],
+            out_specs=pl.BlockSpec((rows, columns), lambda i, place: (0, 0)),
+        ),
+        compiler_params=pltpu.CompilerParams(vmem_limit_bytes=60 << 20),
+        cost_estimate=HINT,
+        name="eighth",
+    )(place.reshape(1), shard)
 
 
 def normalize(hidden):
@@ -323,40 +441,32 @@
     return slice(b * WIDTH, (b + 1) * WIDTH)
 
 
-def base_body(wait, blocks, rows, vectors, outs, sums):
+def base_inward_body(wait, blocks, rows, vectors, outs, sums):
     wait(0)
     total = simple(rows[0][...], blocks[0])
     wait(1)
     total = total + simple(rows[1][...], blocks[1]) + vectors[0][...]
     outs[0][...] = total
-    outs[1][...] = (normalize(total)[0] * vectors[1][...] + vectors[2][...]).astype(
-        BF16
-    )
-
-
-def wide_body(wait, blocks, rows, vectors, outs, sums):
-    for b in range(blocks.shape[0]):
-        wait(b)
-        outs[0][:, columns_of(b)] = simple(rows[0][...], blocks[b]).astype(BF16)
-
-
-def middle_body(wait, blocks, rows, vectors, outs, sums):
+    normed = (normalize(total)[0] * vectors[1][...] + vectors[2][...]).astype(BF16)
+    outs[1][...] = normed
+    for b in range(3):
+        wait(2 + b)
+        outs[2][:, columns_of(b)] = simple(outs[1][...], blocks[2 + b]).astype(BF16)
+
+
+def middle_expand_body(wait, blocks, rows, vectors, outs, sums):
     wait(0)
     total = simple(rows[0][...], blocks[0]) + rows[1][...] + vectors[0][...]
     outs[0][...] = total
-    outs[1][...] = (normalize(total)[0] * vectors[1][...] + vectors[2][...]).astype(
-        BF16
-    )
-
-
-def expand_body(wait, blocks, rows, vectors, outs, sums):
-    for b in range(blocks.shape[0]):
-        wait(b)
-        upper = simple(rows[0][...], blocks[b]) + vectors[0][:, columns_of(b)]
+    normed = (normalize(total)[0] * vectors[1][...] + vectors[2][...]).astype(BF16)
+    outs[1][...] = normed
+    for b in range(4):
+        wait(1 + b)
+        upper = simple(outs[1][...], blocks[1 + b]) + vectors[3][:, columns_of(b)]
         below = 0.5 * (1.0 + lax.erf(upper * 0.7071067811865476))
         bell = jnp.exp(-0.5 * upper * upper) * 0.3989422804014327
-        outs[0][:, columns_of(b)] = (upper * below).astype(BF16)
-        outs[1][:, columns_of(b)] = (below + upper * bell).astype(BF16)
+        outs[2][:, columns_of(b)] = (upper * below).astype(BF16)
+        outs[3][:, columns_of(b)] = (below + upper * bell).astype(BF16)
 
 
 def contract_body(wait, blocks, rows, vectors, outs, sums):
@@ -378,9 +488,9 @@
         add_sum(sums[0].at[:, columns_of(b)], upper.astype(F32))
 
 
-def norm_back_body(wait, blocks, rows, vectors, outs, sums):
+def norm_back_body(count, wait, blocks, rows, vectors, outs, sums):
     grad = None
-    for b in range(blocks.shape[0]):
+    for b in range(count):
         wait(b)
         part = against(rows[0][:, columns_of(b)], blocks[b])
         grad = part if grad is None else grad + part
@@ -394,11 +504,13 @@
     total = rows[2][...].astype(F32) + back
     rounded = total.astype(BF16)
     outs[0][...] = rounded
-    if len(outs) > 1:
-        outs[1][...] = total
     add_sum(sums[0], grad * xhat)
     add_sum(sums[1], grad)
     add_sum(sums[2], rounded.astype(F32))
+    if len(outs) > 1:
+        outs[1][...] = total
+        wait(count)
+        outs[2][...] = against(outs[0][...], blocks[count]).astype(BF16)
 
 
 def against_body(wait, blocks, rows, vectors, outs, sums):
@@ -428,15 +540,13 @@
         sent, keep = refs[count + len(rights) :]
 
         def run(left_ref, right_ref):
-            grad = across(left_ref[...], right_ref[...]).astype(BF16)
-            for mine in range(2):
-
-                @pl.when(core_ref[0] == mine)
-                def _():
-                    for j in range(per):
-                        own, other = 2 * j + mine, 2 * j + 1 - mine
-                        keep[j] = grad[own * unit : (own + 1) * unit]
-                        sent[j] = grad[other * unit : (other + 1) * unit]
+            grad = across(left_ref[...], right_ref[...])
+            second = core_ref[0] == 1
+            for j in range(0, 2 * per, 2):
+                even = grad[j * unit : (j + 1) * unit].astype(BF16)
+                odd = grad[(j + 1) * unit : (j + 2) * unit].astype(BF16)
+                keep[j // 2] = jnp.where(second, odd, even)
+                sent[j // 2] = jnp.where(second, even, odd)
 
         if count == 1:
             run(left[0], right[0])
@@ -557,7 +667,7 @@
                 pl.BlockSpec((heads * slots, slots), lambda i, _: (i, 0)),
             ),
         ),
-        compiler_params=pltpu.CompilerParams(vmem_limit_bytes=56 << 20),
+        compiler_params=pltpu.CompilerParams(vmem_limit_bytes=60 << 20),
         cost_estimate=HINT,
         name="attend",
     )(lengths, qkv)
@@ -610,7 +720,7 @@
             pl.BlockSpec((slots, width), lambda i: (i, 0)),
         ],
         out_specs=pl.BlockSpec((slots, 3 * width), lambda i: (i, 0)),
-        compiler_params=pltpu.CompilerParams(vmem_limit_bytes=56 << 20),
+        compiler_params=pltpu.CompilerParams(vmem_limit_bytes=60 << 20),
         cost_estimate=HINT,
         name="attend_back",
     )(qkv, probs, grad_mixed)
@@ -646,33 +756,18 @@
     live = jnp.pad(lengths, (0, per * ways - items), constant_values=slots)
     live = pick(live, side, per)
 
-    (
-        skip_offset,
-        gain_first,
-        shift_first,
-        outward_offset,
-        gain_second,
-        shift_second,
-        expand_offset,
-        contract_offset,
-    ) = (
-        vector.reshape(1, -1)
-        for vector in gather_vectors(
-            (
-                skip_bias,
-                first_gain,
-                first_shift,
-                outward_bias,
-                second_gain,
-                second_shift,
-                expand_bias,
-                contract_bias,
-            )
-        )
+    small = (
+        skip_bias,
+        first_gain,
+        first_shift,
+        outward_bias,
+        second_gain,
+        second_shift,
+        expand_bias,
+        contract_bias,
     )
     if fast:
         skip_piece = flip(chain.run(eighth, skip_weight), "seq")
-        skip_parts = (skip_weight, share(skip_piece))
         attention_piece = flip(
             chain.run(
                 lambda a, b: jnp.concatenate([eighth(a), eighth(b)], 1),
@@ -681,22 +776,25 @@
             ),
             "seq",
         )
-        attention_other = share(attention_piece)
+        vectors = gather_vectors(chain, small)
+        expand_piece = flip(chain.run(eighth, expand_weight), "seq")
+        skip_pieces = chain.run(lambda a: start_items(a, per), skip_store)
+        latent_pieces = chain.run(lambda a: start_items(a, per), latents)
+        skip_parts = (skip_weight, share(*chain.enter(skip_piece)))
+        attention_other = share(*chain.enter(attention_piece))
         inward_parts = (inward_weight, attention_other)
         outward_parts = (outward_weight, attention_other)
-        skip_pieces = chain.run(lambda a: start_items(a, per), skip_store)
-        latent_pieces = chain.run(lambda a: start_items(a, per), latents)
-        skip_rows, latent_rows = chain.run(
-            lambda a, b: (
-                joined_pieces(a, 2).reshape(rows, width),
-                joined_pieces(b, 1).reshape(rows, width),
-            ),
-            skip_pieces,
-            latent_pieces,
+        grad_pieces = chain.run(lambda a: split_items(a, per), cotangent)
+        skip_rows = chain.run(
+            lambda *a: joined_pieces(a, 2).reshape(rows, width), *skip_pieces
         )
-        expand_piece = flip(chain.run(eighth, expand_weight), "seq")
-        contract_piece = flip(chain.run(eighth, contract_weight), "seq")
-        grad_pieces = chain.run(lambda a: start_items(a, per), cotangent)
+        expand_parts = (expand_weight, share(*chain.enter(expand_piece)))
+        contract_piece = chain.run(eighth_copy, contract_weight)
+        latent_rows = chain.run(
+            lambda *a: joined_pieces(a, 1).reshape(rows, width), *latent_pieces
+        )
+        contract_piece = flip(*chain.enter(contract_piece), "seq")
+        grad_pieces = swap_pieces(chain.enter(*grad_pieces))
     else:
         skip_parts, inward_parts, outward_parts, expand_parts, contract_parts = (
             (lax.all_gather(shard, "seq", axis=0, tiled=True),)
@@ -711,53 +809,54 @@
         skip_rows = joined_pieces(start_items(skip_store, per), 2)
         latent_rows = joined_pieces(start_items(latents, per), 1)
         grad_pieces = start_items(cotangent, per)
+        vectors = gather_vectors(chain, small)
+    (
+        skip_offset,
+        gain_first,
+        shift_first,
+        outward_offset,
+        gain_second,
+        shift_second,
+        expand_offset,
+        contract_offset,
+    ) = vectors
     skip_matrix, inward_matrix = (2, 0, skip_parts), (3, 0, inward_parts)
     outward_matrix = (1, 3, outward_parts)
     skip_rows, latent_rows = (a.reshape(rows, width) for a in (skip_rows, latent_rows))
-    one, both = [(width, BF16)], [(width, F32), (width, BF16)]
-
-    base, first_normed = chain.run(
-        lambda a, b, *w: dense(
-            "base",
-            base_body,
-            (a, b),
+    one, wide = (width, BF16), (width, F32)
+    hidden = (expand_offset.shape[1], BF16)
+
+    base, first_normed, qkv_vals = chain.run(
+        lambda *a: dense(
+            "base_inward",
+            base_inward_body,
+            a,
             (skip_offset, gain_first, shift_first),
-            (2, 0, w),
-            both,
+            (skip_matrix, inward_matrix),
+            [wide, one, (3 * width, BF16)],
         ),
         latent_rows,
         skip_rows,
-        *skip_parts,
-    )
-    if fast:
-        expand_parts = (expand_weight, share(*chain.enter(expand_piece)))
-    (qkv_vals,) = chain.run(
-        lambda a: dense("inward", wide_body, (a,), (), inward_matrix, [(3 * width, BF16)]),
-        first_normed,
-    )
+    )
+    mixed_rows, probs = chain.run(lambda a: attend(a, live), qkv_vals)
     if fast:
         contract_parts = (contract_weight, share(*chain.enter(contract_piece)))
     expand_matrix, contract_matrix = (4, 0, expand_parts), (4, 0, contract_parts)
-    mixed_rows, probs = chain.run(lambda a: attend(a, live), qkv_vals)
-    middle, second_normed = dense(
-        "middle",
-        middle_body,
-        (mixed_rows, base),
-        (outward_offset, gain_second, shift_second),
-        outward_matrix,
-        both,
-    )
-    activated, slope = dense(
-        "expand",
-        expand_body,
-        (second_normed,),
-        (expand_offset,),
-        expand_matrix,
-        [(expand_offset.shape[1], BF16)] * 2,
-    )
-    chain.leave(activated)
     grad_out = chain.run(
         lambda *a: joined_pieces(a, 1).reshape(rows, width), *grad_pieces
+    )
+    middle, second_normed, activated, slope = chain.run(
+        lambda *a: dense(
+            "middle_expand",
+            middle_expand_body,
+            a,
+            (outward_offset, gain_second, shift_second, expand_offset),
+            (outward_matrix, expand_matrix),
+            [wide, one, hidden, hidden],
+            steps=4,
+        ),
+        mixed_rows,
+        base,
     )
     contract_sum = Reduction(chain, "contract_grad", (activated,), (grad_out,))
     grad_upper, grad_expand_off, grad_contract_off = chain.run(
@@ -766,23 +865,30 @@
             upper_back_body,
             a,
             (),
-            contract_matrix,
-            [(expand_offset.shape[1], BF16)],
-            [expand_offset.shape[1], width],
+            (contract_matrix,),
+            [hidden],
+            [hidden[0], width],
         ),
         grad_out,
         slope,
     )
     contract_sum.step()
     expand_sum = Reduction(chain, "expand_grad", (second_normed,), (grad_upper,))
-    grad_branch, grad_middle, grad_gain_two, grad_shift_two, grad_outward_off = chain.run(
+    (
+        grad_branch,
+        grad_middle,
+        grad_mixed,
+        grad_gain_two,
+        grad_shift_two,
+        grad_outward_off,
+    ) = chain.run(
         lambda *a: dense(
             "middle_back",
-            norm_back_body,
+            functools.partial(norm_back_body, 4),
             a,
             (gain_second,),
-            expand_matrix,
-            both[::-1],
+            (expand_matrix, outward_matrix),
+            [one, wide, one],
             [width] * 3,
         ),
         grad_upper,
@@ -790,27 +896,40 @@
         grad_out,
     )
     expand_sum.step()
-    (grad_mixed,) = chain.run(
-        lambda a: dense("mixed_back", against_body, (a,), (), outward_matrix, one),
-        grad_branch,
-    )
-    grad_qkv = attend_back(qkv_vals, probs, grad_mixed, per)
-    chain.leave(grad_qkv)
     contract_sum.step()
+    grad_qkv = chain.run(lambda a: attend_back(qkv_vals, probs, a, per), grad_mixed)
     attention_sum = Reduction(
         chain,
         "attention_grad",
         (first_normed, mixed_rows),
         (grad_qkv, grad_branch),
-    )
+        lanes=2,
+    )
+    contract_sum.step()
     grad_base, grad_gain_one, grad_shift_one, grad_skip_off = chain.run(
         lambda *a: dense(
-            "base_back", norm_back_body, a, (gain_first,), inward_matrix, one, [width] * 3
+            "base_back",
+            functools.partial(norm_back_body, 3),
+            a,
+            (gain_first,),
+            (inward_matrix,),
+            [one],
+            [width] * 3,
         ),
         grad_qkv,
         base,
         grad_middle,
     )
+    expand_sum.step()
+    contract_sum.step()
+    attention_sum.step(1)
+    attention_sum.step(0)
+    skip_sum = Reduction(chain, "skip_grad", (latent_rows, skip_rows), (grad_base,))
+    expand_sum.step()
+    skip_sum.step()
+    contract_sum.step()
+    attention_sum.step(0)
+    expand_sum.step()
     vector_sum = VectorReduction(
         chain,
         (
@@ -824,11 +943,12 @@
             grad_contract_off,
         ),
     )
-    attention_sum.step()
-    contract_sum.step()
+    attention_sum.step(0)
+    vector_sum.step()
+    attention_sum.step(1)
+    attention_sum.step(0)
     expand_sum.step()
-    skip_sum = Reduction(chain, "skip_grad", (latent_rows, skip_rows), (grad_base,))
-    contract_sum.step()
+    attention_sum.step(1)
     vector_sum.step()
     halves = ways == 2
     columns = [width] + ([width // 2] * 2 if halves else [width])
@@ -838,60 +958,59 @@
             against_body,
             (a,),
             (),
-            skip_matrix,
+            (skip_matrix,),
             [(size, BF16) for size in columns],
         ),
         grad_base,
     )
-    skip_sum.step()
-    contract_sum.step()
-    expand_sum.step()
-    vector_sum.step()
     latent_pieces = chain.run(
-        lambda a: return_items(a.reshape(per, slots, width), 1), grad_latents
+        lambda a: split_parts(a.reshape(per, slots, width), 1), grad_latents
     )
     if halves:
         skip_pieces = chain.run(
             lambda a, b: (jnp.where(side == 0, a, b), jnp.where(side == 0, b, a)),
             *grad_skip,
         )
-        skip_pieces = [a.reshape(per, slots, width // 2) for a in skip_pieces]
-        skip_pieces[1] = flip(skip_pieces[1], "seq")
+        skip_pieces = tuple(a.reshape(per, slots, width // 2) for a in skip_pieces)
     else:
-        skip_pieces = return_items(grad_skip[0].reshape(per, slots, width), 2)
+        skip_pieces = split_parts(grad_skip[0].reshape(per, slots, width), 2)
+    attention_sum.step(1)
+    skip_sum.step()
+    vector_sum.step()
+    latent_pieces = swap_pieces(chain.enter(*latent_pieces))
+    skip_pieces = swap_pieces(chain.enter(*skip_pieces))
+    (sum_contract,) = contract_sum.finish()
+    skip_sum.step()
+    vector_sum.step()
+    attention_sum.join()
+    skip_sum.step()
     (result,) = chain.run(
         lambda *a: dense(
-            "contract", contract_body, a, (contract_offset,), contract_matrix, one
+            "contract",
+            contract_body,
+            a,
+            (contract_offset,),
+            (contract_matrix,),
+            [one],
+            steps=4,
         ),
         activated,
         middle,
     )
-    expand_sum.step()
-    output_pieces = chain.run(
-        lambda a: return_items(a.reshape(per, slots, width), 1), result
-    )
-    attention_sum.step()
-    vector_sum.step()
-    expand_sum.step()
-    vector_sum.step()
-    skip_sum.step()
-    sum_contract = contract_sum.finish()
-    attention_sum.step()
-    vector_sum.step()
-    attention_sum.step()
-    skip_sum.step()
-    skip_sum.step()
-    attention_sum.step()
-    skip_sum.step()
-    sum_expand = expand_sum.finish()
     grad_latents = chain.run(
         lambda *a: joined_pieces(a, 0)[:items].astype(F32), *latent_pieces
     )
+    skip_sum.step()
     grad_skip = chain.run(lambda *a: joined_pieces(a, 0)[:items], *skip_pieces)
+    output_pieces = chain.run(
+        lambda a: split_parts(a.reshape(per, slots, width), 1), result
+    )
+    output_pieces = swap_pieces(output_pieces)
+    (sum_expand,) = expand_sum.finish()
+    vector_sum.step()
+    sum_inward, sum_outward = attention_sum.finish()
+    (sum_skipw,) = skip_sum.finish()
     output = chain.run(lambda *a: joined_pieces(a, 0)[:items], *output_pieces)
-    sum_attention = attention_sum.finish()
-    sum_inward, sum_outward = jnp.split(sum_attention, [3 * width], 1)
-    sum_skipw = skip_sum.finish()
     (
         sum_skipb,
         sum_gain1,

time: 695 us -> 591 us (0.85)
  waiting for transfers between devices: 218 us -> 114 us
  Pallas kernels: 263 us -> 353 us
  other arithmetic: 102 us -> 22.5 us
  local copies, waits for them, and re-layouts: 49.6 us -> 37.5 us
    ppermute x31 -> x34, waiting for transfers between devices: 200 us -> 81.7 us  [flip(): return lax.ppermute(array, axis, [(0, 1), (1, 0)])]
    pallas_call x0 -> x34, Pallas kernels: none -> 111 us  [the longest x15 55.9 us: fold(): pl.pallas_call(fold_kernel, out_shape=(half, half), grid_spec=pltpu.Prefe...]
    convert_element_type x24 -> x1, other arithmetic: 75.9 us -> 0.08 us  [gather_vectors(): out.append(everything[:, start:start + size].reshape(1, -1).astype(F32))]
    pallas_call x10 -> x7, Pallas kernels: 173 us -> 157 us  [dense(): pl.pallas_call(kernel, out_shape=tuple((jax.ShapeDtypeStruct((rows, c), d...]
    ppermute x5 -> x6, waiting for transfers between devices: 16 us -> 28.8 us  [swap_pieces(): lax.ppermute(piece, 'seq', [(i, (i + hop) % ways) for i in range(ways)])]
    split x2 -> x0, local copies, waits for them, and re-layouts: 7.79 us -> none  [per_device(): sum_inward, sum_outward = jnp.split(sum_attention, [3 * width], 1)]
    dynamic_slice x11 -> x10, local copies, waits for them, and re-layouts: 16.2 us -> 14.4 us  [pick(): return lax.dynamic_slice_in_dim(array, index * size, size, axis)]
    ppermute x31 -> x34, starting transfers between devices: 34.2 us -> 35.5 us  [flip(): return lax.ppermute(array, axis, [(0, 1), (1, 0)])]
  transfers between devices with their start and end apart: 44 -> 48, of which waited for: 18 -> 12; matrix products, arithmetic and copies ran while one was open for 19% -> 9% of each run, Pallas kernels for 38% -> 59%
where the time goes in v4:
time: 591 us; the launch traced here: 584 us
  Pallas kernels  353 us (60%)
  waiting for transfers between devices  114 us (19%)
  starting transfers between devices  41 us (7%)
  local copies, waits for them, and re-layouts  37.5 us (6%)
  other arithmetic  22.5 us (4%)
  between operations  15.1 us (3%)
    pallas_call x7, Pallas kernels, dense(): pl.pallas_call(kernel, out_shape=tuple((jax.ShapeDtypeStruct((rows, c), d...  157 us
    ppermute x34, waiting for transfers between devices, flip(): return lax.ppermute(array, axis, [(0, 1), (1, 0)])  81.7 us
    pallas_call x4, Pallas kernels, core_gradients(): pl.pallas_call(kernel, out_shape=(half, half), grid_spec=pltpu.PrefetchSc...  62.2 us
    pallas_call x15, Pallas kernels, fold(): pl.pallas_call(fold_kernel, out_shape=(half, half), grid_spec=pltpu.Prefe...  55.9 us
    ppermute x34, starting transfers between devices, flip(): return lax.ppermute(array, axis, [(0, 1), (1, 0)])  35.5 us
    ppermute x6, waiting for transfers between devices, swap_pieces(): lax.ppermute(piece, 'seq', [(i, (i + hop) % ways) for i in range(ways)])  28.8 us
    pallas_call x14, Pallas kernels, add(): pl.pallas_call(add_kernel, out_shape=jax.ShapeDtypeStruct((rows, columns...  26.8 us
    pallas_call x4, Pallas kernels, widen(): pl.pallas_call(widen_kernel, out_shape=tuple((jax.ShapeDtypeStruct((rows,...  25.9 us
  transfers between devices with their start and end apart: 48, of which 12 were waited for; matrix products, arithmetic and copies ran while one was open for 9% of the time, Pallas kernels for 59%

profile of v4, /device:TPU:0, one launch (start us, length us, event | category | flops | bytes accessed | tf_op | source)
XLA Modules:
  0.0 584.0 jit_solution(2032481828765701412)
XLA Ops:
  27.4 25.3 %collective-permute-done.2 = bf16[1,6336]{1,0:T(2,128)(2,1)S(1)} collective-permute-done((bf16[1,6336]{1,0:T(2,128)(2,1)S(1)}, bf16[1,6336]{1,0:T(2,128)(2,1)S(1)}, u32[]{:S(2)}, u32[]{:S(2)}) %collective-permute-start.2) | collective-permute-done | bytes 12704 | tf_op jit(solution)/shard_map/ppermute | solution.py:43
  58.4 16.6 %collective-permute-done.1 = bf16[7,128,576]{1,2,0:T(8,128)(2,1)} collective-permute-done((bf16[7,128,576]{1,2,0:T(8,128)(2,1)}, bf16[7,128,576]{1,2,0:T(8,128)(2,1)}, u32[]{:S(2)}, u32[]{:S(2)}) %collective-permute-start.1) | collective-permute-done | bytes 1032224 | tf_op jit(solution)/shard_map/ppermute | solution.py:201
  83.5 12.2 %collective-permute-done = bf16[7,64,1152]{2,1,0:T(8,128)(2,1)} collective-permute-done((bf16[7,64,1152]{2,1,0:T(8,128)(2,1)}, bf16[7,64,1152]{2,1,0:T(8,128)(2,1)}, u32[]{:S(2)}, u32[]{:S(2)}) %collective-permute-start) | collective-permute-done | bytes 1032224 | tf_op jit(solution)/shard_map/ppermute | solution.py:201
  101.8 24.9 %base_inward.1 = (f32[896,1152]{1,0:T(8,128)}, bf16[896,1152]{1,0:T(8,128)(2,1)}, bf16[896,3456]{1,0:T(8,128)(2,1)}) custom-call(s32[1]{0:T(128)} %bitcast.side.index_ref, bf16[896,1152]{1,0:T(8,128)(2,1)} %bitcast.91, bf16[896,1152]{1,0:T(8,128)(2,1)} %maximum_select_fusion.refs_1_, f32[1,1152]{1,0:T(1,128)} %reshape.541.refs_2_, ...), custom_call_target="tpu_custom_call" | custom-call | flops 9999999827968 | bytes 1000000000 | tf_op jit(solution)/shard_map/base_inward/pallas_call | solution.py:299
  126.7 10.9 %attend.1 = (bf16[896,1152]{1,0:T(8,128)(2,1)}, bf16[14336,128]{1,0:T(8,128)(2,1)}) custom-call(s32[7]{0:T(128)} %pad_dynamic-slice_fusion.6.lengths, bf16[896,3456]{1,0:T(8,128)(2,1)} %get-tuple-element.247.qkv), custom_call_target="tpu_custom_call" | custom-call | flops 9999999827968 | bytes 1000000000 | tf_op jit(solution)/shard_map/attend/pallas_call | solution.py:655
  141.4 28.7 %middle_expand.1 = (f32[896,1152]{1,0:T(8,128)}, bf16[896,1152]{1,0:T(8,128)(2,1)}, bf16[896,4608]{1,0:T(8,128)(2,1)}, bf16[896,4608]{1,0:T(8,128)(2,1)}) custom-call(s32[1]{0:T(128)} %bitcast.side.index_ref, bf16[896,1152]{1,0:T(8,128)(2,1)} %get-tuple-element.294.refs_0_.refs_1_, f32[896,1152]{1,0:T(8,128)} %get-tuple-element.302.refs_1_, ...), custom_call_target="tpu_custom_call" | custom-call | flops 9999999827968 | bytes 1000000000 | tf_op jit(solution)/shard_map/middle_expand/pallas_call | solution.py:299
  170.1 16.7 %contract_grad.1 = (bf16[8,288,1152]{2,1,0:T(8,128)(2,1)}, bf16[8,288,1152]{2,1,0:T(8,128)(2,1)}) custom-call(s32[1]{0:T(128)} %bitcast.8.core_ref, bf16[896,4608]{1,0:T(8,128)(2,1)} %get-tuple-element.406.refs_0_, bf16[896,1152]{1,0:T(8,128)(2,1)} %bitcast.93), custom_call_target="tpu_custom_call" | custom-call | flops 9999999827968 | bytes 1000000000 | tf_op jit(solution)/shard_map/contract_grad/pallas_call | solution.py:579
  186.9 22.9 %upper_back.1 = (bf16[896,4608]{1,0:T(8,128)(2,1)}, f32[1,4608]{1,0:T(1,128)}, f32[1,1152]{1,0:T(1,128)}) custom-call(s32[1]{0:T(128)} %bitcast.side.index_ref, bf16[896,1152]{1,0:T(8,128)(2,1)} %bitcast.94, bf16[896,4608]{1,0:T(8,128)(2,1)} %get-tuple-element.264.refs_1_, bf16[2304,1152]{1,0:T(8,128)(2,1)} %refs_3_.1, ...), custom_call_target="tpu_custom_call" | custom-call | flops 9999999827968 | bytes 1000000000 | tf_op jit(solution)/shard_map/upper_back/pallas_call | solution.py:299
  209.8 6.9 %fold_seq.5 = (bf16[1,4,288,1152]{3,2,1,0:T(8,128)(2,1)}, bf16[1,4,288,1152]{3,2,1,0:T(8,128)(2,1)}) custom-call(s32[1]{0:T(128)} %bitcast.side.index_ref, bf16[1,2,4,288,1152]{4,3,2,1,0:T(8,128)(2,1)} %bitcast.115, bf16[1,2,4,288,1152]{4,3,2,1,0:T(8,128)(2,1)} %bitcast.10.refs_1_), custom_call_target="tpu_custom_call" | custom-call | flops 9999999827968 | bytes 1000000000 | tf_op jit(solution)/shard_map/fold_seq/pallas_call | solution.py:342
  217.2 16.6 %expand_grad.1 = (bf16[8,72,4608]{2,1,0:T(8,128)(2,1)}, bf16[8,72,4608]{2,1,0:T(8,128)(2,1)}) custom-call(s32[1]{0:T(128)} %bitcast.8.core_ref, bf16[896,1152]{1,0:T(8,128)(2,1)} %get-tuple-element.273.refs_0_, bf16[896,4608]{1,0:T(8,128)(2,1)} %get-tuple-element.276.refs_1_.refs_0_), custom_call_target="tpu_custom_call" | custom-call | flops 9999999827968 | bytes 1000000000 | tf_op jit(solution)/shard_map/expand_grad/pallas_call | solution.py:579
  233.9 28.0 %middle_back.1 = (bf16[896,1152]{1,0:T(8,128)(2,1)}, f32[896,1152]{1,0:T(8,128)}, bf16[896,1152]{1,0:T(8,128)(2,1)}, f32[1,1152]{1,0:T(1,128)}, f32[1,1152]{1,0:T(1,128)}, /*index=5*/f32[1,1152]{1,0:T(1,128)}) custom-call(s32[1]{0:T(128)} %bitcast.side.index_ref, bf16[896,4608]{1,0:T(8,128)(2,1)} %get-tuple-element.276.refs_1_.refs_0_, ...), custom_call_target="tpu_custom_call" | custom-call | flops 9999999827968 | bytes 1000000000 | tf_op jit(solution)/shard_map/middle_back/pallas_call | solution.py:299
  262.0 6.9 %fold_seq.6 = (bf16[1,4,72,4608]{3,2,1,0:T(8,128)(2,1)}, bf16[1,4,72,4608]{3,2,1,0:T(8,128)(2,1)}) custom-call(s32[1]{0:T(128)} %bitcast.side.index_ref, bf16[1,2,4,72,4608]{4,3,2,1,0:T(8,128)(2,1)} %bitcast.114, bf16[1,2,4,72,4608]{4,3,2,1,0:T(8,128)(2,1)} %bitcast.14.refs_1_), custom_call_target="tpu_custom_call" | custom-call | flops 9999999827968 | bytes 1000000000 | tf_op jit(solution)/shard_map/fold_seq/pallas_call | solution.py:342
  270.4 6.9 %collective-permute-done.9 = bf16[4,288,1152]{2,1,0:T(8,128)(2,1)} collective-permute-done((bf16[4,288,1152]{2,1,0:T(8,128)(2,1)}, bf16[4,288,1152]{2,1,0:T(8,128)(2,1)}, u32[]{:S(2)}, u32[]{:S(2)}) %collective-permute-start.9) | collective-permute-done | bytes 2654240 | tf_op jit(solution)/shard_map/ppermute | solution.py:43
  282.7 12.7 %attend_back.1.refs_2_.refs_0_ = bf16[896,3456]{1,0:T(8,128)(2,1)} custom-call(bf16[896,3456]{1,0:T(8,128)(2,1)} %get-tuple-element.247.qkv, bf16[14336,128]{1,0:T(8,128)(2,1)} %get-tuple-element.258.probs_in, bf16[896,1152]{1,0:T(8,128)(2,1)} %get-tuple-element.289.grad_mixed), custom_call_target="tpu_custom_call" | custom-call | flops 9999999827968 | bytes 1000000000 | tf_op jit(solution)/shard_map/attend_back/pallas_call | solution.py:713
  295.3 18.1 %attention_grad.1 = (bf16[8,72,4608]{2,1,0:T(8,128)(2,1)}, bf16[8,72,4608]{2,1,0:T(8,128)(2,1)}) custom-call(s32[1]{0:T(128)} %bitcast.8.core_ref, bf16[896,1152]{1,0:T(8,128)(2,1)} %get-tuple-element.293.refs_0_, bf16[896,1152]{1,0:T(8,128)(2,1)} %get-tuple-element.294.refs_0_.refs_1_, bf16[896,3456]{1,0:T(8,128)(2,1)} %attend_back.1.refs_2_.refs_0_, ...), custom_call_target="tpu_custom_call" | custom-call | flops 9999999827968 | bytes 1000000000 | tf_op jit(solution)/shard_map/attention_grad/pallas_call | solution.py:579
  317.8 20.3 %base_back.1 = (bf16[896,1152]{1,0:T(8,128)(2,1)}, f32[1,1152]{1,0:T(1,128)}, f32[1,1152]{1,0:T(1,128)}, f32[1,1152]{1,0:T(1,128)}) custom-call(s32[1]{0:T(128)} %bitcast.side.index_ref, bf16[896,3456]{1,0:T(8,128)(2,1)} %attend_back.1.refs_2_.refs_0_, f32[896,1152]{1,0:T(8,128)} %get-tuple-element.302.refs_1_, f32[896,1152]{1,0:T(8,128)} %get-tuple-element.303.refs_2_, ...), custom_call_target="tpu_custom_call" | custom-call | flops 9999999827968 | bytes 1000000000 | tf_op jit(solution)/shard_map/base_back/pallas_call | solution.py:299
  358.8 10.8 %skip_grad.1 = (bf16[8,144,1152]{2,1,0:T(8,128)(2,1)}, bf16[8,144,1152]{2,1,0:T(8,128)(2,1)}) custom-call(s32[1]{0:T(128)} %bitcast.8.core_ref, bf16[896,1152]{1,0:T(8,128)(2,1)} %bitcast.92, bf16[896,1152]{1,0:T(8,128)(2,1)} %maximum_select_fusion.refs_1_, bf16[896,1152]{1,0:T(8,128)(2,1)} %get-tuple-element.379.refs_2_.refs_0_), custom_call_target="tpu_custom_call" | custom-call | flops 9999999827968 | bytes 1000000000 | tf_op jit(solution)/shard_map/skip_grad/pallas_call | solution.py:579
  403.3 17.3 %collective-permute-done.23 = bf16[2,72,2304]{2,1,0:T(8,128)(2,1)} collective-permute-done((bf16[2,72,2304]{2,1,0:T(8,128)(2,1)}, bf16[2,72,2304]{2,1,0:T(8,128)(2,1)}, u32[]{:S(2)}, u32[]{:S(2)}) %collective-permute-start.23) | collective-permute-done | bytes 663584 | tf_op jit(solution)/shard_map/ppermute | solution.py:43
  429.3 8.9 %collective-permute-done.26 = bf16[1,72,2304]{2,1,0:T(8,128)(2,1)} collective-permute-done((bf16[1,72,2304]{2,1,0:T(8,128)(2,1)}, bf16[1,72,2304]{2,1,0:T(8,128)(2,1)}, u32[]{:S(2)}, u32[]{:S(2)}) %collective-permute-start.26) | collective-permute-done | bytes 331808 | tf_op jit(solution)/shard_map/ppermute | solution.py:43
  450.7 12.2 %joined_back.1 = (bf16[896,1152]{1,0:T(8,128)(2,1)}, bf16[896,576]{1,0:T(8,128)(2,1)}, bf16[896,576]{1,0:T(8,128)(2,1)}) custom-call(s32[1]{0:T(128)} %bitcast.side.index_ref, bf16[896,1152]{1,0:T(8,128)(2,1)} %get-tuple-element.379.refs_2_.refs_0_, bf16[1152,1152]{1,0:T(8,128)(2,1)} %refs_1_.1, bf16[1152,1152]{1,0:T(8,128)(2,1)} %all-gather.9.cloned.1.call-done.refs_6_.refs_2_), custom_call_target="tpu_custom_call" | custom-call | flops 9999999827968 | bytes 1000000000 | tf_op jit(solution)/shard_map/joined_back/pallas_call | solution.py:299
  484.2 7.1 %widen.4 = f32[2304,1152]{1,0:T(8,128)} custom-call(bf16[2304,1152]{1,0:T(8,128)(2,1)} %all-gather.17.cloned.1.call-done.value), custom_call_target="tpu_custom_call" | custom-call | flops 9999999827968 | bytes 1000000000 | tf_op jit(solution)/shard_map/widen/pallas_call | solution.py:393
  511.3 20.0 %contract.1 = bf16[896,1152]{1,0:T(8,128)(2,1)} custom-call(s32[1]{0:T(128)} %bitcast.side.index_ref, bf16[896,4608]{1,0:T(8,128)(2,1)} %get-tuple-element.406.refs_0_, f32[896,1152]{1,0:T(8,128)} %get-tuple-element.407.refs_1_, f32[1,1152]{1,0:T(1,128)} %reshape.548.refs_2_, bf16[2304,1152]{1,0:T(8,128)(2,1)} %refs_3_.1, ...), custom_call_target="tpu_custom_call" | custom-call | flops 9999999827968 | bytes 1000000000 | tf_op jit(solution)/shard_map/contract/pallas_call | solution.py:299
  544.3 7.1 %widen.5 = f32[576,4608]{1,0:T(8,128)} custom-call(bf16[576,4608]{1,0:T(8,128)(2,1)} %all-gather.23.cloned.1.call-done.value), custom_call_target="tpu_custom_call" | custom-call | flops 9999999827968 | bytes 1000000000 | tf_op jit(solution)/shard_map/widen/pallas_call | solution.py:393
  558.2 7.0 %widen.6 = (f32[576,3456]{1,0:T(8,128)}, f32[576,1152]{1,0:T(8,128)}) custom-call(bf16[576,4608]{1,0:T(8,128)(2,1)} %all-gather.21.cloned.1.call-done.value), custom_call_target="tpu_custom_call" | custom-call | flops 9999999827968 | bytes 1000000000 | tf_op jit(solution)/shard_map/widen/pallas_call | solution.py:393
  (243 shorter events, 203.9 us)
Async XLA Ops:
  7.3 94.5 %all-gather.9.cloned.1.call-start = ((), (), s32[]{:S(2)}) async-start(), calls=%async_computation | async-start | bytes 2985984 | tf_op jit(solution)/shard_map/all_gather | solution.py:86
  19.9 81.9 %all-gather.11.cloned.1.call-start = ((), (), s32[]{:S(2)}) async-start(), calls=%async_computation.1 | async-start | bytes 5971968 | tf_op jit(solution)/shard_map/all_gather | solution.py:86
  19.9 79.2 %collective-permute-start.6 = (bf16[72,4608]{1,0:T(8,128)(2,1)}, bf16[72,4608]{1,0:T(8,128)(2,1)}, u32[]{:S(2)}, u32[]{:S(2)}) collective-permute-start(bf16[72,4608]{1,0:T(8,128)(2,1)} %constant_dynamic-slice_fusion.11), channel_id=1, source_target_pairs={{0,1},{1,0},{2,3},{3,2},{4,5},{5,4},{6,7},{7,6},{8,9},{9,8},{10,11... | collective-permute-start | bytes 1990664 | tf_op jit(solution)/shard_map/ppermute | solution.py:43
  21.2 37.2 %collective-permute-start.4 = (bf16[72,4608]{1,0:T(8,128)(2,1)}, bf16[72,4608]{1,0:T(8,128)(2,1)}, u32[]{:S(2)}, u32[]{:S(2)}) collective-permute-start(bf16[72,4608]{1,0:T(8,128)(2,1)} %pad_maximum_fusion.6), channel_id=1, source_target_pairs={{0,1},{1,0},{2,3},{3,2},{4,5},{5,4},{6,7},{7,6},{8,9},{9,8},{10,11... | collective-permute-start | bytes 1990664 | tf_op jit(solution)/shard_map/ppermute | solution.py:43
  23.3 51.7 %collective-permute-start.1 = (bf16[7,128,576]{1,2,0:T(8,128)(2,1)}, bf16[7,128,576]{1,2,0:T(8,128)(2,1)}, u32[]{:S(2)}, u32[]{:S(2)}) collective-permute-start(bf16[7,128,576]{1,2,0:T(8,128)(2,1)} %get-tuple-element.443), channel_id=1, source_target_pairs={{0,1},{1,0},{2,3},{3,2},{4,5},{5,4},{6,7},{7,6},{8,9},{9,8},{10,11... | collective-permute-start | bytes 3096584 | tf_op jit(solution)/shard_map/ppermute | solution.py:201
  24.1 71.6 %collective-permute-start = (bf16[7,64,1152]{2,1,0:T(8,128)(2,1)}, bf16[7,64,1152]{2,1,0:T(8,128)(2,1)}, u32[]{:S(2)}, u32[]{:S(2)}) collective-permute-start(bf16[7,64,1152]{2,1,0:T(8,128)(2,1)} %get-tuple-element.445), channel_id=1, source_target_pairs={{0,1},{1,0},{2,3},{3,2},{4,5},{5,4},{6,7},{7,6},{8,9},{9,8},{10,11... | collective-permute-start | bytes 3096584 | tf_op jit(solution)/shard_map/ppermute | solution.py:201
  58.4 83.0 %all-gather.13.cloned.1.call-start = ((), (), s32[]{:S(2)}) async-start(), calls=%async_computation.2 | async-start | bytes 5971968 | tf_op jit(solution)/shard_map/all_gather | solution.py:86
  99.1 38.6 %collective-permute-start.7 = (bf16[288,1152]{1,0:T(8,128)(2,1)}, bf16[288,1152]{1,0:T(8,128)(2,1)}, u32[]{:S(2)}, u32[]{:S(2)}) collective-permute-start(bf16[288,1152]{1,0:T(8,128)(2,1)} %eighth.1), channel_id=1, source_target_pairs={{0,1},{1,0},{2,3},{3,2},{4,5},{5,4},{6,7},{7,6},{8,9},{9,8},{10,11... | collective-permute-start | bytes 1990664 | tf_op jit(solution)/shard_map/ppermute | solution.py:43
  99.7 38.0 %collective-permute-start.5 = (bf16[7,64,1152]{2,1,0:T(8,128)(2,1)}, bf16[7,64,1152]{2,1,0:T(8,128)(2,1)}, u32[]{:S(2)}, u32[]{:S(2)}) collective-permute-start(bf16[7,64,1152]{2,1,0:T(8,128)(2,1)} %get-tuple-element.250), channel_id=1, source_target_pairs={{0,1},{1,0},{2,3},{3,2},{4,5},{5,4},{6,7},{7,6},{8,9},{9,8},{10,11... | collective-permute-start | bytes 3096584 | tf_op jit(solution)/shard_map/ppermute | solution.py:201
  101.2 85.7 %all-gather.15.cloned.1.call-start = ((), (), s32[]{:S(2)}) async-start(), calls=%async_computation.3 | async-start | bytes 5971968 | tf_op jit(solution)/shard_map/all_gather | solution.py:86
  141.2 343.0 %all-gather.17.cloned.1.call-start = ((), (), s32[]{:S(2)}) async-start(), calls=%async_computation.4 | async-start | bytes 5971968 | tf_op jit(solution)/shard_map/all_gather | solution.py:86
  216.7 60.7 %collective-permute-start.9 = (bf16[4,288,1152]{2,1,0:T(8,128)(2,1)}, bf16[4,288,1152]{2,1,0:T(8,128)(2,1)}, u32[]{:S(2)}, u32[]{:S(2)}) collective-permute-start(bf16[4,288,1152]{2,1,0:T(8,128)(2,1)} %bitcast.100), channel_id=1, source_target_pairs={{0,1},{1,0},{2,3},{3,2},{4,5},{5,4},{6,7},{7,6},{8,9},{9,8},{10,11... | collective-permute-start | bytes 7962632 | tf_op jit(solution)/shard_map/ppermute | solution.py:43
  268.9 69.2 %collective-permute-start.14 = (bf16[4,72,4608]{2,1,0:T(8,128)(2,1)}, bf16[4,72,4608]{2,1,0:T(8,128)(2,1)}, u32[]{:S(2)}, u32[]{:S(2)}) collective-permute-start(bf16[4,72,4608]{2,1,0:T(8,128)(2,1)} %bitcast.99), channel_id=1, source_target_pairs={{0,1},{1,0},{2,3},{3,2},{4,5},{5,4},{6,7},{7,6},{8,9},{9,8},{10,11... | collective-permute-start | bytes 7962632 | tf_op jit(solution)/shard_map/ppermute | solution.py:43
  344.9 37.4 %collective-permute-start.21 = (bf16[288,1152]{1,0:T(8,128)(2,1)}, bf16[288,1152]{1,0:T(8,128)(2,1)}, u32[]{:S(2)}, u32[]{:S(2)}) collective-permute-start(bf16[288,1152]{1,0:T(8,128)(2,1)} %add.128.refs_0_), channel_id=1, source_target_pairs={{0,16},{16,0},{1,17},{17,1},{2,18},{18,2},{3,19},{19,3},{4,20},{20... | collective-permute-start | bytes 1990664 | tf_op jit(solution)/shard_map/ppermute | solution.py:43
  357.5 69.2 %collective-permute-start.18 = (bf16[4,72,2304]{2,1,0:T(8,128)(2,1)}, bf16[4,72,2304]{2,1,0:T(8,128)(2,1)}, u32[]{:S(2)}, u32[]{:S(2)}) collective-permute-start(bf16[4,72,2304]{2,1,0:T(8,128)(2,1)} %bitcast.32), channel_id=1, source_target_pairs={{0,1},{1,0},{2,3},{3,2},{4,5},{5,4},{6,7},{7,6},{8,9},{9,8},{10,11... | collective-permute-start | bytes 3981320 | tf_op jit(solution)/shard_map/ppermute | solution.py:43
  381.7 93.6 %collective-permute-start.17 = (bf16[4,144,1152]{2,1,0:T(8,128)(2,1)}, bf16[4,144,1152]{2,1,0:T(8,128)(2,1)}, u32[]{:S(2)}, u32[]{:S(2)}) collective-permute-start(bf16[4,144,1152]{2,1,0:T(8,128)(2,1)} %bitcast.101), channel_id=1, source_target_pairs={{0,1},{1,0},{2,3},{3,2},{4,5},{5,4},{6,7},{7,6},{8,9},{9,8},{10,11... | collective-permute-start | bytes 3981320 | tf_op jit(solution)/shard_map/ppermute | solution.py:43
  384.6 159.6 %all-gather.23.cloned.1.call-start = ((), (), s32[]{:S(2)}) async-start(), calls=%async_computation.7 | async-start | bytes 5971968 | tf_op jit(solution)/shard_map/all_gather | solution.py:86
  395.8 46.7 %collective-permute-start.25 = (bf16[72,4608]{1,0:T(8,128)(2,1)}, bf16[72,4608]{1,0:T(8,128)(2,1)}, u32[]{:S(2)}, u32[]{:S(2)}) collective-permute-start(bf16[72,4608]{1,0:T(8,128)(2,1)} %add.130.refs_0_), channel_id=1, source_target_pairs={{0,16},{16,0},{1,17},{17,1},{2,18},{18,2},{3,19},{19,3},{4,20},{20... | collective-permute-start | bytes 1990664 | tf_op jit(solution)/shard_map/ppermute | solution.py:43
  440.2 60.0 %collective-permute-start.32 = (bf16[72,2304]{1,0:T(8,128)(2,1)}, bf16[72,2304]{1,0:T(8,128)(2,1)}, u32[]{:S(2)}, u32[]{:S(2)}) collective-permute-start(bf16[72,2304]{1,0:T(8,128)(2,1)} %add.132.refs_0_), channel_id=1, source_target_pairs={{0,16},{16,0},{1,17},{17,1},{2,18},{18,2},{3,19},{19,3},{4,20},{20... | collective-permute-start | bytes 995336 | tf_op jit(solution)/shard_map/ppermute | solution.py:43
  444.9 113.3 %all-gather.21.cloned.1.call-start = ((), (), s32[]{:S(2)}) async-start(), calls=%async_computation.6 | async-start | bytes 5971968 | tf_op jit(solution)/shard_map/all_gather | solution.py:86
  484.2 53.0 %collective-permute-start.35 = (bf16[7,128,576]{1,2,0:T(8,128)(2,1)}, bf16[7,128,576]{1,2,0:T(8,128)(2,1)}, u32[]{:S(2)}, u32[]{:S(2)}) collective-permute-start(bf16[7,128,576]{1,2,0:T(8,128)(2,1)} %copy.35), channel_id=1, source_target_pairs={{0,1},{1,0},{2,3},{3,2},{4,5},{5,4},{6,7},{7,6},{8,9},{9,8},{10,11... | collective-permute-start | bytes 3096584 | tf_op jit(solution)/shard_map/ppermute | solution.py:201
  496.5 34.8 %collective-permute-start.37 = (bf16[7,64,1152]{2,1,0:T(8,128)(2,1)}, bf16[7,64,1152]{2,1,0:T(8,128)(2,1)}, u32[]{:S(2)}, u32[]{:S(2)}) collective-permute-start(bf16[7,64,1152]{2,1,0:T(8,128)(2,1)} %get-tuple-element.411), channel_id=1, source_target_pairs={{0,1},{1,0},{2,3},{3,2},{4,5},{5,4},{6,7},{7,6},{8,9},{9,8},{10,11... | collective-permute-start | bytes 3096584 | tf_op jit(solution)/shard_map/ppermute | solution.py:201
  500.2 51.2 %collective-permute-start.39 = (f32[1,12672]{1,0:T(1,128)}, f32[1,12672]{1,0:T(1,128)}, u32[]{:S(2)}, u32[]{:S(2)}) collective-permute-start(f32[1,12672]{1,0:T(1,128)} %add.137.refs_0_), channel_id=1, source_target_pairs={{0,1},{1,0},{2,3},{3,2},{4,5},{5,4},{6,7},{7,6},{8,9},{9,8},{10,11... | collective-permute-start | bytes 152072 | tf_op jit(solution)/shard_map/ppermute | solution.py:43
  504.5 64.4 %all-gather.19.cloned.1.call-start = ((), (), s32[]{:S(2)}) async-start(), calls=%async_computation.5 | async-start | bytes 2985984 | tf_op jit(solution)/shard_map/all_gather | solution.py:86
  (53 other events, 765.2 us)
Sparse Core Ops, SparseCore 0:
  20.0 24.0 all-gather.8
  58.5 34.8 all-gather.10
  101.3 34.2 all-gather.12
  141.3 34.1 all-gather.14
  384.8 54.7 all-gather.16
  445.0 51.3 all-gather.22
  504.6 40.3 all-gather.20
  546.6 22.2 all-gather.18

commit v5 on v4

--- a/solution.py
+++ b/solution.py
@@ -234,12 +234,12 @@
         copies.append([])
         target = base + b
         if len(parts) == 1:
-            row, column = divmod(b, columns // size)
+            row, column = divmod(b + offset, columns // size)
             source = parts[0].at[pl.ds(row * size, size), pl.ds(column * size, size)]
             copy = pltpu.make_async_copy(source, blocks.at[target], sems.at[0, target])
             copies[b].append((first, copy))
         elif rows >= size:
-            half, place = divmod(b, rows // size)
+            half, place = divmod(b + offset, rows // size)
             for p, part in enumerate(parts):
                 mine = side == half if p == 0 else side != half
                 source = part.at[pl.ds(place * size, size), :]
@@ -337,20 +337,22 @@
     index = lax.axis_index(name).reshape(1)
     count, unit, columns = parts[0].shape
     inner = count // (2 * outer)
-    size = columns // lanes
+    size, together = columns // lanes, min(inner, 2)
     half = jax.ShapeDtypeStruct((outer, inner, unit, size), BF16)
     out = pl.pallas_call(
         fold_kernel,
         out_shape=(half, half),
         grid_spec=pltpu.PrefetchScalarGridSpec(
             num_scalar_prefetch=1,
-            grid=(outer, inner),
+            grid=(outer, inner // together),
             in_specs=[
-                pl.BlockSpec((1, 2, 1, unit, size), lambda i, j, _: (i, 0, j, 0, lane))
+                pl.BlockSpec(
+                    (1, 2, together, unit, size), lambda i, j, _: (i, 0, j, 0, lane)
+                )
                 for _ in parts
             ],
             out_specs=(
-                pl.BlockSpec((1, 1, unit, size), lambda i, j, _: (i, j, 0, 0)),
+                pl.BlockSpec((1, together, unit, size), lambda i, j, _: (i, j, 0, 0)),
             )
             * 2,
         ),
@@ -389,7 +391,7 @@
 
 def widen(cuts, value):
     rows, columns = value.shape
-    steps = 4 if rows % 32 == 0 else 2
+    steps = 2
     return pl.pallas_call(
         widen_kernel,
         out_shape=tuple(jax.ShapeDtypeStruct((rows, size), F32) for size in cuts),
@@ -441,17 +443,20 @@
     return slice(b * WIDTH, (b + 1) * WIDTH)
 
 
+def skip_base_body(wait, blocks, rows, vectors, outs, sums):
+    wait(0)
+    outs[0][...] = simple(rows[0][...], blocks[0])
+
+
 def base_inward_body(wait, blocks, rows, vectors, outs, sums):
     wait(0)
-    total = simple(rows[0][...], blocks[0])
-    wait(1)
-    total = total + simple(rows[1][...], blocks[1]) + vectors[0][...]
+    total = simple(rows[0][...], blocks[0]) + rows[1][...] + vectors[0][...]
     outs[0][...] = total
     normed = (normalize(total)[0] * vectors[1][...] + vectors[2][...]).astype(BF16)
     outs[1][...] = normed
     for b in range(3):
-        wait(2 + b)
-        outs[2][:, columns_of(b)] = simple(outs[1][...], blocks[2 + b]).astype(BF16)
+        wait(1 + b)
+        outs[2][:, columns_of(b)] = simple(outs[1][...], blocks[1 + b]).astype(BF16)
 
 
 def middle_expand_body(wait, blocks, rows, vectors, outs, sums):
@@ -787,6 +792,12 @@
         grad_pieces = chain.run(lambda a: split_items(a, per), cotangent)
         skip_rows = chain.run(
             lambda *a: joined_pieces(a, 2).reshape(rows, width), *skip_pieces
+        )
+        skip_base = chain.run(
+            lambda a: dense(
+                "skip_base", skip_base_body, (a,), (), ((1, 1, skip_parts),), [(width, F32)]
+            )[0],
+            skip_rows,
         )
         expand_parts = (expand_weight, share(*chain.enter(expand_piece)))
         contract_piece = chain.run(eighth_copy, contract_weight)
@@ -821,8 +832,15 @@
         contract_offset,
     ) = vectors
     skip_matrix, inward_matrix = (2, 0, skip_parts), (3, 0, inward_parts)
-    outward_matrix = (1, 3, outward_parts)
+    outward_matrix = (1, 3 if fast else 0, outward_parts)
     skip_rows, latent_rows = (a.reshape(rows, width) for a in (skip_rows, latent_rows))
+    if not fast:
+        skip_base = chain.run(
+            lambda a: dense(
+                "skip_base", skip_base_body, (a,), (), ((1, 1, skip_parts),), [(width, F32)]
+            )[0],
+            skip_rows,
+        )
     one, wide = (width, BF16), (width, F32)
     hidden = (expand_offset.shape[1], BF16)
 
@@ -832,19 +850,16 @@
             base_inward_body,
             a,
             (skip_offset, gain_first, shift_first),
-            (skip_matrix, inward_matrix),
+            ((1, 0, skip_parts), inward_matrix),
             [wide, one, (3 * width, BF16)],
         ),
         latent_rows,
-        skip_rows,
+        skip_base,
     )
     mixed_rows, probs = chain.run(lambda a: attend(a, live), qkv_vals)
     if fast:
         contract_parts = (contract_weight, share(*chain.enter(contract_piece)))
     expand_matrix, contract_matrix = (4, 0, expand_parts), (4, 0, contract_parts)
-    grad_out = chain.run(
-        lambda *a: joined_pieces(a, 1).reshape(rows, width), *grad_pieces
-    )
     middle, second_normed, activated, slope = chain.run(
         lambda *a: dense(
             "middle_expand",
@@ -857,6 +872,9 @@
         ),
         mixed_rows,
         base,
+    )
+    grad_out = chain.run(
+        lambda *a: joined_pieces(a, 1).reshape(rows, width), *grad_pieces
     )
     contract_sum = Reduction(chain, "contract_grad", (activated,), (grad_out,))
     grad_upper, grad_expand_off, grad_contract_off = chain.run(

time: 591 us -> 587 us (level)
    ppermute x6, waiting for transfers between devices: 28.8 us -> 21.1 us  [swap_pieces(): lax.ppermute(piece, 'seq', [(i, (i + hop) % ways) for i in range(ways)])]
    pallas_call x7 -> x8, Pallas kernels: 157 us -> 161 us  [dense(): pl.pallas_call(kernel, out_shape=tuple((jax.ShapeDtypeStruct((rows, c), d...]
  transfers between devices with their start and end apart: 48 -> 48, of which waited for: 12 -> 14; matrix products, arithmetic and copies ran while one was open for 9% -> 9% of each run, Pallas kernels for 59% -> 59%
where the time goes in v5:
time: 587 us; the launch traced here: 581 us
  Pallas kernels  350 us (60%)
  waiting for transfers between devices  111 us (19%)
  starting transfers between devices  44.8 us (8%)
  local copies, waits for them, and re-layouts  37.6 us (6%)
  other arithmetic  22.5 us (4%)
  between operations  15.1 us (3%)
    pallas_call x8, Pallas kernels, dense(): pl.pallas_call(kernel, out_shape=tuple((jax.ShapeDtypeStruct((rows, c), d...  161 us
    ppermute x34, waiting for transfers between devices, flip(): return lax.ppermute(array, axis, [(0, 1), (1, 0)])  83.2 us
    pallas_call x4, Pallas kernels, core_gradients(): pl.pallas_call(kernel, out_shape=(half, half), grid_spec=pltpu.PrefetchSc...  62.1 us
    pallas_call x15, Pallas kernels, fold(): pl.pallas_call(fold_kernel, out_shape=(half, half), grid_spec=pltpu.Prefe...  52.3 us
    ppermute x34, starting transfers between devices, flip(): return lax.ppermute(array, axis, [(0, 1), (1, 0)])  36.4 us
    pallas_call x14, Pallas kernels, add(): pl.pallas_call(add_kernel, out_shape=jax.ShapeDtypeStruct((rows, columns...  26.7 us
    pallas_call x4, Pallas kernels, widen(): pl.pallas_call(widen_kernel, out_shape=tuple((jax.ShapeDtypeStruct((rows,...  22.5 us
    ppermute x6, waiting for transfers between devices, swap_pieces(): lax.ppermute(piece, 'seq', [(i, (i + hop) % ways) for i in range(ways)])  21.1 us
  transfers between devices with their start and end apart: 48, of which 14 were waited for; matrix products, arithmetic and copies ran while one was open for 9% of the time, Pallas kernels for 59%

profile of v5, /device:TPU:0, one launch (start us, length us, event | category | flops | bytes accessed | tf_op | source)
XLA Modules:
  0.0 580.8 jit_solution(16168676709501328933)
XLA Ops:
  27.5 25.3 %collective-permute-done.3 = bf16[1,6336]{1,0:T(2,128)(2,1)S(1)} collective-permute-done((bf16[1,6336]{1,0:T(2,128)(2,1)S(1)}, bf16[1,6336]{1,0:T(2,128)(2,1)S(1)}, u32[]{:S(2)}, u32[]{:S(2)}) %collective-permute-start.3) | collective-permute-done | bytes 12704 | tf_op jit(solution)/shard_map/ppermute | solution.py:43
  58.5 16.6 %collective-permute-done.1 = bf16[7,128,576]{1,2,0:T(8,128)(2,1)} collective-permute-done((bf16[7,128,576]{1,2,0:T(8,128)(2,1)}, bf16[7,128,576]{1,2,0:T(8,128)(2,1)}, u32[]{:S(2)}, u32[]{:S(2)}) %collective-permute-start.1) | collective-permute-done | bytes 1032224 | tf_op jit(solution)/shard_map/ppermute | solution.py:201
  81.3 7.7 %skip_base.1.refs_1_ = f32[896,1152]{1,0:T(8,128)} custom-call(s32[1]{0:T(128)} %bitcast.side.index_ref, bf16[896,1152]{1,0:T(8,128)(2,1)} %maximum_select_fusion.refs_0_.refs_1_, bf16[1152,1152]{1,0:T(8,128)(2,1)} %refs_1_.3, bf16[1152,1152]{1,0:T(8,128)(2,1)} %all-gather.9.cloned.1.call-done.refs_2_.refs_6_), custom_call_target="tpu_custom_call" | custom-call | flops 9999999827968 | bytes 1000000000 | tf_op jit(solution)/shard_map/skip_base/pallas_call | solution.py:299
  101.8 21.4 %base_inward.1 = (f32[896,1152]{1,0:T(8,128)}, bf16[896,1152]{1,0:T(8,128)(2,1)}, bf16[896,3456]{1,0:T(8,128)(2,1)}) custom-call(s32[1]{0:T(128)} %bitcast.side.index_ref, bf16[896,1152]{1,0:T(8,128)(2,1)} %bitcast.91, f32[896,1152]{1,0:T(8,128)} %skip_base.1.refs_1_, f32[1,1152]{1,0:T(1,128)} %reshape.542.refs_2_, f32[1,1152]{1,0:T(1,128)} %reshape.543.refs_3_, ...), custom_call_target="tpu_custom_call" | custom-call | flops 9999999827968 | bytes 1000000000 | tf_op jit(solution)/shard_map/base_inward/pallas_call | solution.py:299
  123.2 10.8 %attend.1 = (bf16[896,1152]{1,0:T(8,128)(2,1)}, bf16[14336,128]{1,0:T(8,128)(2,1)}) custom-call(s32[7]{0:T(128)} %pad_dynamic-slice_fusion.6.lengths, bf16[896,3456]{1,0:T(8,128)(2,1)} %get-tuple-element.249.qkv), custom_call_target="tpu_custom_call" | custom-call | flops 9999999827968 | bytes 1000000000 | tf_op jit(solution)/shard_map/attend/pallas_call | solution.py:660
  135.7 28.7 %middle_expand.1 = (f32[896,1152]{1,0:T(8,128)}, bf16[896,1152]{1,0:T(8,128)(2,1)}, bf16[896,4608]{1,0:T(8,128)(2,1)}, bf16[896,4608]{1,0:T(8,128)(2,1)}) custom-call(s32[1]{0:T(128)} %bitcast.side.index_ref, bf16[896,1152]{1,0:T(8,128)(2,1)} %get-tuple-element.296.refs_0_.refs_1_, f32[896,1152]{1,0:T(8,128)} %get-tuple-element.304.refs_1_, ...), custom_call_target="tpu_custom_call" | custom-call | flops 9999999827968 | bytes 1000000000 | tf_op jit(solution)/shard_map/middle_expand/pallas_call | solution.py:299
  168.0 16.7 %contract_grad.1 = (bf16[8,288,1152]{2,1,0:T(8,128)(2,1)}, bf16[8,288,1152]{2,1,0:T(8,128)(2,1)}) custom-call(s32[1]{0:T(128)} %bitcast.7.core_ref, bf16[896,4608]{1,0:T(8,128)(2,1)} %get-tuple-element.408.refs_0_, bf16[896,1152]{1,0:T(8,128)(2,1)} %bitcast.93), custom_call_target="tpu_custom_call" | custom-call | flops 9999999827968 | bytes 1000000000 | tf_op jit(solution)/shard_map/contract_grad/pallas_call | solution.py:584
  184.8 22.9 %upper_back.1 = (bf16[896,4608]{1,0:T(8,128)(2,1)}, f32[1,4608]{1,0:T(1,128)}, f32[1,1152]{1,0:T(1,128)}) custom-call(s32[1]{0:T(128)} %bitcast.side.index_ref, bf16[896,1152]{1,0:T(8,128)(2,1)} %bitcast.94, bf16[896,4608]{1,0:T(8,128)(2,1)} %get-tuple-element.266.refs_1_, bf16[2304,1152]{1,0:T(8,128)(2,1)} %refs_3_.1, ...), custom_call_target="tpu_custom_call" | custom-call | flops 9999999827968 | bytes 1000000000 | tf_op jit(solution)/shard_map/upper_back/pallas_call | solution.py:299
  207.7 6.2 %fold_seq.5 = (bf16[1,4,288,1152]{3,2,1,0:T(8,128)(2,1)}, bf16[1,4,288,1152]{3,2,1,0:T(8,128)(2,1)}) custom-call(s32[1]{0:T(128)} %bitcast.side.index_ref, bf16[1,2,4,288,1152]{4,3,2,1,0:T(8,128)(2,1)} %bitcast.115, bf16[1,2,4,288,1152]{4,3,2,1,0:T(8,128)(2,1)} %bitcast.10.refs_1_), custom_call_target="tpu_custom_call" | custom-call | flops 9999999827968 | bytes 1000000000 | tf_op jit(solution)/shard_map/fold_seq/pallas_call | solution.py:342
  215.4 16.6 %expand_grad.1 = (bf16[8,72,4608]{2,1,0:T(8,128)(2,1)}, bf16[8,72,4608]{2,1,0:T(8,128)(2,1)}) custom-call(s32[1]{0:T(128)} %bitcast.7.core_ref, bf16[896,1152]{1,0:T(8,128)(2,1)} %get-tuple-element.275.refs_0_, bf16[896,4608]{1,0:T(8,128)(2,1)} %get-tuple-element.278.refs_1_.refs_0_), custom_call_target="tpu_custom_call" | custom-call | flops 9999999827968 | bytes 1000000000 | tf_op jit(solution)/shard_map/expand_grad/pallas_call | solution.py:584
  232.0 28.1 %middle_back.1 = (bf16[896,1152]{1,0:T(8,128)(2,1)}, f32[896,1152]{1,0:T(8,128)}, bf16[896,1152]{1,0:T(8,128)(2,1)}, f32[1,1152]{1,0:T(1,128)}, f32[1,1152]{1,0:T(1,128)}, /*index=5*/f32[1,1152]{1,0:T(1,128)}) custom-call(s32[1]{0:T(128)} %bitcast.side.index_ref, bf16[896,4608]{1,0:T(8,128)(2,1)} %get-tuple-element.278.refs_1_.refs_0_, ...), custom_call_target="tpu_custom_call" | custom-call | flops 9999999827968 | bytes 1000000000 | tf_op jit(solution)/shard_map/middle_back/pallas_call | solution.py:299
  260.1 6.2 %fold_seq.6 = (bf16[1,4,72,4608]{3,2,1,0:T(8,128)(2,1)}, bf16[1,4,72,4608]{3,2,1,0:T(8,128)(2,1)}) custom-call(s32[1]{0:T(128)} %bitcast.side.index_ref, bf16[1,2,4,72,4608]{4,3,2,1,0:T(8,128)(2,1)} %bitcast.114, bf16[1,2,4,72,4608]{4,3,2,1,0:T(8,128)(2,1)} %bitcast.14.refs_1_), custom_call_target="tpu_custom_call" | custom-call | flops 9999999827968 | bytes 1000000000 | tf_op jit(solution)/shard_map/fold_seq/pallas_call | solution.py:342
  266.9 7.7 %collective-permute-done.9 = bf16[4,288,1152]{2,1,0:T(8,128)(2,1)} collective-permute-done((bf16[4,288,1152]{2,1,0:T(8,128)(2,1)}, bf16[4,288,1152]{2,1,0:T(8,128)(2,1)}, u32[]{:S(2)}, u32[]{:S(2)}) %collective-permute-start.9) | collective-permute-done | bytes 2654240 | tf_op jit(solution)/shard_map/ppermute | solution.py:43
  279.9 12.7 %attend_back.1.refs_2_.refs_0_ = bf16[896,3456]{1,0:T(8,128)(2,1)} custom-call(bf16[896,3456]{1,0:T(8,128)(2,1)} %get-tuple-element.249.qkv, bf16[14336,128]{1,0:T(8,128)(2,1)} %get-tuple-element.256.probs_in, bf16[896,1152]{1,0:T(8,128)(2,1)} %get-tuple-element.291.grad_mixed), custom_call_target="tpu_custom_call" | custom-call | flops 9999999827968 | bytes 1000000000 | tf_op jit(solution)/shard_map/attend_back/pallas_call | solution.py:718
  292.6 18.1 %attention_grad.1 = (bf16[8,72,4608]{2,1,0:T(8,128)(2,1)}, bf16[8,72,4608]{2,1,0:T(8,128)(2,1)}) custom-call(s32[1]{0:T(128)} %bitcast.7.core_ref, bf16[896,1152]{1,0:T(8,128)(2,1)} %get-tuple-element.295.refs_0_, bf16[896,1152]{1,0:T(8,128)(2,1)} %get-tuple-element.296.refs_0_.refs_1_, bf16[896,3456]{1,0:T(8,128)(2,1)} %attend_back.1.refs_2_.refs_0_, ...), custom_call_target="tpu_custom_call" | custom-call | flops 9999999827968 | bytes 1000000000 | tf_op jit(solution)/shard_map/attention_grad/pallas_call | solution.py:584
  314.2 20.3 %base_back.1 = (bf16[896,1152]{1,0:T(8,128)(2,1)}, f32[1,1152]{1,0:T(1,128)}, f32[1,1152]{1,0:T(1,128)}, f32[1,1152]{1,0:T(1,128)}) custom-call(s32[1]{0:T(128)} %bitcast.side.index_ref, bf16[896,3456]{1,0:T(8,128)(2,1)} %attend_back.1.refs_2_.refs_0_, f32[896,1152]{1,0:T(8,128)} %get-tuple-element.304.refs_1_, f32[896,1152]{1,0:T(8,128)} %get-tuple-element.305.refs_2_, ...), custom_call_target="tpu_custom_call" | custom-call | flops 9999999827968 | bytes 1000000000 | tf_op jit(solution)/shard_map/base_back/pallas_call | solution.py:299
  354.2 10.8 %skip_grad.1 = (bf16[8,144,1152]{2,1,0:T(8,128)(2,1)}, bf16[8,144,1152]{2,1,0:T(8,128)(2,1)}) custom-call(s32[1]{0:T(128)} %bitcast.7.core_ref, bf16[896,1152]{1,0:T(8,128)(2,1)} %bitcast.92, bf16[896,1152]{1,0:T(8,128)(2,1)} %maximum_select_fusion.refs_0_.refs_1_, bf16[896,1152]{1,0:T(8,128)(2,1)} %get-tuple-element.381.refs_2_.refs_0_), custom_call_target="tpu_custom_call" | custom-call | flops 9999999827968 | bytes 1000000000 | tf_op jit(solution)/shard_map/skip_grad/pallas_call | solution.py:584
  399.4 16.1 %collective-permute-done.23 = bf16[2,72,2304]{2,1,0:T(8,128)(2,1)} collective-permute-done((bf16[2,72,2304]{2,1,0:T(8,128)(2,1)}, bf16[2,72,2304]{2,1,0:T(8,128)(2,1)}, u32[]{:S(2)}, u32[]{:S(2)}) %collective-permute-start.23) | collective-permute-done | bytes 663584 | tf_op jit(solution)/shard_map/ppermute | solution.py:43
  424.4 9.2 %collective-permute-done.26 = bf16[1,72,2304]{2,1,0:T(8,128)(2,1)} collective-permute-done((bf16[1,72,2304]{2,1,0:T(8,128)(2,1)}, bf16[1,72,2304]{2,1,0:T(8,128)(2,1)}, u32[]{:S(2)}, u32[]{:S(2)}) %collective-permute-start.26) | collective-permute-done | bytes 331808 | tf_op jit(solution)/shard_map/ppermute | solution.py:43
  446.7 12.2 %joined_back.1 = (bf16[896,1152]{1,0:T(8,128)(2,1)}, bf16[896,576]{1,0:T(8,128)(2,1)}, bf16[896,576]{1,0:T(8,128)(2,1)}) custom-call(s32[1]{0:T(128)} %bitcast.side.index_ref, bf16[896,1152]{1,0:T(8,128)(2,1)} %get-tuple-element.381.refs_2_.refs_0_, bf16[1152,1152]{1,0:T(8,128)(2,1)} %refs_1_.3, bf16[1152,1152]{1,0:T(8,128)(2,1)} %all-gather.9.cloned.1.call-done.refs_2_.refs_6_), custom_call_target="tpu_custom_call" | custom-call | flops 9999999827968 | bytes 1000000000 | tf_op jit(solution)/shard_map/joined_back/pallas_call | solution.py:299
  483.5 6.2 %widen.4 = f32[2304,1152]{1,0:T(8,128)} custom-call(bf16[2304,1152]{1,0:T(8,128)(2,1)} %all-gather.17.cloned.1.call-done.value), custom_call_target="tpu_custom_call" | custom-call | flops 9999999827968 | bytes 1000000000 | tf_op jit(solution)/shard_map/widen/pallas_call | solution.py:395
  510.0 19.6 %contract.1 = bf16[896,1152]{1,0:T(8,128)(2,1)} custom-call(s32[1]{0:T(128)} %bitcast.side.index_ref, bf16[896,4608]{1,0:T(8,128)(2,1)} %get-tuple-element.408.refs_0_, f32[896,1152]{1,0:T(8,128)} %get-tuple-element.409.refs_1_, f32[1,1152]{1,0:T(1,128)} %reshape.549.refs_2_, bf16[2304,1152]{1,0:T(8,128)(2,1)} %refs_3_.1, ...), custom_call_target="tpu_custom_call" | custom-call | flops 9999999827968 | bytes 1000000000 | tf_op jit(solution)/shard_map/contract/pallas_call | solution.py:299
  542.4 6.2 %widen.5 = f32[576,4608]{1,0:T(8,128)} custom-call(bf16[576,4608]{1,0:T(8,128)(2,1)} %all-gather.23.cloned.1.call-done.value), custom_call_target="tpu_custom_call" | custom-call | flops 9999999827968 | bytes 1000000000 | tf_op jit(solution)/shard_map/widen/pallas_call | solution.py:395
  555.5 6.1 %widen.6 = (f32[576,3456]{1,0:T(8,128)}, f32[576,1152]{1,0:T(8,128)}) custom-call(bf16[576,4608]{1,0:T(8,128)(2,1)} %all-gather.21.cloned.1.call-done.value), custom_call_target="tpu_custom_call" | custom-call | flops 9999999827968 | bytes 1000000000 | tf_op jit(solution)/shard_map/widen/pallas_call | solution.py:395
  (244 shorter events, 213.4 us)
Async XLA Ops:
  7.3 74.0 %all-gather.9.cloned.1.call-start = ((), (), s32[]{:S(2)}) async-start(), calls=%async_computation | async-start | bytes 2985984 | tf_op jit(solution)/shard_map/all_gather | solution.py:86
  19.9 82.0 %all-gather.11.cloned.1.call-start = ((), (), s32[]{:S(2)}) async-start(), calls=%async_computation.1 | async-start | bytes 5971968 | tf_op jit(solution)/shard_map/all_gather | solution.py:86
  19.9 79.3 %collective-permute-start.5 = (bf16[72,4608]{1,0:T(8,128)(2,1)}, bf16[72,4608]{1,0:T(8,128)(2,1)}, u32[]{:S(2)}, u32[]{:S(2)}) collective-permute-start(bf16[72,4608]{1,0:T(8,128)(2,1)} %constant_dynamic-slice_fusion.11), channel_id=1, source_target_pairs={{0,1},{1,0},{2,3},{3,2},{4,5},{5,4},{6,7},{7,6},{8,9},{9,8},{10,11... | collective-permute-start | bytes 1990664 | tf_op jit(solution)/shard_map/ppermute | solution.py:43
  21.2 37.2 %collective-permute-start.4 = (bf16[72,4608]{1,0:T(8,128)(2,1)}, bf16[72,4608]{1,0:T(8,128)(2,1)}, u32[]{:S(2)}, u32[]{:S(2)}) collective-permute-start(bf16[72,4608]{1,0:T(8,128)(2,1)} %pad_maximum_fusion.6), channel_id=1, source_target_pairs={{0,1},{1,0},{2,3},{3,2},{4,5},{5,4},{6,7},{7,6},{8,9},{9,8},{10,11... | collective-permute-start | bytes 1990664 | tf_op jit(solution)/shard_map/ppermute | solution.py:43
  23.3 51.7 %collective-permute-start.1 = (bf16[7,128,576]{1,2,0:T(8,128)(2,1)}, bf16[7,128,576]{1,2,0:T(8,128)(2,1)}, u32[]{:S(2)}, u32[]{:S(2)}) collective-permute-start(bf16[7,128,576]{1,2,0:T(8,128)(2,1)} %get-tuple-element.445), channel_id=1, source_target_pairs={{0,1},{1,0},{2,3},{3,2},{4,5},{5,4},{6,7},{7,6},{8,9},{9,8},{10,11... | collective-permute-start | bytes 3096584 | tf_op jit(solution)/shard_map/ppermute | solution.py:201
  24.1 71.6 %collective-permute-start = (bf16[7,64,1152]{2,1,0:T(8,128)(2,1)}, bf16[7,64,1152]{2,1,0:T(8,128)(2,1)}, u32[]{:S(2)}, u32[]{:S(2)}) collective-permute-start(bf16[7,64,1152]{2,1,0:T(8,128)(2,1)} %get-tuple-element.447), channel_id=1, source_target_pairs={{0,1},{1,0},{2,3},{3,2},{4,5},{5,4},{6,7},{7,6},{8,9},{9,8},{10,11... | collective-permute-start | bytes 3096584 | tf_op jit(solution)/shard_map/ppermute | solution.py:201
  58.4 77.3 %all-gather.13.cloned.1.call-start = ((), (), s32[]{:S(2)}) async-start(), calls=%async_computation.2 | async-start | bytes 5971968 | tf_op jit(solution)/shard_map/all_gather | solution.py:86
  99.2 34.8 %collective-permute-start.7 = (bf16[288,1152]{1,0:T(8,128)(2,1)}, bf16[288,1152]{1,0:T(8,128)(2,1)}, u32[]{:S(2)}, u32[]{:S(2)}) collective-permute-start(bf16[288,1152]{1,0:T(8,128)(2,1)} %eighth.1), channel_id=1, source_target_pairs={{0,1},{1,0},{2,3},{3,2},{4,5},{5,4},{6,7},{7,6},{8,9},{9,8},{10,11... | collective-permute-start | bytes 1990664 | tf_op jit(solution)/shard_map/ppermute | solution.py:43
  99.8 64.6 %collective-permute-start.6 = (bf16[7,64,1152]{2,1,0:T(8,128)(2,1)}, bf16[7,64,1152]{2,1,0:T(8,128)(2,1)}, u32[]{:S(2)}, u32[]{:S(2)}) collective-permute-start(bf16[7,64,1152]{2,1,0:T(8,128)(2,1)} %get-tuple-element.258), channel_id=1, source_target_pairs={{0,1},{1,0},{2,3},{3,2},{4,5},{5,4},{6,7},{7,6},{8,9},{9,8},{10,11... | collective-permute-start | bytes 3096584 | tf_op jit(solution)/shard_map/ppermute | solution.py:201
  101.2 83.6 %all-gather.15.cloned.1.call-start = ((), (), s32[]{:S(2)}) async-start(), calls=%async_computation.3 | async-start | bytes 5971968 | tf_op jit(solution)/shard_map/all_gather | solution.py:86
  134.0 349.4 %all-gather.17.cloned.1.call-start = ((), (), s32[]{:S(2)}) async-start(), calls=%async_computation.4 | async-start | bytes 5971968 | tf_op jit(solution)/shard_map/all_gather | solution.py:86
  213.9 60.7 %collective-permute-start.9 = (bf16[4,288,1152]{2,1,0:T(8,128)(2,1)}, bf16[4,288,1152]{2,1,0:T(8,128)(2,1)}, u32[]{:S(2)}, u32[]{:S(2)}) collective-permute-start(bf16[4,288,1152]{2,1,0:T(8,128)(2,1)} %bitcast.100), channel_id=1, source_target_pairs={{0,1},{1,0},{2,3},{3,2},{4,5},{5,4},{6,7},{7,6},{8,9},{9,8},{10,11... | collective-permute-start | bytes 7962632 | tf_op jit(solution)/shard_map/ppermute | solution.py:43
  266.3 68.2 %collective-permute-start.14 = (bf16[4,72,4608]{2,1,0:T(8,128)(2,1)}, bf16[4,72,4608]{2,1,0:T(8,128)(2,1)}, u32[]{:S(2)}, u32[]{:S(2)}) collective-permute-start(bf16[4,72,4608]{2,1,0:T(8,128)(2,1)} %bitcast.99), channel_id=1, source_target_pairs={{0,1},{1,0},{2,3},{3,2},{4,5},{5,4},{6,7},{7,6},{8,9},{9,8},{10,11... | collective-permute-start | bytes 7962632 | tf_op jit(solution)/shard_map/ppermute | solution.py:43
  341.8 37.9 %collective-permute-start.21 = (bf16[288,1152]{1,0:T(8,128)(2,1)}, bf16[288,1152]{1,0:T(8,128)(2,1)}, u32[]{:S(2)}, u32[]{:S(2)}) collective-permute-start(bf16[288,1152]{1,0:T(8,128)(2,1)} %add.128.refs_0_), channel_id=1, source_target_pairs={{0,16},{16,0},{1,17},{17,1},{2,18},{18,2},{3,19},{19,3},{4,20},{20... | collective-permute-start | bytes 1990664 | tf_op jit(solution)/shard_map/ppermute | solution.py:43
  353.6 68.1 %collective-permute-start.18 = (bf16[4,72,2304]{2,1,0:T(8,128)(2,1)}, bf16[4,72,2304]{2,1,0:T(8,128)(2,1)}, u32[]{:S(2)}, u32[]{:S(2)}) collective-permute-start(bf16[4,72,2304]{2,1,0:T(8,128)(2,1)} %bitcast.32), channel_id=1, source_target_pairs={{0,1},{1,0},{2,3},{3,2},{4,5},{5,4},{6,7},{7,6},{8,9},{9,8},{10,11... | collective-permute-start | bytes 3981320 | tf_op jit(solution)/shard_map/ppermute | solution.py:43
  378.3 93.1 %collective-permute-start.17 = (bf16[4,144,1152]{2,1,0:T(8,128)(2,1)}, bf16[4,144,1152]{2,1,0:T(8,128)(2,1)}, u32[]{:S(2)}, u32[]{:S(2)}) collective-permute-start(bf16[4,144,1152]{2,1,0:T(8,128)(2,1)} %bitcast.101), channel_id=1, source_target_pairs={{0,1},{1,0},{2,3},{3,2},{4,5},{5,4},{6,7},{7,6},{8,9},{9,8},{10,11... | collective-permute-start | bytes 3981320 | tf_op jit(solution)/shard_map/ppermute | solution.py:43
  382.1 160.3 %all-gather.23.cloned.1.call-start = ((), (), s32[]{:S(2)}) async-start(), calls=%async_computation.7 | async-start | bytes 5971968 | tf_op jit(solution)/shard_map/all_gather | solution.py:86
  392.0 46.7 %collective-permute-start.25 = (bf16[72,4608]{1,0:T(8,128)(2,1)}, bf16[72,4608]{1,0:T(8,128)(2,1)}, u32[]{:S(2)}, u32[]{:S(2)}) collective-permute-start(bf16[72,4608]{1,0:T(8,128)(2,1)} %add.130.refs_0_), channel_id=1, source_target_pairs={{0,16},{16,0},{1,17},{17,1},{2,18},{18,2},{3,19},{19,3},{4,20},{20... | collective-permute-start | bytes 1990664 | tf_op jit(solution)/shard_map/ppermute | solution.py:43
  435.5 64.3 %collective-permute-start.32 = (bf16[72,2304]{1,0:T(8,128)(2,1)}, bf16[72,2304]{1,0:T(8,128)(2,1)}, u32[]{:S(2)}, u32[]{:S(2)}) collective-permute-start(bf16[72,2304]{1,0:T(8,128)(2,1)} %add.132.refs_0_), channel_id=1, source_target_pairs={{0,16},{16,0},{1,17},{17,1},{2,18},{18,2},{3,19},{19,3},{4,20},{20... | collective-permute-start | bytes 995336 | tf_op jit(solution)/shard_map/ppermute | solution.py:43
  440.9 114.5 %all-gather.21.cloned.1.call-start = ((), (), s32[]{:S(2)}) async-start(), calls=%async_computation.6 | async-start | bytes 5971968 | tf_op jit(solution)/shard_map/all_gather | solution.py:86
  482.0 53.4 %collective-permute-start.35 = (bf16[7,128,576]{1,2,0:T(8,128)(2,1)}, bf16[7,128,576]{1,2,0:T(8,128)(2,1)}, u32[]{:S(2)}, u32[]{:S(2)}) collective-permute-start(bf16[7,128,576]{1,2,0:T(8,128)(2,1)} %copy.35), channel_id=1, source_target_pairs={{0,1},{1,0},{2,3},{3,2},{4,5},{5,4},{6,7},{7,6},{8,9},{9,8},{10,11... | collective-permute-start | bytes 3096584 | tf_op jit(solution)/shard_map/ppermute | solution.py:201
  494.6 35.0 %collective-permute-start.37 = (bf16[7,64,1152]{2,1,0:T(8,128)(2,1)}, bf16[7,64,1152]{2,1,0:T(8,128)(2,1)}, u32[]{:S(2)}, u32[]{:S(2)}) collective-permute-start(bf16[7,64,1152]{2,1,0:T(8,128)(2,1)} %get-tuple-element.413), channel_id=1, source_target_pairs={{0,1},{1,0},{2,3},{3,2},{4,5},{5,4},{6,7},{7,6},{8,9},{9,8},{10,11... | collective-permute-start | bytes 3096584 | tf_op jit(solution)/shard_map/ppermute | solution.py:201
  499.8 48.8 %collective-permute-start.39 = (f32[1,12672]{1,0:T(1,128)}, f32[1,12672]{1,0:T(1,128)}, u32[]{:S(2)}, u32[]{:S(2)}) collective-permute-start(f32[1,12672]{1,0:T(1,128)} %add.137.refs_0_), channel_id=1, source_target_pairs={{0,1},{1,0},{2,3},{3,2},{4,5},{5,4},{6,7},{7,6},{8,9},{9,8},{10,11... | collective-permute-start | bytes 152072 | tf_op jit(solution)/shard_map/ppermute | solution.py:43
  502.7 63.8 %all-gather.19.cloned.1.call-start = ((), (), s32[]{:S(2)}) async-start(), calls=%async_computation.5 | async-start | bytes 2985984 | tf_op jit(solution)/shard_map/all_gather | solution.py:86
  (53 other events, 780.5 us)
Sparse Core Ops, SparseCore 0:
  20.0 24.0 all-gather.8
  58.5 34.8 all-gather.10
  101.4 34.2 all-gather.12
  137.2 33.8 all-gather.14
  382.2 53.6 all-gather.16
  441.1 51.3 all-gather.22
  502.8 39.4 all-gather.20
  543.9 22.5 all-gather.18

commit v6 on v5

--- a/solution.py
+++ b/solution.py
@@ -1015,20 +1015,20 @@
         activated,
         middle,
     )
+    output_pieces = chain.run(
+        lambda a: split_parts(a.reshape(per, slots, width), 1), result
+    )
+    output_pieces = swap_pieces(output_pieces)
     grad_latents = chain.run(
         lambda *a: joined_pieces(a, 0)[:items].astype(F32), *latent_pieces
     )
     skip_sum.step()
     grad_skip = chain.run(lambda *a: joined_pieces(a, 0)[:items], *skip_pieces)
-    output_pieces = chain.run(
-        lambda a: split_parts(a.reshape(per, slots, width), 1), result
-    )
-    output_pieces = swap_pieces(output_pieces)
     (sum_expand,) = expand_sum.finish()
     vector_sum.step()
     sum_inward, sum_outward = attention_sum.finish()
+    output = chain.run(lambda *a: joined_pieces(a, 0)[:items], *output_pieces)
     (sum_skipw,) = skip_sum.finish()
-    output = chain.run(lambda *a: joined_pieces(a, 0)[:items], *output_pieces)
     (
         sum_skipb,
         sum_gain1,

time: 587 us -> 584 us (level)
  transfers between devices with their start and end apart: 48 -> 48, of which waited for: 14 -> 13; matrix products, arithmetic and copies ran while one was open for 9% -> 10% of each run, Pallas kernels for 59% -> 59%
where the time goes in v6:
time: 584 us; the launch traced here: 577 us
  Pallas kernels  350 us (60%)
  waiting for transfers between devices  106 us (18%)
  starting transfers between devices  44.6 us (8%)
  local copies, waits for them, and re-layouts  39.1 us (7%)
  other arithmetic  22.5 us (4%)
  between operations  15.1 us (3%)
    pallas_call x8, Pallas kernels, dense(): pl.pallas_call(kernel, out_shape=tuple((jax.ShapeDtypeStruct((rows, c), d...  161 us
    ppermute x34, waiting for transfers between devices, flip(): return lax.ppermute(array, axis, [(0, 1), (1, 0)])  83.4 us
    pallas_call x4, Pallas kernels, core_gradients(): pl.pallas_call(kernel, out_shape=(half, half), grid_spec=pltpu.PrefetchSc...  62.1 us
    pallas_call x15, Pallas kernels, fold(): pl.pallas_call(fold_kernel, out_shape=(half, half), grid_spec=pltpu.Prefe...  52.3 us
    ppermute x34, starting transfers between devices, flip(): return lax.ppermute(array, axis, [(0, 1), (1, 0)])  36.4 us
    pallas_call x14, Pallas kernels, add(): pl.pallas_call(add_kernel, out_shape=jax.ShapeDtypeStruct((rows, columns...  26.7 us
    pallas_call x4, Pallas kernels, widen(): pl.pallas_call(widen_kernel, out_shape=tuple((jax.ShapeDtypeStruct((rows,...  22.5 us
    ppermute x6, waiting for transfers between devices, swap_pieces(): lax.ppermute(piece, 'seq', [(i, (i + hop) % ways) for i in range(ways)])  21.2 us
  transfers between devices with their start and end apart: 48, of which 13 were waited for; matrix products, arithmetic and copies ran while one was open for 10% of the time, Pallas kernels for 59%

profile of v6, /device:TPU:0, one launch (start us, length us, event | category | flops | bytes accessed | tf_op | source)
XLA Modules:
  0.0 577.3 jit_solution(16059158379665705841)
XLA Ops:
  27.5 25.3 %collective-permute-done.3 = bf16[1,6336]{1,0:T(2,128)(2,1)S(1)} collective-permute-done((bf16[1,6336]{1,0:T(2,128)(2,1)S(1)}, bf16[1,6336]{1,0:T(2,128)(2,1)S(1)}, u32[]{:S(2)}, u32[]{:S(2)}) %collective-permute-start.3) | collective-permute-done | bytes 12704 | tf_op jit(solution)/shard_map/ppermute | solution.py:43
  58.4 16.6 %collective-permute-done.1 = bf16[7,128,576]{1,2,0:T(8,128)(2,1)} collective-permute-done((bf16[7,128,576]{1,2,0:T(8,128)(2,1)}, bf16[7,128,576]{1,2,0:T(8,128)(2,1)}, u32[]{:S(2)}, u32[]{:S(2)}) %collective-permute-start.1) | collective-permute-done | bytes 1032224 | tf_op jit(solution)/shard_map/ppermute | solution.py:201
  81.3 7.7 %skip_base.1.refs_1_ = f32[896,1152]{1,0:T(8,128)} custom-call(s32[1]{0:T(128)} %bitcast.side.index_ref, bf16[896,1152]{1,0:T(8,128)(2,1)} %maximum_select_fusion.refs_0_.refs_1_, bf16[1152,1152]{1,0:T(8,128)(2,1)} %refs_1_.3, bf16[1152,1152]{1,0:T(8,128)(2,1)} %all-gather.9.cloned.1.call-done.refs_2_.refs_6_), custom_call_target="tpu_custom_call" | custom-call | flops 9999999827968 | bytes 1000000000 | tf_op jit(solution)/shard_map/skip_base/pallas_call | solution.py:299
  101.9 21.4 %base_inward.1 = (f32[896,1152]{1,0:T(8,128)}, bf16[896,1152]{1,0:T(8,128)(2,1)}, bf16[896,3456]{1,0:T(8,128)(2,1)}) custom-call(s32[1]{0:T(128)} %bitcast.side.index_ref, bf16[896,1152]{1,0:T(8,128)(2,1)} %bitcast.91, f32[896,1152]{1,0:T(8,128)} %skip_base.1.refs_1_, f32[1,1152]{1,0:T(1,128)} %reshape.542.refs_2_, f32[1,1152]{1,0:T(1,128)} %reshape.543.refs_3_, ...), custom_call_target="tpu_custom_call" | custom-call | flops 9999999827968 | bytes 1000000000 | tf_op jit(solution)/shard_map/base_inward/pallas_call | solution.py:299
  123.2 10.8 %attend.1 = (bf16[896,1152]{1,0:T(8,128)(2,1)}, bf16[14336,128]{1,0:T(8,128)(2,1)}) custom-call(s32[7]{0:T(128)} %pad_dynamic-slice_fusion.6.lengths, bf16[896,3456]{1,0:T(8,128)(2,1)} %get-tuple-element.248.qkv), custom_call_target="tpu_custom_call" | custom-call | flops 9999999827968 | bytes 1000000000 | tf_op jit(solution)/shard_map/attend/pallas_call | solution.py:660
  135.7 28.7 %middle_expand.1 = (f32[896,1152]{1,0:T(8,128)}, bf16[896,1152]{1,0:T(8,128)(2,1)}, bf16[896,4608]{1,0:T(8,128)(2,1)}, bf16[896,4608]{1,0:T(8,128)(2,1)}) custom-call(s32[1]{0:T(128)} %bitcast.side.index_ref, bf16[896,1152]{1,0:T(8,128)(2,1)} %get-tuple-element.295.refs_0_.refs_1_, f32[896,1152]{1,0:T(8,128)} %get-tuple-element.303.refs_1_, ...), custom_call_target="tpu_custom_call" | custom-call | flops 9999999827968 | bytes 1000000000 | tf_op jit(solution)/shard_map/middle_expand/pallas_call | solution.py:299
  168.0 16.7 %contract_grad.1 = (bf16[8,288,1152]{2,1,0:T(8,128)(2,1)}, bf16[8,288,1152]{2,1,0:T(8,128)(2,1)}) custom-call(s32[1]{0:T(128)} %bitcast.7.core_ref, bf16[896,4608]{1,0:T(8,128)(2,1)} %get-tuple-element.407.refs_0_, bf16[896,1152]{1,0:T(8,128)(2,1)} %bitcast.93), custom_call_target="tpu_custom_call" | custom-call | flops 9999999827968 | bytes 1000000000 | tf_op jit(solution)/shard_map/contract_grad/pallas_call | solution.py:584
  184.9 22.9 %upper_back.1 = (bf16[896,4608]{1,0:T(8,128)(2,1)}, f32[1,4608]{1,0:T(1,128)}, f32[1,1152]{1,0:T(1,128)}) custom-call(s32[1]{0:T(128)} %bitcast.side.index_ref, bf16[896,1152]{1,0:T(8,128)(2,1)} %bitcast.94, bf16[896,4608]{1,0:T(8,128)(2,1)} %get-tuple-element.265.refs_1_, bf16[2304,1152]{1,0:T(8,128)(2,1)} %refs_3_.1, ...), custom_call_target="tpu_custom_call" | custom-call | flops 9999999827968 | bytes 1000000000 | tf_op jit(solution)/shard_map/upper_back/pallas_call | solution.py:299
  207.8 6.2 %fold_seq.5 = (bf16[1,4,288,1152]{3,2,1,0:T(8,128)(2,1)}, bf16[1,4,288,1152]{3,2,1,0:T(8,128)(2,1)}) custom-call(s32[1]{0:T(128)} %bitcast.side.index_ref, bf16[1,2,4,288,1152]{4,3,2,1,0:T(8,128)(2,1)} %bitcast.115, bf16[1,2,4,288,1152]{4,3,2,1,0:T(8,128)(2,1)} %bitcast.10.refs_1_), custom_call_target="tpu_custom_call" | custom-call | flops 9999999827968 | bytes 1000000000 | tf_op jit(solution)/shard_map/fold_seq/pallas_call | solution.py:342
  215.4 16.6 %expand_grad.1 = (bf16[8,72,4608]{2,1,0:T(8,128)(2,1)}, bf16[8,72,4608]{2,1,0:T(8,128)(2,1)}) custom-call(s32[1]{0:T(128)} %bitcast.7.core_ref, bf16[896,1152]{1,0:T(8,128)(2,1)} %get-tuple-element.274.refs_0_, bf16[896,4608]{1,0:T(8,128)(2,1)} %get-tuple-element.277.refs_1_.refs_0_), custom_call_target="tpu_custom_call" | custom-call | flops 9999999827968 | bytes 1000000000 | tf_op jit(solution)/shard_map/expand_grad/pallas_call | solution.py:584
  232.0 28.0 %middle_back.1 = (bf16[896,1152]{1,0:T(8,128)(2,1)}, f32[896,1152]{1,0:T(8,128)}, bf16[896,1152]{1,0:T(8,128)(2,1)}, f32[1,1152]{1,0:T(1,128)}, f32[1,1152]{1,0:T(1,128)}, /*index=5*/f32[1,1152]{1,0:T(1,128)}) custom-call(s32[1]{0:T(128)} %bitcast.side.index_ref, bf16[896,4608]{1,0:T(8,128)(2,1)} %get-tuple-element.277.refs_1_.refs_0_, ...), custom_call_target="tpu_custom_call" | custom-call | flops 9999999827968 | bytes 1000000000 | tf_op jit(solution)/shard_map/middle_back/pallas_call | solution.py:299
  260.1 6.2 %fold_seq.6 = (bf16[1,4,72,4608]{3,2,1,0:T(8,128)(2,1)}, bf16[1,4,72,4608]{3,2,1,0:T(8,128)(2,1)}) custom-call(s32[1]{0:T(128)} %bitcast.side.index_ref, bf16[1,2,4,72,4608]{4,3,2,1,0:T(8,128)(2,1)} %bitcast.114, bf16[1,2,4,72,4608]{4,3,2,1,0:T(8,128)(2,1)} %bitcast.14.refs_1_), custom_call_target="tpu_custom_call" | custom-call | flops 9999999827968 | bytes 1000000000 | tf_op jit(solution)/shard_map/fold_seq/pallas_call | solution.py:342
  266.9 7.7 %collective-permute-done.9 = bf16[4,288,1152]{2,1,0:T(8,128)(2,1)} collective-permute-done((bf16[4,288,1152]{2,1,0:T(8,128)(2,1)}, bf16[4,288,1152]{2,1,0:T(8,128)(2,1)}, u32[]{:S(2)}, u32[]{:S(2)}) %collective-permute-start.9) | collective-permute-done | bytes 2654240 | tf_op jit(solution)/shard_map/ppermute | solution.py:43
  280.0 12.7 %attend_back.1.refs_2_.refs_0_ = bf16[896,3456]{1,0:T(8,128)(2,1)} custom-call(bf16[896,3456]{1,0:T(8,128)(2,1)} %get-tuple-element.248.qkv, bf16[14336,128]{1,0:T(8,128)(2,1)} %get-tuple-element.255.probs_in, bf16[896,1152]{1,0:T(8,128)(2,1)} %get-tuple-element.290.grad_mixed), custom_call_target="tpu_custom_call" | custom-call | flops 9999999827968 | bytes 1000000000 | tf_op jit(solution)/shard_map/attend_back/pallas_call | solution.py:718
  292.6 18.1 %attention_grad.1 = (bf16[8,72,4608]{2,1,0:T(8,128)(2,1)}, bf16[8,72,4608]{2,1,0:T(8,128)(2,1)}) custom-call(s32[1]{0:T(128)} %bitcast.7.core_ref, bf16[896,1152]{1,0:T(8,128)(2,1)} %get-tuple-element.294.refs_0_, bf16[896,1152]{1,0:T(8,128)(2,1)} %get-tuple-element.295.refs_0_.refs_1_, bf16[896,3456]{1,0:T(8,128)(2,1)} %attend_back.1.refs_2_.refs_0_, ...), custom_call_target="tpu_custom_call" | custom-call | flops 9999999827968 | bytes 1000000000 | tf_op jit(solution)/shard_map/attention_grad/pallas_call | solution.py:584
  314.2 20.3 %base_back.1 = (bf16[896,1152]{1,0:T(8,128)(2,1)}, f32[1,1152]{1,0:T(1,128)}, f32[1,1152]{1,0:T(1,128)}, f32[1,1152]{1,0:T(1,128)}) custom-call(s32[1]{0:T(128)} %bitcast.side.index_ref, bf16[896,3456]{1,0:T(8,128)(2,1)} %attend_back.1.refs_2_.refs_0_, f32[896,1152]{1,0:T(8,128)} %get-tuple-element.303.refs_1_, f32[896,1152]{1,0:T(8,128)} %get-tuple-element.304.refs_2_, ...), custom_call_target="tpu_custom_call" | custom-call | flops 9999999827968 | bytes 1000000000 | tf_op jit(solution)/shard_map/base_back/pallas_call | solution.py:299
  354.2 10.8 %skip_grad.1 = (bf16[8,144,1152]{2,1,0:T(8,128)(2,1)}, bf16[8,144,1152]{2,1,0:T(8,128)(2,1)}) custom-call(s32[1]{0:T(128)} %bitcast.7.core_ref, bf16[896,1152]{1,0:T(8,128)(2,1)} %bitcast.92, bf16[896,1152]{1,0:T(8,128)(2,1)} %maximum_select_fusion.refs_0_.refs_1_, bf16[896,1152]{1,0:T(8,128)(2,1)} %get-tuple-element.380.refs_2_.refs_0_), custom_call_target="tpu_custom_call" | custom-call | flops 9999999827968 | bytes 1000000000 | tf_op jit(solution)/shard_map/skip_grad/pallas_call | solution.py:584
  399.4 16.2 %collective-permute-done.23 = bf16[2,72,2304]{2,1,0:T(8,128)(2,1)} collective-permute-done((bf16[2,72,2304]{2,1,0:T(8,128)(2,1)}, bf16[2,72,2304]{2,1,0:T(8,128)(2,1)}, u32[]{:S(2)}, u32[]{:S(2)}) %collective-permute-start.23) | collective-permute-done | bytes 663584 | tf_op jit(solution)/shard_map/ppermute | solution.py:43
  424.6 9.2 %collective-permute-done.26 = bf16[1,72,2304]{2,1,0:T(8,128)(2,1)} collective-permute-done((bf16[1,72,2304]{2,1,0:T(8,128)(2,1)}, bf16[1,72,2304]{2,1,0:T(8,128)(2,1)}, u32[]{:S(2)}, u32[]{:S(2)}) %collective-permute-start.26) | collective-permute-done | bytes 331808 | tf_op jit(solution)/shard_map/ppermute | solution.py:43
  446.7 12.2 %joined_back.1 = (bf16[896,1152]{1,0:T(8,128)(2,1)}, bf16[896,576]{1,0:T(8,128)(2,1)}, bf16[896,576]{1,0:T(8,128)(2,1)}) custom-call(s32[1]{0:T(128)} %bitcast.side.index_ref, bf16[896,1152]{1,0:T(8,128)(2,1)} %get-tuple-element.380.refs_2_.refs_0_, bf16[1152,1152]{1,0:T(8,128)(2,1)} %refs_1_.3, bf16[1152,1152]{1,0:T(8,128)(2,1)} %all-gather.9.cloned.1.call-done.refs_2_.refs_6_), custom_call_target="tpu_custom_call" | custom-call | flops 9999999827968 | bytes 1000000000 | tf_op jit(solution)/shard_map/joined_back/pallas_call | solution.py:299
  483.5 6.2 %widen.4 = f32[2304,1152]{1,0:T(8,128)} custom-call(bf16[2304,1152]{1,0:T(8,128)(2,1)} %all-gather.17.cloned.1.call-done.value), custom_call_target="tpu_custom_call" | custom-call | flops 9999999827968 | bytes 1000000000 | tf_op jit(solution)/shard_map/widen/pallas_call | solution.py:395
  510.0 19.5 %contract.1 = bf16[896,1152]{1,0:T(8,128)(2,1)} custom-call(s32[1]{0:T(128)} %bitcast.side.index_ref, bf16[896,4608]{1,0:T(8,128)(2,1)} %get-tuple-element.407.refs_0_, f32[896,1152]{1,0:T(8,128)} %get-tuple-element.408.refs_1_, f32[1,1152]{1,0:T(1,128)} %reshape.549.refs_2_, bf16[2304,1152]{1,0:T(8,128)(2,1)} %refs_3_.1, ...), custom_call_target="tpu_custom_call" | custom-call | flops 9999999827968 | bytes 1000000000 | tf_op jit(solution)/shard_map/contract/pallas_call | solution.py:299
  543.9 6.2 %widen.5 = f32[576,4608]{1,0:T(8,128)} custom-call(bf16[576,4608]{1,0:T(8,128)(2,1)} %all-gather.21.cloned.1.call-done.value), custom_call_target="tpu_custom_call" | custom-call | flops 9999999827968 | bytes 1000000000 | tf_op jit(solution)/shard_map/widen/pallas_call | solution.py:395
  556.9 6.2 %widen.6 = (f32[576,3456]{1,0:T(8,128)}, f32[576,1152]{1,0:T(8,128)}) custom-call(bf16[576,4608]{1,0:T(8,128)(2,1)} %all-gather.19.cloned.1.call-done.value), custom_call_target="tpu_custom_call" | custom-call | flops 9999999827968 | bytes 1000000000 | tf_op jit(solution)/shard_map/widen/pallas_call | solution.py:395
  (242 shorter events, 209.8 us)
Async XLA Ops:
  7.3 74.0 %all-gather.9.cloned.1.call-start = ((), (), s32[]{:S(2)}) async-start(), calls=%async_computation | async-start | bytes 2985984 | tf_op jit(solution)/shard_map/all_gather | solution.py:86
  19.9 82.0 %all-gather.11.cloned.1.call-start = ((), (), s32[]{:S(2)}) async-start(), calls=%async_computation.1 | async-start | bytes 5971968 | tf_op jit(solution)/shard_map/all_gather | solution.py:86
  19.9 79.3 %collective-permute-start.5 = (bf16[72,4608]{1,0:T(8,128)(2,1)}, bf16[72,4608]{1,0:T(8,128)(2,1)}, u32[]{:S(2)}, u32[]{:S(2)}) collective-permute-start(bf16[72,4608]{1,0:T(8,128)(2,1)} %constant_dynamic-slice_fusion.11), channel_id=1, source_target_pairs={{0,1},{1,0},{2,3},{3,2},{4,5},{5,4},{6,7},{7,6},{8,9},{9,8},{10,11... | collective-permute-start | bytes 1990664 | tf_op jit(solution)/shard_map/ppermute | solution.py:43
  21.2 37.2 %collective-permute-start.4 = (bf16[72,4608]{1,0:T(8,128)(2,1)}, bf16[72,4608]{1,0:T(8,128)(2,1)}, u32[]{:S(2)}, u32[]{:S(2)}) collective-permute-start(bf16[72,4608]{1,0:T(8,128)(2,1)} %pad_maximum_fusion.6), channel_id=1, source_target_pairs={{0,1},{1,0},{2,3},{3,2},{4,5},{5,4},{6,7},{7,6},{8,9},{9,8},{10,11... | collective-permute-start | bytes 1990664 | tf_op jit(solution)/shard_map/ppermute | solution.py:43
  23.3 51.7 %collective-permute-start.1 = (bf16[7,128,576]{1,2,0:T(8,128)(2,1)}, bf16[7,128,576]{1,2,0:T(8,128)(2,1)}, u32[]{:S(2)}, u32[]{:S(2)}) collective-permute-start(bf16[7,128,576]{1,2,0:T(8,128)(2,1)} %get-tuple-element.443), channel_id=1, source_target_pairs={{0,1},{1,0},{2,3},{3,2},{4,5},{5,4},{6,7},{7,6},{8,9},{9,8},{10,11... | collective-permute-start | bytes 3096584 | tf_op jit(solution)/shard_map/ppermute | solution.py:201
  24.1 71.6 %collective-permute-start = (bf16[7,64,1152]{2,1,0:T(8,128)(2,1)}, bf16[7,64,1152]{2,1,0:T(8,128)(2,1)}, u32[]{:S(2)}, u32[]{:S(2)}) collective-permute-start(bf16[7,64,1152]{2,1,0:T(8,128)(2,1)} %get-tuple-element.445), channel_id=1, source_target_pairs={{0,1},{1,0},{2,3},{3,2},{4,5},{5,4},{6,7},{7,6},{8,9},{9,8},{10,11... | collective-permute-start | bytes 3096584 | tf_op jit(solution)/shard_map/ppermute | solution.py:201
  58.4 77.3 %all-gather.13.cloned.1.call-start = ((), (), s32[]{:S(2)}) async-start(), calls=%async_computation.2 | async-start | bytes 5971968 | tf_op jit(solution)/shard_map/all_gather | solution.py:86
  99.2 34.8 %collective-permute-start.7 = (bf16[288,1152]{1,0:T(8,128)(2,1)}, bf16[288,1152]{1,0:T(8,128)(2,1)}, u32[]{:S(2)}, u32[]{:S(2)}) collective-permute-start(bf16[288,1152]{1,0:T(8,128)(2,1)} %eighth.1), channel_id=1, source_target_pairs={{0,1},{1,0},{2,3},{3,2},{4,5},{5,4},{6,7},{7,6},{8,9},{9,8},{10,11... | collective-permute-start | bytes 1990664 | tf_op jit(solution)/shard_map/ppermute | solution.py:43
  99.8 64.6 %collective-permute-start.6 = (bf16[7,64,1152]{2,1,0:T(8,128)(2,1)}, bf16[7,64,1152]{2,1,0:T(8,128)(2,1)}, u32[]{:S(2)}, u32[]{:S(2)}) collective-permute-start(bf16[7,64,1152]{2,1,0:T(8,128)(2,1)} %get-tuple-element.257), channel_id=1, source_target_pairs={{0,1},{1,0},{2,3},{3,2},{4,5},{5,4},{6,7},{7,6},{8,9},{9,8},{10,11... | collective-permute-start | bytes 3096584 | tf_op jit(solution)/shard_map/ppermute | solution.py:201
  101.3 83.6 %all-gather.15.cloned.1.call-start = ((), (), s32[]{:S(2)}) async-start(), calls=%async_computation.3 | async-start | bytes 5971968 | tf_op jit(solution)/shard_map/all_gather | solution.py:86
  134.0 349.4 %all-gather.17.cloned.1.call-start = ((), (), s32[]{:S(2)}) async-start(), calls=%async_computation.4 | async-start | bytes 5971968 | tf_op jit(solution)/shard_map/all_gather | solution.py:86
  213.9 60.7 %collective-permute-start.9 = (bf16[4,288,1152]{2,1,0:T(8,128)(2,1)}, bf16[4,288,1152]{2,1,0:T(8,128)(2,1)}, u32[]{:S(2)}, u32[]{:S(2)}) collective-permute-start(bf16[4,288,1152]{2,1,0:T(8,128)(2,1)} %bitcast.100), channel_id=1, source_target_pairs={{0,1},{1,0},{2,3},{3,2},{4,5},{5,4},{6,7},{7,6},{8,9},{9,8},{10,11... | collective-permute-start | bytes 7962632 | tf_op jit(solution)/shard_map/ppermute | solution.py:43
  266.3 68.2 %collective-permute-start.14 = (bf16[4,72,4608]{2,1,0:T(8,128)(2,1)}, bf16[4,72,4608]{2,1,0:T(8,128)(2,1)}, u32[]{:S(2)}, u32[]{:S(2)}) collective-permute-start(bf16[4,72,4608]{2,1,0:T(8,128)(2,1)} %bitcast.99), channel_id=1, source_target_pairs={{0,1},{1,0},{2,3},{3,2},{4,5},{5,4},{6,7},{7,6},{8,9},{9,8},{10,11... | collective-permute-start | bytes 7962632 | tf_op jit(solution)/shard_map/ppermute | solution.py:43
  341.8 37.9 %collective-permute-start.21 = (bf16[288,1152]{1,0:T(8,128)(2,1)}, bf16[288,1152]{1,0:T(8,128)(2,1)}, u32[]{:S(2)}, u32[]{:S(2)}) collective-permute-start(bf16[288,1152]{1,0:T(8,128)(2,1)} %add.128.refs_0_), channel_id=1, source_target_pairs={{0,16},{16,0},{1,17},{17,1},{2,18},{18,2},{3,19},{19,3},{4,20},{20... | collective-permute-start | bytes 1990664 | tf_op jit(solution)/shard_map/ppermute | solution.py:43
  353.7 68.2 %collective-permute-start.18 = (bf16[4,72,2304]{2,1,0:T(8,128)(2,1)}, bf16[4,72,2304]{2,1,0:T(8,128)(2,1)}, u32[]{:S(2)}, u32[]{:S(2)}) collective-permute-start(bf16[4,72,2304]{2,1,0:T(8,128)(2,1)} %bitcast.32), channel_id=1, source_target_pairs={{0,1},{1,0},{2,3},{3,2},{4,5},{5,4},{6,7},{7,6},{8,9},{9,8},{10,11... | collective-permute-start | bytes 3981320 | tf_op jit(solution)/shard_map/ppermute | solution.py:43
  378.3 93.0 %collective-permute-start.17 = (bf16[4,144,1152]{2,1,0:T(8,128)(2,1)}, bf16[4,144,1152]{2,1,0:T(8,128)(2,1)}, u32[]{:S(2)}, u32[]{:S(2)}) collective-permute-start(bf16[4,144,1152]{2,1,0:T(8,128)(2,1)} %bitcast.101), channel_id=1, source_target_pairs={{0,1},{1,0},{2,3},{3,2},{4,5},{5,4},{6,7},{7,6},{8,9},{9,8},{10,11... | collective-permute-start | bytes 3981320 | tf_op jit(solution)/shard_map/ppermute | solution.py:43
  382.1 161.8 %all-gather.21.cloned.1.call-start = ((), (), s32[]{:S(2)}) async-start(), calls=%async_computation.6 | async-start | bytes 5971968 | tf_op jit(solution)/shard_map/all_gather | solution.py:86
  392.0 46.6 %collective-permute-start.25 = (bf16[72,4608]{1,0:T(8,128)(2,1)}, bf16[72,4608]{1,0:T(8,128)(2,1)}, u32[]{:S(2)}, u32[]{:S(2)}) collective-permute-start(bf16[72,4608]{1,0:T(8,128)(2,1)} %add.130.refs_0_), channel_id=1, source_target_pairs={{0,16},{16,0},{1,17},{17,1},{2,18},{18,2},{3,19},{19,3},{4,20},{20... | collective-permute-start | bytes 1990664 | tf_op jit(solution)/shard_map/ppermute | solution.py:43
  435.6 64.2 %collective-permute-start.32 = (bf16[72,2304]{1,0:T(8,128)(2,1)}, bf16[72,2304]{1,0:T(8,128)(2,1)}, u32[]{:S(2)}, u32[]{:S(2)}) collective-permute-start(bf16[72,2304]{1,0:T(8,128)(2,1)} %add.132.refs_0_), channel_id=1, source_target_pairs={{0,16},{16,0},{1,17},{17,1},{2,18},{18,2},{3,19},{19,3},{4,20},{20... | collective-permute-start | bytes 995336 | tf_op jit(solution)/shard_map/ppermute | solution.py:43
  440.9 115.9 %all-gather.19.cloned.1.call-start = ((), (), s32[]{:S(2)}) async-start(), calls=%async_computation.5 | async-start | bytes 5971968 | tf_op jit(solution)/shard_map/all_gather | solution.py:86
  482.0 57.3 %collective-permute-start.37 = (bf16[7,128,576]{1,2,0:T(8,128)(2,1)}, bf16[7,128,576]{1,2,0:T(8,128)(2,1)}, u32[]{:S(2)}, u32[]{:S(2)}) collective-permute-start(bf16[7,128,576]{1,2,0:T(8,128)(2,1)} %copy.35), channel_id=1, source_target_pairs={{0,1},{1,0},{2,3},{3,2},{4,5},{5,4},{6,7},{7,6},{8,9},{9,8},{10,11... | collective-permute-start | bytes 3096584 | tf_op jit(solution)/shard_map/ppermute | solution.py:201
  494.6 38.0 %collective-permute-start.39 = (bf16[7,64,1152]{2,1,0:T(8,128)(2,1)}, bf16[7,64,1152]{2,1,0:T(8,128)(2,1)}, u32[]{:S(2)}, u32[]{:S(2)}) collective-permute-start(bf16[7,64,1152]{2,1,0:T(8,128)(2,1)} %get-tuple-element.412), channel_id=1, source_target_pairs={{0,1},{1,0},{2,3},{3,2},{4,5},{5,4},{6,7},{7,6},{8,9},{9,8},{10,11... | collective-permute-start | bytes 3096584 | tf_op jit(solution)/shard_map/ppermute | solution.py:201
  499.8 50.3 %collective-permute-start.36 = (f32[1,12672]{1,0:T(1,128)}, f32[1,12672]{1,0:T(1,128)}, u32[]{:S(2)}, u32[]{:S(2)}) collective-permute-start(f32[1,12672]{1,0:T(1,128)} %add.137.refs_0_), channel_id=1, source_target_pairs={{0,1},{1,0},{2,3},{3,2},{4,5},{5,4},{6,7},{7,6},{8,9},{9,8},{10,11... | collective-permute-start | bytes 152072 | tf_op jit(solution)/shard_map/ppermute | solution.py:43
  502.7 63.5 %all-gather.23.cloned.1.call-start = ((), (), s32[]{:S(2)}) async-start(), calls=%async_computation.7 | async-start | bytes 2985984 | tf_op jit(solution)/shard_map/all_gather | solution.py:86
  (52 other events, 768.8 us)
Sparse Core Ops, SparseCore 0:
  20.0 24.0 all-gather.8
  58.5 34.8 all-gather.10
  101.4 34.2 all-gather.12
  137.2 33.8 all-gather.14
  382.2 53.6 all-gather.16
  441.0 51.2 all-gather.20
  502.8 39.4 all-gather.18
  543.9 22.2 all-gather.22
